TPU v7x, 128 devices: a whole 4x4x4 slice. The times are simulated.
128 devices in a mesh: sector: 64 (over y, z, x_hi, core), lift: 2 (over x_lo).
Axes of the slice: x: 4 (x_hi: 2, x_lo: 2; x = x_hi * 2 + x_lo), y: 4, z: 4, core: 2. Of those that a mesh axis runs over, the one named last changes fastest.
Arguments:
- right_side: float32 [128, 262144], P('lift', 'sector'), may hold values from -40 to 40
- diagonal: float32 [262144], P('sector'), may hold values from 1.9 to 2.6
- coupling: float32 [262144], P('sector'), may hold values from 0.3 to 0.94
- local_inverse: bfloat16 [256, 1024, 2048], P('sector'), may hold values from -0.1 to 0.6
- coarse_basis: bfloat16 [256, 16, 1024], P('sector'), may hold values from -0.1875 to 0.1875
- coarse_inverse: float32 [4096, 4096], P('sector', 'lift'), may hold values from -8 to 12
Outputs:
- solution: float32 [128, 262144], P('lift', 'sector')
- residual: float32 [128, 262144], P('lift', 'sector')
All inputs are finite; a program needn't handle non-finite values.
Results may differ from a plain program's by a relative error of at most 0.019.
Values may be sent and summed in bfloat16 or wider, within the bound.
No kernel may reach another device: no remote copies, remote signals or barrier semaphores. Data moves between devices by JAX's collectives and lax.ppermute only.
A program may use at most 128 MiB of HBM per device.

v0:
```python
import functools

import jax
import jax.numpy as jnp
from jax import lax
from jax.experimental import pallas as pl
from jax.experimental.pallas import tpu as pltpu
from jax.sharding import PartitionSpec as P

SWEEPS = 4
F32, BF16 = jnp.float32, jnp.bfloat16
CH = 512
TILE = 128


def lane_of(shape):
    return lax.broadcasted_iota(jnp.int32, shape, 1)


def dot_t(a, b):
    return lax.dot_general(a, b, (((1,), (1,)), ((), ())), preferred_element_type=F32)


def split(x):
    hi = x.astype(BF16)
    return hi, (x - hi.astype(F32)).astype(BF16)


def spread(x):
    hi = x.astype(BF16).astype(F32)
    lo = (x - hi).astype(BF16).astype(F32)
    lane = lane_of((x.shape[0], TILE))
    return jnp.where(lane == 0, hi, jnp.where(lane == 1, lo, 0.0)).astype(BF16)


def column(tile, at):
    return tile[:, at : at + 1].astype(F32) + tile[:, at + 1 : at + 2].astype(F32)


def op_chunk(cur, before, after, dg, cp):
    width = cur.shape[1]
    lane = lane_of(cur.shape)
    left = jnp.where(lane == 0, before, pltpu.roll(cur, 1, 1))
    right = jnp.where(lane == width - 1, after, pltpu.roll(cur, width - 1, 1))
    return dg * cur - cp * (left + right)


def parts(v_ref, u0_ref, u3_ref, own):
    total = v_ref.shape[1]

    def get(lo, hi):
        if hi <= own:
            return u0_ref[:, lo:hi]
        if lo >= total - own:
            return u3_ref[:, lo - (total - own) : hi - (total - own)]
        return v_ref[:, lo:hi]

    return get


def chunks_of(get, total):
    for lo in range(0, total, CH):
        hi = lo + CH
        before = get(lo - 1, lo) if lo > 0 else None
        after = get(hi, hi + 1) if hi < total else None
        yield lo, hi, get(lo, hi), before, after


def pick(core_ref, a_ref, b_ref, left_ref, right_ref):
    @pl.when(core_ref[0] == 0)
    def _():
        left_ref[...] = b_ref[...]
        right_ref[...] = a_ref[...]

    @pl.when(core_ref[0] != 0)
    def _():
        left_ref[...] = a_ref[...]
        right_ref[...] = b_ref[...]


def first_edges(core_ref, r_hbm, cp_hbm, basis_hbm, ci_hbm, a_ref, b_ref,
                r_ref, cp_ref, basis_ref, ci_ref, left_ref, right_ref, sem):
    rows, total = r_hbm.shape
    subs, modes, own = basis_hbm.shape
    copies = []
    for k, (at, sub, tile_lo, cp_lo) in enumerate(
        ((0, 0, 0, 0), (total - CH, subs - 1, own - TILE, total - TILE))
    ):
        for n, (src, dst) in enumerate(
            (
                (r_hbm.at[:, pl.ds(at, CH)], r_ref.at[k]),
                (cp_hbm.at[:, pl.ds(cp_lo, TILE)], cp_ref.at[k]),
                (basis_hbm.at[sub, :, pl.ds(tile_lo, TILE)], basis_ref.at[k]),
                (ci_hbm.at[pl.ds(sub * modes, modes), :], ci_ref.at[k]),
            )
        ):
            copies.append(pltpu.make_async_copy(src, dst, sem.at[4 * k + n]))
    for c in copies:
        c.start()
    for c in copies:
        c.wait()
    lane = lane_of((modes, TILE))
    for k, (out, col, roll) in enumerate(((left_ref, 0, 2), (right_ref, TILE - 1, 3))):
        out[:, :CH] = r_ref[k].astype(BF16)
        one = cp_ref[k][:, col : col + 1]
        meta = spread(jnp.broadcast_to(one, (rows, 1))).astype(F32)
        weight = basis_ref[k].astype(F32)
        edge = pltpu.roll(weight, roll, 1) * one
        hi = edge.astype(BF16).astype(F32)
        lo = pltpu.roll(edge - hi, 1, 1)
        both = jnp.where(lane == 2, hi, jnp.where(lane == 3, lo, 0.0))
        out[:, CH : CH + TILE] = meta.astype(BF16)
        out[:modes, CH : CH + TILE] = (meta[:modes] + both).astype(BF16)
        line = jnp.sum(weight[:, col : col + 1] * ci_ref[k], axis=0, keepdims=True)
        count = line.shape[1] // TILE
        out[:, CH + TILE :] = jnp.zeros((rows, TILE), BF16)
        out[:count, CH + TILE :] = jnp.concatenate(
            [line[:, n * TILE : (n + 1) * TILE] for n in range(count)], axis=0
        ).astype(BF16)
    send_pair(core_ref, left_ref, right_ref, a_ref, b_ref)


def send_pair(core_ref, left_ref, right_ref, a_ref, b_ref):
    @pl.when(core_ref[0] == 0)
    def _():
        a_ref[...] = right_ref[...]
        b_ref[...] = left_ref[...]

    @pl.when(core_ref[0] != 0)
    def _():
        a_ref[...] = left_ref[...]
        b_ref[...] = right_ref[...]


def lines_of(core_ref, ci_ref, a_ref, b_ref, out_ref, left_ref, right_ref):
    pick(core_ref, a_ref, b_ref, left_ref, right_ref)
    rows, width = ci_ref.shape
    out_ref[:rows, :] = ci_ref[...].astype(BF16)
    extra = []
    for ref in (left_ref, right_ref):
        block = ref[:, CH + TILE :].astype(F32)
        extra.append(
            jnp.concatenate([block[k : k + 1, :] for k in range(width // TILE)], axis=1)
        )
    extra.append(jnp.zeros((6, width), F32))
    out_ref[rows:, :] = jnp.concatenate(extra, axis=0).astype(BF16)


def weave(core_ref, mine_ref, other_ref, out_ref, all_ref):
    rows, half = mine_ref.shape
    low = core_ref[3] == 0

    @pl.when(low)
    def _():
        all_ref[:, TILE : TILE + half] = mine_ref[...].astype(F32)
        all_ref[:, TILE + half : TILE + 2 * half] = other_ref[...].astype(F32)

    @pl.when(jnp.logical_not(low))
    def _():
        all_ref[:, TILE : TILE + half] = other_ref[...].astype(F32)
        all_ref[:, TILE + half : TILE + 2 * half] = mine_ref[...].astype(F32)

    all_ref[:, :TILE] = all_ref[:, 2 * half : 2 * half + TILE]
    all_ref[:, 2 * half + TILE :] = all_ref[:, TILE : 2 * TILE]
    lane = lane_of((rows, TILE))
    core = core_ref[0]
    zero = jnp.zeros((rows, TILE), F32)

    def step(k, carry):
        at = pl.multiple_of(k * TILE, TILE)
        prev = all_ref[:, pl.ds(at, TILE)]
        tile = all_ref[:, pl.ds(pl.multiple_of(at + TILE, TILE), TILE)]
        after = all_ref[:, pl.ds(pl.multiple_of(at + 2 * TILE, TILE), TILE)]
        near = pltpu.roll(tile, 16, 1)
        even = jnp.where(lane < 64, tile, jnp.where(lane < 80, pltpu.roll(prev, 80, 1), near))
        odd = jnp.where(lane < 64, pltpu.roll(tile, 64, 1), jnp.where(lane < 80, near, pltpu.roll(after, 80, 1)))
        at = 2 * k * TILE
        out_ref[:, pl.ds(pl.multiple_of(at + core * TILE, TILE), TILE)] = jnp.where(
            lane < 96, even, zero
        ).astype(BF16)
        out_ref[:, pl.ds(pl.multiple_of(at + (1 - core) * TILE, TILE), TILE)] = jnp.where(
            lane < 96, odd, zero
        ).astype(BF16)
        return carry

    lax.fori_loop(0, 2 * half // TILE, step, 0)


def products(s_ref, L_ref, own, order, store):
    total = s_ref.shape[1]
    margin = (order - own) // 2
    subs = L_ref.shape[0]
    part = own // 2

    def rows_at(k):
        return pl.ds(pl.multiple_of(k * part, part), part)

    def first(k, carry):
        p = dot_t(s_ref[:, TILE : order - margin], L_ref[0, rows_at(k), margin + TILE :])
        store(pl.multiple_of(k * part, part), part, p)
        return carry

    def last(k, carry):
        start = (subs - 1) * own - margin
        p = dot_t(
            s_ref[:, start : total - TILE], L_ref[subs - 1, rows_at(k), : total - TILE - start]
        )
        store(pl.multiple_of((subs - 1) * own + k * part, part), part, p)
        return carry

    def inner(n, carry):
        j, k = 1 + n // 2, n % 2
        start = pl.multiple_of(j * own - margin, TILE)
        p = dot_t(s_ref[:, pl.ds(start, order)], L_ref[j, rows_at(k), :])
        store(pl.multiple_of(j * own + k * part, part), part, p)
        return carry

    lax.fori_loop(0, 2, first, 0)
    lax.fori_loop(0, 2 * (subs - 2), inner, 0)
    lax.fori_loop(0, 2, last, 0)


def middle_first(r_ref, L_ref, v_ref, s_ref):
    own, order = L_ref.shape[1], L_ref.shape[2]
    s_ref[...] = r_ref[...].astype(BF16)

    def store(at, size, p):
        v_ref[:, pl.ds(at, size)] = p

    products(s_ref, L_ref, own, order, store)


def middle(r_ref, v_ref, u0_ref, u3_ref, dg_ref, cp_ref, L_ref, out_ref, s_ref):
    own, order = L_ref.shape[1], L_ref.shape[2]
    get = parts(v_ref, u0_ref, u3_ref, own)
    for lo, hi, cur, before, after in chunks_of(get, r_ref.shape[1]):
        before = 0.0 if before is None else before
        after = 0.0 if after is None else after
        s = r_ref[:, lo:hi] - op_chunk(cur, before, after, dg_ref[:, lo:hi], cp_ref[:, lo:hi])
        s_ref[:, lo:hi] = s.astype(BF16)
        out_ref[:, lo:hi] = cur

    def store(at, size, p):
        out_ref[:, pl.ds(at, size)] += p

    products(s_ref, L_ref, own, order, store)


def edge_sends(r_ref, dg_ref, cp_ref, u0, u3, left_ref, right_ref):
    total = r_ref.shape[1]
    own = u0.shape[1]
    s = r_ref[:, :CH] - op_chunk(
        u0[:, :CH], 0.0, u0[:, CH : CH + 1], dg_ref[:, :CH], cp_ref[:, :CH]
    )
    left_ref[:, :CH] = s.astype(BF16)
    left_ref[:, CH : CH + TILE] = spread(u0[:, :1])
    at = total - CH
    s = r_ref[:, at:] - op_chunk(
        u3[:, own - CH :], u3[:, own - CH - 1 : own - CH], 0.0, dg_ref[:, at:], cp_ref[:, at:]
    )
    right_ref[:, :CH] = s.astype(BF16)
    right_ref[:, CH : CH + TILE] = spread(u3[:, own - 1 :])


def edges(first, send, *refs):
    (core_ref, v_ref, gota_ref, gotb_ref, owna_ref, ownb_ref, metaa_ref, metab_ref) = refs[:8]
    (r_ref, dg_ref, cp_ref, L_ref) = refs[8:12]
    outs = refs[12 : 16 if send else 14]
    (gotl_ref, gotr_ref, ownl_ref, ownr_ref, metal_ref, metar_ref, sl_ref, sr_ref) = refs[-8:]
    total = v_ref.shape[1]
    subs, own, order = L_ref.shape
    wide = CH + TILE
    pick(core_ref, gota_ref, gotb_ref, gotl_ref, gotr_ref)
    pick(core_ref, owna_ref, ownb_ref, ownl_ref, ownr_ref)
    tile_l, tile_r = ownl_ref[:, :TILE], ownr_ref[:, CH - TILE : CH]
    halo_l, halo_r = gotl_ref[:, :CH], gotr_ref[:, :CH]
    if not first:
        pick(core_ref, metaa_ref, metab_ref, metal_ref, metar_ref)
        lane_t = lane_of(tile_l.shape)
        lane_h = lane_of(halo_l.shape)
        mine_l = column(ownl_ref[:, CH : CH + TILE], 0)
        mine_r = column(ownr_ref[:, CH : CH + TILE], 0)
        rim_l = column(gotl_ref[:, CH : CH + TILE], 0)
        rim_r = column(gotr_ref[:, CH : CH + TILE], 0)
        coup_l = column(metal_ref[:, CH : CH + TILE], 0)
        coup_r = column(metar_ref[:, CH : CH + TILE], 0)
        add = lambda x, lane, at, y: (x.astype(F32) + jnp.where(lane == at, y, 0.0)).astype(BF16)
        tile_l = add(tile_l, lane_t, 0, cp_ref[:, :1] * rim_l)
        tile_r = add(tile_r, lane_t, TILE - 1, cp_ref[:, total - 1 :] * rim_r)
        halo_l = add(halo_l, lane_h, CH - 1, coup_l * mine_l)
        halo_r = add(halo_r, lane_h, 0, coup_r * mine_r)
    u0 = v_ref[:, :own] + (
        dot_t(halo_l, L_ref[0, :, :CH]) + dot_t(tile_l, L_ref[0, :, CH:wide])
    )
    u3 = v_ref[:, total - own :] + (
        dot_t(halo_r, L_ref[subs - 1, :, order - CH :])
        + dot_t(tile_r, L_ref[subs - 1, :, order - wide : order - CH])
    )
    outs[0][...] = u0
    outs[1][...] = u3
    if send:
        edge_sends(r_ref, dg_ref, cp_ref, u0, u3, sl_ref, sr_ref)
        send_pair(core_ref, sl_ref, sr_ref, outs[2], outs[3])


def project(core_ref, v_ref, u0_ref, u3_ref, r_ref, dg_ref, cp_ref, basis_ref, metaa_ref, metab_ref,
            out_ref, metal_ref, metar_ref):
    rows, total = r_ref.shape
    own = basis_ref.shape[2]
    modes = basis_ref.shape[1]
    get = parts(v_ref, u0_ref, u3_ref, own)
    lane = lane_of((rows, TILE))
    pick(core_ref, metaa_ref, metab_ref, metal_ref, metar_ref)
    sums = []
    for lo, hi, cur, before, after in chunks_of(get, total):
        before = 0.0 if before is None else before
        after = 0.0 if after is None else after
        s = r_ref[:, lo:hi] - op_chunk(cur, before, after, dg_ref[:, lo:hi], cp_ref[:, lo:hi])
        j, k = lo // own, lo % own
        sums.append(dot_t(s.astype(BF16), basis_ref[j, :, k : k + CH]))
    per = own // CH
    pieces = []
    for j in range(total // own):
        p = sums[j * per]
        for k in range(1, per):
            p = p + sums[j * per + k]
        pieces.append(p)
    first, last = get(0, 1), get(total - 1, total)
    chosen = (lane == 2) | (lane == 3)
    for value, meta in ((first, metal_ref), (last, metar_ref)):
        hi, lo = split(value)
        coef = meta[:modes, CH : CH + TILE]
        pieces.append(
            dot_t(jnp.where(chosen, hi.astype(F32), 0.0).astype(BF16), coef)
            + dot_t(jnp.where(chosen, lo.astype(F32), 0.0).astype(BF16), coef)
        )
    rims = jnp.zeros((rows, 32), F32)
    lane32 = lane_of((rows, 32))
    for k, value in enumerate((first, last)):
        hi, lo = split(value)
        rims = jnp.where(lane32 == 2 * k, hi.astype(F32), rims)
        rims = jnp.where(lane32 == 2 * k + 1, lo.astype(F32), rims)
    chunk = jnp.concatenate(pieces + [rims], axis=1).astype(BF16)
    for d in range(out_ref.shape[0]):
        out_ref[d] = chunk


def coarse(send, core_ref, mine_ref, other_ref, W_ref, v_ref, u0_ref, u3_ref, r_ref, dg_ref, cp_ref,
           basis_ref, x_ref, image_ref, sums_ref, *rest):
    rows, total = r_ref.shape
    own = basis_ref.shape[2]
    modes = basis_ref.shape[1]
    get = parts(v_ref, u0_ref, u3_ref, own)
    count = mine_ref.shape[0]
    group = min(8, count)
    c = None
    for k in range(0, count, group):
        tiles = []
        for d in range(k, k + group):
            tiles += [mine_ref[d], other_ref[d]]
        p = dot_t(
            jnp.concatenate(tiles, axis=1), W_ref[:, 2 * k * TILE : 2 * (k + group) * TILE]
        )
        c = p if c is None else c + p
    subs = total // own
    for j in range(subs):
        hi, lo = split(c[:, j * modes : (j + 1) * modes])
        both = jnp.concatenate([hi, lo], axis=1)
        for k in range(0, own, CH):
            b = basis_ref[j, :, k : k + CH]
            at = j * own + k
            x_ref[:, at : at + CH] = get(at, at + CH) + jnp.dot(
                both, jnp.concatenate([b, b], axis=0), preferred_element_type=F32
            )
    n = subs * modes
    before = other_ref[core_ref[1]]
    after = other_ref[core_ref[2]]
    rim_l = column(before, 98) + c[:, n : n + 1]
    rim_r = column(after, 96) + c[:, n + 1 : n + 2]
    num = jnp.zeros((rows, 1), F32)
    den = jnp.zeros((rows, 1), F32)
    read = lambda lo, hi: x_ref[:, lo:hi]
    for lo, hi, cur, b, a in chunks_of(read, total):
        b = rim_l if b is None else b
        a = rim_r if a is None else a
        image = op_chunk(cur, b, a, dg_ref[:, lo:hi], cp_ref[:, lo:hi])
        image_ref[:, lo:hi] = image
        num = num + jnp.sum(r_ref[:, lo:hi] * image, axis=1, keepdims=True)
        den = den + jnp.sum(image * image, axis=1, keepdims=True)
    both = jnp.concatenate([num, den], axis=0)
    flat = jnp.transpose(jnp.broadcast_to(both, (2 * rows, 2 * rows)))
    sums_ref[...] = flat[: sums_ref.shape[0]]
    if send:
        a_ref, b_ref, left_ref, right_ref = rest
        left_ref[...] = image_ref[:, :CH].astype(BF16)
        right_ref[...] = image_ref[:, total - CH :].astype(BF16)
        send_pair(core_ref, left_ref, right_ref, a_ref, b_ref)


def step_of(sums_ref, rows):
    s = jnp.sum(sums_ref[...], axis=0, keepdims=True)
    t = jnp.transpose(jnp.broadcast_to(s, (2 * rows, 2 * rows)))
    return t[:rows, :1] / (t[rows:, :1] + 1e-6)


def second(core_ref, sums_ref, x_ref, image_ref, r_ref, ha0_ref, hb0_ref, ha_ref, hb_ref,
           dg_ref, cp_ref, L_ref, sol_ref, res_ref, u_ref, u0_ref, u3_ref, a_ref, b_ref,
           s_ref, sl_ref, sr_ref, hl0_ref, hr0_ref, hl_ref, hr_ref):
    rows, total = r_ref.shape
    own, order = L_ref.shape[1], L_ref.shape[2]
    alpha = step_of(sums_ref, rows)
    pick(core_ref, ha0_ref, hb0_ref, hl0_ref, hr0_ref)
    pick(core_ref, ha_ref, hb_ref, hl_ref, hr_ref)
    s_ref[:, :CH] = (hl0_ref[:, :CH].astype(F32) - alpha * hl_ref[...].astype(F32)).astype(BF16)
    s_ref[:, CH + total :] = (
        hr0_ref[:, :CH].astype(F32) - alpha * hr_ref[...].astype(F32)
    ).astype(BF16)
    for lo in range(0, total, CH):
        hi = lo + CH
        r = r_ref[:, lo:hi] - alpha * image_ref[:, lo:hi]
        res_ref[:, lo:hi] = r
        sol_ref[:, lo:hi] = alpha * x_ref[:, lo:hi]
        s_ref[:, CH + lo : CH + hi] = r.astype(BF16)
    subs = L_ref.shape[0]
    part = own // 2

    def step(n, carry):
        j, k = n // 2, n % 2
        p = dot_t(
            s_ref[:, pl.ds(pl.multiple_of(j * own, own), order)],
            L_ref[j, pl.ds(pl.multiple_of(k * part, part), part), :],
        )
        u_ref[:, pl.ds(pl.multiple_of(n * part, part), part)] = p
        return carry

    lax.fori_loop(0, 2 * subs, step, 0)
    u0 = u_ref[:, :own]
    u3 = u_ref[:, total - own :]
    u0_ref[...] = u0
    u3_ref[...] = u3
    edge_sends(res_ref, dg_ref, cp_ref, u0, u3, sl_ref, sr_ref)
    send_pair(core_ref, sl_ref, sr_ref, a_ref, b_ref)


def finish(sums_ref, x_ref, image_ref, r_ref, sol_in_ref, sol_ref, res_ref):
    rows, total = r_ref.shape
    alpha = step_of(sums_ref, rows)
    for lo in range(0, total, CH):
        hi = lo + CH
        res_ref[:, lo:hi] = r_ref[:, lo:hi] - alpha * image_ref[:, lo:hi]
        sol_ref[:, lo:hi] = sol_in_ref[:, lo:hi] + alpha * x_ref[:, lo:hi]


def call(kernel, name, outs, args, scratch=(), limit=8, flops=0, smem=1, specs=None):
    vmem = pl.BlockSpec(memory_space=pltpu.VMEM)
    size = sum(a.size * a.dtype.itemsize for a in args)
    return pl.pallas_call(
        kernel,
        out_shape=outs,
        in_specs=specs
        or [pl.BlockSpec(memory_space=pltpu.SMEM)] * smem + [vmem] * (len(args) - smem),
        out_specs=jax.tree.map(lambda _: vmem, outs),
        scratch_shapes=list(scratch),
        compiler_params=pltpu.CompilerParams(vmem_limit_bytes=limit << 20),
        cost_estimate=pl.CostEstimate(flops=flops, bytes_accessed=size, transcendentals=0),
        name=name,
    )(*args)


def body(right_side, diagonal, coupling, local_inverse, coarse_basis, coarse_inverse):
    rows, total = right_side.shape
    subs, own, order = local_inverse.shape
    modes = coarse_basis.shape[1]
    sectors = lax.axis_size("sector")
    chip = [(i, i ^ 1) for i in range(sectors)]
    side = [(i, (i + 1 if i % 2 else i - 1) % sectors) for i in range(sectors)]
    planes = [[2 * k + c for k in range(sectors // 2)] for c in range(2)]
    here = lax.axis_index("sector")
    core = jnp.stack(
        [
            here % 2,
            (here + sectors - 1) % sectors // 2,
            (here + 1) % sectors // 2,
            lax.axis_index("lift"),
        ]
    ).astype(jnp.int32)
    L, basis = local_inverse, coarse_basis
    r = right_side
    dg, cp = diagonal.reshape(1, total), coupling.reshape(1, total)
    wide = CH + TILE
    shape = jax.ShapeDtypeStruct
    full = shape((rows, total), F32)
    sub = shape((rows, own), F32)
    send = shape((rows, wide), BF16)
    long = shape((rows, wide + TILE), BF16)
    s_scratch = pltpu.VMEM((rows, total), BF16)
    pair = lambda like: [pltpu.VMEM(like.shape, like.dtype)] * 2
    work = 2 * rows * subs * own * order

    def exchange(a, b):
        got_b = lax.ppermute(b, "sector", side)
        got_a = lax.ppermute(a, "sector", chip)
        return got_a, got_b

    hbm = pl.BlockSpec(memory_space=pltpu.HBM)
    sa, sb = call(
        first_edges, "first_edges", [long, long], [core, r, cp, basis, coarse_inverse],
        [
            pltpu.VMEM((2, rows, CH), F32),
            pltpu.VMEM((2, 1, TILE), F32),
            pltpu.VMEM((2, modes, TILE), BF16),
            pltpu.VMEM((2, modes, coarse_inverse.shape[1]), F32),
        ]
        + pair(long)
        + [pltpu.SemaphoreType.DMA((8,))],
        specs=[pl.BlockSpec(memory_space=pltpu.SMEM)] + [hbm] * 4,
    )
    got_a0, got_b0 = exchange(sa, sb)
    v = call(middle_first, "middle_first", full, [r, L], [s_scratch], 8, work, 0)
    weights = []

    def sweeps(v, u0, u3, sa, sb, start):
        for sweep in range(start, SWEEPS):
            last = sweep == SWEEPS - 1
            if sweep == 0:
                vv, ga, gb = v, got_a0, got_b0
            else:
                ga, gb = exchange(sa, sb)
                vv = call(
                    middle, "middle", full, [r, v, u0, u3, dg, cp, L], [s_scratch], 8, work, 0
                )
            if sweep == 1 and not weights:
                ci, _ = lax.optimization_barrier((coarse_inverse, vv))
                lines = call(
                    lines_of, "lines", shape((ci.shape[0] + 8, ci.shape[1]), BF16),
                    [core, ci, got_a0, got_b0], pair(long),
                )
                other = lax.ppermute(lines, "lift", [(0, 1), (1, 0)])
                weights.append((lines, other))
            if sweep == 2 and len(weights) == 1:
                lines, other = weights[0]
                other, _ = lax.optimization_barrier((other, vv))
                weights.append(
                    call(
                        weave, "weave", shape((lines.shape[0], sectors * TILE), BF16),
                        [core, lines, other],
                        [pltpu.VMEM((lines.shape[0], 2 * lines.shape[1] + 2 * TILE), F32)],
                    )
                )
            first = sweep == 0
            outs = call(
                functools.partial(edges, first, not last), f"edges_{sweep}",
                [sub, sub] if last else [sub, sub, send, send],
                [core, vv, ga, gb, sa, sb, got_a0, got_b0, r, dg, cp, L],
                (pair(long) * 2 if first else pair(send) * 2) + pair(long) + pair(send),
                8, work // 8,
            )
            v, u0, u3 = vv, outs[0], outs[1]
            if not last:
                sa, sb = outs[2], outs[3]
        return v, u0, u3

    edge = shape((rows, CH), BF16)

    def coarse_step(v, u0, u3, sending):
        W = weights[1]
        chunk = call(
            project, "project", shape((sectors // 2, rows, TILE), BF16),
            [core, v, u0, u3, r, dg, cp, basis, got_a0, got_b0], pair(long),
        )
        chunk, W = lax.optimization_barrier((chunk, W))
        mine = lax.all_to_all(
            chunk, "sector", 0, 0, axis_index_groups=planes, tiled=True
        )
        other = lax.ppermute(mine, "sector", chip)
        return call(
            functools.partial(coarse, sending), "coarse",
            [full, full, shape((sectors, 2 * rows), F32)] + ([edge, edge] if sending else []),
            [core, mine, other, W, v, u0, u3, r, dg, cp, basis],
            pair(edge) if sending else (),
        )

    v, u0, u3 = sweeps(v, None, None, sa, sb, 0)
    x, image, sums, ia, ib = coarse_step(v, u0, u3, True)
    halo_a, halo_b = exchange(ia, ib)
    sums = lax.all_to_all(sums, "sector", 0, 0, tiled=True)
    sol, r, v, u0, u3, sa, sb = call(
        second, "second", [full, full, full, sub, sub, send, send],
        [core, sums, x, image, r, got_a0, got_b0, halo_a, halo_b, dg, cp, L],
        [pltpu.VMEM((rows, total + 2 * CH), BF16)] + pair(send) + pair(long) + pair(edge), 8, work,
    )
    v, u0, u3 = sweeps(v, u0, u3, sa, sb, 1)
    x, image, sums = coarse_step(v, u0, u3, False)
    sums = lax.all_to_all(sums, "sector", 0, 0, tiled=True)
    sol, res = call(finish, "finish", [full, full], [sums, x, image, r, sol], smem=0)
    return sol, res


def solution(mesh):
    in_specs = (
        P("lift", "sector"),
        P("sector"),
        P("sector"),
        P("sector", None, None),
        P("sector", None, None),
        P("sector", "lift"),
    )
    out_specs = (P("lift", "sector"), P("lift", "sector"))
    return jax.shard_map(body, mesh=mesh, in_specs=in_specs, out_specs=out_specs, check_vma=False)
```

profile of v0, /device:TPU:1, one launch (start us, length us, event | category | flops | bytes accessed | tf_op | source)
XLA Modules:
  0.0 195.7 jit_solution(6573013841107844691)
XLA Ops:
  0.6 0.0 copy-start.4
  0.7 0.1 pad_add_fusion.core_ref.refs_0_
  0.8 1.2 copy-done.1
  2.0 0.7 copy-done.3
  2.7 0.9 copy-done.6
  3.6 1.0 copy-done.8
  4.7 1.2 first_edges.1
  5.9 1.5 collective-permute-start
  7.3 2.8 %collective-permute-start.1 = (bf16[64,768]{1,0:T(8,128)(2,1)S(1)}, bf16[64,768]{1,0:T(8,128)(2,1)S(1)}, u32[]{:S(2)}, u32[]{:S(2)}) collective-permute-start(bf16[64,768]{1,0:T(8,128)(2,1)S(1)} %get-tuple-element.50.refs_5_), channel_id=1, source_target_pairs={{0,126},{2,4},{4,2},{6,8},{8,6},{10,12},{12,10},{14,16},{16,14},{1... | collective-permute-start | bytes 294920 | tf_op jit(solution)/shard_map/ppermute | solution.py:501
  10.2 5.8 %copy-done = bf16[4,1024,2048]{2,1,0:T(8,128)(2,1)S(1)} copy-done((bf16[4,1024,2048]{2,1,0:T(8,128)(2,1)S(1)}, bf16[4,1024,2048]{2,1,0:T(8,128)(2,1)}, u32[]{:S(2)}) %copy-start) | copy-done | bytes 16777240
  15.9 5.3 %middle_first.1.refs_1_.v_ref = f32[64,4096]{1,0:T(8,128)S(1)} custom-call(f32[64,4096]{1,0:T(8,128)S(1)} %copy-done.1, bf16[4,1024,2048]{2,1,0:T(8,128)(2,1)S(1)} %copy-done), custom_call_target="tpu_custom_call" | custom-call | flops 1073741824 | bytes 17825792 | tf_op jit(solution)/shard_map/middle_first/pallas_call | solution.py:457
  21.3 0.0 collective-permute-done.refs_2_.refs_6_.metaa_ref.a_ref.ha0_ref
  21.3 0.0 copy-start.9
  21.3 0.0 copy-start.2
  21.3 1.7 edges_0.1
  23.0 6.4 %collective-permute-start.2 = (bf16[64,640]{1,0:T(8,128)(2,1)S(1)}, bf16[64,640]{1,0:T(8,128)(2,1)S(1)}, u32[]{:S(2)}, u32[]{:S(2)}) collective-permute-start(bf16[64,640]{1,0:T(8,128)(2,1)S(1)} %get-tuple-element.53.refs_4_), channel_id=1, source_target_pairs={{0,2},{2,0},{4,6},{6,4},{8,10},{10,8},{12,14},{14,12},{16,18},{18,... | collective-permute-start | bytes 245768 | tf_op jit(solution)/shard_map/ppermute | solution.py:502
  29.5 6.1 %middle.6.refs_1_.v_ref = f32[64,4096]{1,0:T(8,128)S(1)} custom-call(f32[64,4096]{1,0:T(8,128)S(1)} %copy-done.1, f32[64,4096]{1,0:T(8,128)S(1)} %middle_first.1.refs_1_.v_ref, f32[64,1024]{1,0:T(8,128)S(1)} %get-tuple-element.51.u0_ref, f32[64,1024]{1,0:T(8,128)S(1)} %get-tuple-element.52.u3_ref, f32[1,4096]{1,0:T(1,128)S(1)} %bitcast.36, ...), custom_call_target="tpu_custom_call" | custom-call | flops 1073741824 | bytes 19431424 | tf_op jit(solution)/shard_map/middle/pallas_call | solution.py:457
  35.5 0.6 lines.1.mine_ref
  36.1 0.4 collective-permute-start.8
  36.5 1.8 edges_1.2
  38.4 2.7 %collective-permute-start.4 = (bf16[64,640]{1,0:T(8,128)(2,1)S(1)}, bf16[64,640]{1,0:T(8,128)(2,1)S(1)}, u32[]{:S(2)}, u32[]{:S(2)}) collective-permute-start(bf16[64,640]{1,0:T(8,128)(2,1)S(1)} %get-tuple-element.57.refs_4_), channel_id=1, source_target_pairs={{0,2},{2,0},{4,6},{6,4},{8,10},{10,8},{12,14},{14,12},{16,18},{18,... | collective-permute-start | bytes 245768 | tf_op jit(solution)/shard_map/ppermute | solution.py:502
  41.0 1.6 collective-permute-start.5
  42.7 6.1 %middle.7.refs_1_.v_ref = f32[64,4096]{1,0:T(8,128)S(1)} custom-call(f32[64,4096]{1,0:T(8,128)S(1)} %copy-done.2, f32[64,4096]{1,0:T(8,128)S(1)} %middle.6.refs_1_.v_ref, f32[64,1024]{1,0:T(8,128)S(1)} %get-tuple-element.55.u0_ref, f32[64,1024]{1,0:T(8,128)S(1)} %get-tuple-element.56.u3_ref, f32[1,4096]{1,0:T(1,128)S(1)} %bitcast.38, ...), custom_call_target="tpu_custom_call" | custom-call | flops 1073741824 | bytes 19431424 | tf_op jit(solution)/shard_map/middle/pallas_call | solution.py:457
  48.8 0.0 collective-permute-done.4.refs_2_
  48.8 1.8 edges_2.2
  50.6 4.1 %collective-permute-start.6 = (bf16[64,640]{1,0:T(8,128)(2,1)S(1)}, bf16[64,640]{1,0:T(8,128)(2,1)S(1)}, u32[]{:S(2)}, u32[]{:S(2)}) collective-permute-start(bf16[64,640]{1,0:T(8,128)(2,1)S(1)} %get-tuple-element.61.refs_4_), channel_id=1, source_target_pairs={{0,2},{2,0},{4,6},{6,4},{8,10},{10,8},{12,14},{14,12},{16,18},{18,... | collective-permute-start | bytes 245768 | tf_op jit(solution)/shard_map/ppermute | solution.py:502
  54.7 0.0 collective-permute-start.7
  54.7 6.1 %middle.8.refs_1_.v_ref = f32[64,4096]{1,0:T(8,128)S(1)} custom-call(f32[64,4096]{1,0:T(8,128)S(1)} %copy-done.2, f32[64,4096]{1,0:T(8,128)S(1)} %middle.7.refs_1_.v_ref, f32[64,1024]{1,0:T(8,128)S(1)} %get-tuple-element.59.u0_ref, f32[64,1024]{1,0:T(8,128)S(1)} %get-tuple-element.60.u3_ref, f32[1,4096]{1,0:T(1,128)S(1)} %bitcast.40, ...), custom_call_target="tpu_custom_call" | custom-call | flops 1073741824 | bytes 19431424 | tf_op jit(solution)/shard_map/middle/pallas_call | solution.py:457
  60.9 0.0 slice-start
  60.9 0.0 slice-start.1
  60.9 0.0 slice-start.2
  60.9 0.0 collective-permute-done.6.refs_2_
  60.9 0.0 collective-permute-done.7.refs_3_
  60.9 1.8 edges_3.2
  62.8 1.8 project.2
  64.5 0.0 slice-start.3
  64.5 0.0 collective-permute-done.8.other_ref
  64.5 3.6 %weave.1.W_ref = bf16[72,8192]{1,0:T(8,128)(2,1)S(1)} custom-call(s32[4]{0:T(128)S(1)} %pad_add_fusion.core_ref.refs_0_, bf16[72,2048]{1,0:T(8,128)(2,1)S(1)} %lines.1.mine_ref, bf16[72,2048]{1,0:T(8,128)(2,1)S(1)} %collective-permute-done.8.other_ref), custom_call_target="tpu_custom_call" | custom-call | bytes 589840 | tf_op jit(solution)/shard_map/weave/pallas_call | solution.py:457
  68.1 21.0 %all_to_all.32.mine_ref = bf16[32,64,128]{2,1,0:T(8,128)(2,1)S(1)} all-to-all(bf16[32,64,128]{2,1,0:T(8,128)(2,1)S(1)} %project.2), channel_id=1, replica_groups={{0,4,8,12,16,20,24,28,32,36,40,44,48,52,56,60,64,68,72,76,80,84,88,92,9..., dimensions={0} | all-to-all | bytes 1048576 | tf_op jit(solution)/shard_map/all_to_all | solution.py:572
  89.2 1.9 collective-permute-done.9.other_ref
  91.1 3.2 %coarse.2 = (f32[64,4096]{1,0:T(8,128)S(1)}, f32[64,4096]{1,0:T(8,128)S(1)}, f32[64,128]{1,0:T(8,128)S(1)}, bf16[64,512]{1,0:T(8,128)(2,1)S(1)}, bf16[64,512]{1,0:T(8,128)(2,1)S(1)}) custom-call(s32[4]{0:T(128)S(1)} %pad_add_fusion.core_ref.refs_0_, bf16[32,64,128]{2,1,0:T(8,128)(2,1)S(1)} %all_to_all.32.mine_ref, ...), custom_call_target="tpu_custom_call" | custom-call | bytes 5013520 | tf_op jit(solution)/shard_map/coarse/pallas_call | solution.py:457
  94.3 0.2 collective-permute-start.10
  94.5 0.5 collective-permute-start.11
  94.9 18.3 %all_to_all.33 = f32[64,1,128]{2,1,0:T(1,128)S(1)} all-to-all(f32[64,1,128]{2,1,0:T(1,128)S(1)} %bitcast.55), channel_id=1, replica_groups=mesh['sector'=64,'lift'=2] {'sector'}, dimensions={0} | all-to-all | bytes 65536 | tf_op jit(solution)/shard_map/all_to_all | solution.py:586
  113.2 0.0 collective-permute-done.10.ha_ref
  113.2 0.0 collective-permute-done.11.hb_ref
  113.3 7.4 %second.1 = (f32[64,4096]{1,0:T(8,128)S(1)}, f32[64,4096]{1,0:T(8,128)S(1)}, f32[64,4096]{1,0:T(8,128)S(1)}, f32[64,1024]{1,0:T(8,128)S(1)}, f32[64,1024]{1,0:T(...) custom-call(s32[4]{0:T(128)S(1)} %pad_add_fusion.core_ref.refs_0_, f32[64,128]{1,0:T(8,128)S(1)} %bitcast.53, ...), custom_call_target="tpu_custom_call" | custom-call | flops 1073741824 | bytes 20316176 | tf_op jit(solution)/shard_map/second/pallas_call | solution.py:457
  120.6 0.8 collective-permute-start.12
  121.5 0.2 collective-permute-start.13
  121.7 6.1 %middle.9.refs_1_.v_ref = f32[64,4096]{1,0:T(8,128)S(1)} custom-call(f32[64,4096]{1,0:T(8,128)S(1)} %get-tuple-element.74.r_ref.refs_8_, f32[64,4096]{1,0:T(8,128)S(1)} %get-tuple-element.75.v_ref, f32[64,1024]{1,0:T(8,128)S(1)} %get-tuple-element.76.u0_ref, f32[64,1024]{1,0:T(8,128)S(1)} %get-tuple-element.77.u3_ref, f32[1,4096]{1,0:T(1,128)S(1)} %bitcast.45, ...), custom_call_target="tpu_custom_call" | custom-call | flops 1073741824 | bytes 19431424 | tf_op jit(solution)/shard_map/middle/pallas_call | solution.py:457
  127.9 1.8 edges_1.3
  129.7 3.4 %collective-permute-start.14 = (bf16[64,640]{1,0:T(8,128)(2,1)S(1)}, bf16[64,640]{1,0:T(8,128)(2,1)S(1)}, u32[]{:S(2)}, u32[]{:S(2)}) collective-permute-start(bf16[64,640]{1,0:T(8,128)(2,1)S(1)} %get-tuple-element.82.refs_4_), channel_id=1, source_target_pairs={{0,2},{2,0},{4,6},{6,4},{8,10},{10,8},{12,14},{14,12},{16,18},{18,... | collective-permute-start | bytes 245768 | tf_op jit(solution)/shard_map/ppermute | solution.py:502
  133.1 0.0 collective-permute-start.15
  133.1 6.1 %middle.10.refs_1_.v_ref = f32[64,4096]{1,0:T(8,128)S(1)} custom-call(f32[64,4096]{1,0:T(8,128)S(1)} %get-tuple-element.74.r_ref.refs_8_, f32[64,4096]{1,0:T(8,128)S(1)} %middle.9.refs_1_.v_ref, f32[64,1024]{1,0:T(8,128)S(1)} %get-tuple-element.80.u0_ref, f32[64,1024]{1,0:T(8,128)S(1)} %get-tuple-element.81.u3_ref, f32[1,4096]{1,0:T(1,128)S(1)} %bitcast.47, ...), custom_call_target="tpu_custom_call" | custom-call | flops 1073741824 | bytes 19431424 | tf_op jit(solution)/shard_map/middle/pallas_call | solution.py:457
  139.3 1.8 edges_2.3
  141.1 4.4 %collective-permute-start.16 = (bf16[64,640]{1,0:T(8,128)(2,1)S(1)}, bf16[64,640]{1,0:T(8,128)(2,1)S(1)}, u32[]{:S(2)}, u32[]{:S(2)}) collective-permute-start(bf16[64,640]{1,0:T(8,128)(2,1)S(1)} %get-tuple-element.86.refs_4_), channel_id=1, source_target_pairs={{0,2},{2,0},{4,6},{6,4},{8,10},{10,8},{12,14},{14,12},{16,18},{18,... | collective-permute-start | bytes 245768 | tf_op jit(solution)/shard_map/ppermute | solution.py:502
  145.5 6.1 %middle.11.refs_1_.v_ref = f32[64,4096]{1,0:T(8,128)S(1)} custom-call(f32[64,4096]{1,0:T(8,128)S(1)} %get-tuple-element.74.r_ref.refs_8_, f32[64,4096]{1,0:T(8,128)S(1)} %middle.10.refs_1_.v_ref, f32[64,1024]{1,0:T(8,128)S(1)} %get-tuple-element.84.u0_ref, f32[64,1024]{1,0:T(8,128)S(1)} %get-tuple-element.85.u3_ref, f32[1,4096]{1,0:T(1,128)S(1)} %bitcast.49, ...), custom_call_target="tpu_custom_call" | custom-call | flops 1073741824 | bytes 19431424 | tf_op jit(solution)/shard_map/middle/pallas_call | solution.py:457
  151.6 1.7 edges_3.3
  153.3 1.8 project.3
  155.0 21.0 %all_to_all.34.mine_ref = bf16[32,64,128]{2,1,0:T(8,128)(2,1)S(1)} all-to-all(bf16[32,64,128]{2,1,0:T(8,128)(2,1)S(1)} %project.3), channel_id=1, replica_groups={{0,4,8,12,16,20,24,28,32,36,40,44,48,52,56,60,64,68,72,76,80,84,88,92,9..., dimensions={0} | all-to-all | bytes 1048576 | tf_op jit(solution)/shard_map/all_to_all | solution.py:572
  176.1 1.9 collective-permute-done.18.other_ref
  178.0 3.1 %coarse.3 = (f32[64,4096]{1,0:T(8,128)S(1)}, f32[64,4096]{1,0:T(8,128)S(1)}, f32[64,128]{1,0:T(8,128)S(1)}) custom-call(s32[4]{0:T(128)S(1)} %pad_add_fusion.core_ref.refs_0_, bf16[32,64,128]{2,1,0:T(8,128)(2,1)S(1)} %all_to_all.34.mine_ref, bf16[32,64,128]{2,1,0:T(8,128)(2,1)S(1)} %collective-permute-done.18.other_ref, bf16[72,8192]{1,0:T(8,128)(2,1)S(1)} %weave.1.W_ref, ...), custom_call_target="tpu_custom_call" | custom-call | bytes 5013520 | tf_op jit(solution)/shard_map/coarse/pallas_call | solution.py:457
  181.1 12.9 %all_to_all.35 = f32[64,1,128]{2,1,0:T(1,128)S(1)} all-to-all(f32[64,1,128]{2,1,0:T(1,128)S(1)} %bitcast.56), channel_id=1, replica_groups=mesh['sector'=64,'lift'=2] {'sector'}, dimensions={0} | all-to-all | bytes 65536 | tf_op jit(solution)/shard_map/all_to_all | solution.py:594
  194.0 1.7 finish.1
  (31 shorter events, 0.1 us)
Async XLA Ops:
  0.6 20.7 %copy-start.4 = (f32[4096]{0:T(1024)S(1)}, f32[4096]{0:T(1024)}, u32[]{:S(2)}) copy-start(f32[4096]{0:T(1024)} %param.8) | copy-start | bytes 49156
  0.6 20.7 %copy-start.5 = (f32[4096]{0:T(1024)S(1)}, f32[4096]{0:T(1024)}, u32[]{:S(2)}) copy-start(f32[4096]{0:T(1024)} %param.7) | copy-start | bytes 49156
  0.8 1.2 copy-start.1
  2.0 0.7 copy-start.3
  2.7 0.9 copy-start.6
  3.6 1.0 copy-start.8
  5.9 15.4 %collective-permute-start = (bf16[64,768]{1,0:T(8,128)(2,1)S(1)}, bf16[64,768]{1,0:T(8,128)(2,1)S(1)}, u32[]{:S(2)}, u32[]{:S(2)}) collective-permute-start(bf16[64,768]{1,0:T(8,128)(2,1)S(1)} %get-tuple-element.49.refs_4_), channel_id=1, source_target_pairs={{0,2},{2,0},{4,6},{6,4},{8,10},{10,8},{12,14},{14,12},{16,18},{18,... | collective-permute-start | bytes 294920 | tf_op jit(solution)/shard_map/ppermute | solution.py:502
  7.3 14.0 %collective-permute-start.1 = (bf16[64,768]{1,0:T(8,128)(2,1)S(1)}, bf16[64,768]{1,0:T(8,128)(2,1)S(1)}, u32[]{:S(2)}, u32[]{:S(2)}) collective-permute-start(bf16[64,768]{1,0:T(8,128)(2,1)S(1)} %get-tuple-element.50.refs_5_), channel_id=1, source_target_pairs={{0,126},{2,4},{4,2},{6,8},{8,6},{10,12},{12,10},{14,16},{16,14},{1... | collective-permute-start | bytes 294920 | tf_op jit(solution)/shard_map/ppermute | solution.py:501
  10.2 5.8 %copy-start = (bf16[4,1024,2048]{2,1,0:T(8,128)(2,1)S(1)}, bf16[4,1024,2048]{2,1,0:T(8,128)(2,1)}, u32[]{:S(2)}) copy-start(bf16[4,1024,2048]{2,1,0:T(8,128)(2,1)} %refs_11_.13) | copy-start | bytes 50331652
  21.3 14.2 %copy-start.9 = (f32[64,2048]{1,0:T(8,128)S(1)}, f32[64,2048]{1,0:T(8,128)}, u32[]{:S(2)}) copy-start(f32[64,2048]{1,0:T(8,128)} %ci_ref) | copy-start | bytes 1572868
  21.3 15.2 %copy-start.2 = (f32[64,4096]{1,0:T(8,128)S(1)}, f32[64,4096]{1,0:T(8,128)}, u32[]{:S(2)}) copy-start(f32[64,4096]{1,0:T(8,128)} %r_ref.13) | copy-start | bytes 3145732
  23.0 13.5 %collective-permute-start.2 = (bf16[64,640]{1,0:T(8,128)(2,1)S(1)}, bf16[64,640]{1,0:T(8,128)(2,1)S(1)}, u32[]{:S(2)}, u32[]{:S(2)}) collective-permute-start(bf16[64,640]{1,0:T(8,128)(2,1)S(1)} %get-tuple-element.53.refs_4_), channel_id=1, source_target_pairs={{0,2},{2,0},{4,6},{6,4},{8,10},{10,8},{12,14},{14,12},{16,18},{18,... | collective-permute-start | bytes 245768 | tf_op jit(solution)/shard_map/ppermute | solution.py:502
  29.5 7.1 %collective-permute-start.3 = (bf16[64,640]{1,0:T(8,128)(2,1)S(1)}, bf16[64,640]{1,0:T(8,128)(2,1)S(1)}, u32[]{:S(2)}, u32[]{:S(2)}) collective-permute-start(bf16[64,640]{1,0:T(8,128)(2,1)S(1)} %get-tuple-element.54.refs_5_), channel_id=1, source_target_pairs={{0,126},{2,4},{4,2},{6,8},{8,6},{10,12},{12,10},{14,16},{16,14},{1... | collective-permute-start | bytes 245768 | tf_op jit(solution)/shard_map/ppermute | solution.py:501
  36.1 28.4 %collective-permute-start.8 = (bf16[72,2048]{1,0:T(8,128)(2,1)S(1)}, bf16[72,2048]{1,0:T(8,128)(2,1)S(1)}, u32[]{:S(2)}, u32[]{:S(2)}) collective-permute-start(bf16[72,2048]{1,0:T(8,128)(2,1)S(1)} %lines.1.mine_ref), channel_id=1, source_target_pairs={{0,1},{1,0},{2,3},{3,2},{4,5},{5,4},{6,7},{7,6},{8,9},{9,8},{10,11... | collective-permute-start | bytes 884744 | tf_op jit(solution)/shard_map/ppermute | solution.py:538
  38.4 10.4 %collective-permute-start.4 = (bf16[64,640]{1,0:T(8,128)(2,1)S(1)}, bf16[64,640]{1,0:T(8,128)(2,1)S(1)}, u32[]{:S(2)}, u32[]{:S(2)}) collective-permute-start(bf16[64,640]{1,0:T(8,128)(2,1)S(1)} %get-tuple-element.57.refs_4_), channel_id=1, source_target_pairs={{0,2},{2,0},{4,6},{6,4},{8,10},{10,8},{12,14},{14,12},{16,18},{18,... | collective-permute-start | bytes 245768 | tf_op jit(solution)/shard_map/ppermute | solution.py:502
  41.0 7.7 %collective-permute-start.5 = (bf16[64,640]{1,0:T(8,128)(2,1)S(1)}, bf16[64,640]{1,0:T(8,128)(2,1)S(1)}, u32[]{:S(2)}, u32[]{:S(2)}) collective-permute-start(bf16[64,640]{1,0:T(8,128)(2,1)S(1)} %get-tuple-element.58.refs_5_), channel_id=1, source_target_pairs={{0,126},{2,4},{4,2},{6,8},{8,6},{10,12},{12,10},{14,16},{16,14},{1... | collective-permute-start | bytes 245768 | tf_op jit(solution)/shard_map/ppermute | solution.py:501
  50.6 10.3 %collective-permute-start.6 = (bf16[64,640]{1,0:T(8,128)(2,1)S(1)}, bf16[64,640]{1,0:T(8,128)(2,1)S(1)}, u32[]{:S(2)}, u32[]{:S(2)}) collective-permute-start(bf16[64,640]{1,0:T(8,128)(2,1)S(1)} %get-tuple-element.61.refs_4_), channel_id=1, source_target_pairs={{0,2},{2,0},{4,6},{6,4},{8,10},{10,8},{12,14},{14,12},{16,18},{18,... | collective-permute-start | bytes 245768 | tf_op jit(solution)/shard_map/ppermute | solution.py:502
  54.7 6.2 %collective-permute-start.7 = (bf16[64,640]{1,0:T(8,128)(2,1)S(1)}, bf16[64,640]{1,0:T(8,128)(2,1)S(1)}, u32[]{:S(2)}, u32[]{:S(2)}) collective-permute-start(bf16[64,640]{1,0:T(8,128)(2,1)S(1)} %get-tuple-element.62.refs_5_), channel_id=1, source_target_pairs={{0,126},{2,4},{4,2},{6,8},{8,6},{10,12},{12,10},{14,16},{16,14},{1... | collective-permute-start | bytes 245768 | tf_op jit(solution)/shard_map/ppermute | solution.py:501
  54.7 8.0 %copy-start.7 = (bf16[4,16,1024]{2,1,0:T(8,128)(2,1)S(1)}, bf16[4,16,1024]{2,1,0:T(8,128)(2,1)}, u32[]{:S(2)}) copy-start(bf16[4,16,1024]{2,1,0:T(8,128)(2,1)} %basis_ref.7) | copy-start | bytes 393220
  60.9 52.4 %slice-start = ((s8[16777216]{0:T(1024)(128)(4,1)}), s8[4194304]{0:T(1024)(128)(4,1)S(1)}, s32[]{:S(2)}) async-start(s8[16777216]{0:T(1024)(128)(4,1)} %bitcast.14), calls=%async_computation.4 | async-start | bytes 8388608
  60.9 52.4 %slice-start.1 = ((s8[16777216]{0:T(1024)(128)(4,1)}), s8[4194304]{0:T(1024)(128)(4,1)S(1)}, s32[]{:S(2)}) async-start(s8[16777216]{0:T(1024)(128)(4,1)} %bitcast.14), calls=%async_computation.5 | async-start | bytes 8388608
  60.9 52.4 %slice-start.2 = ((s8[16777216]{0:T(1024)(128)(4,1)}), s8[4194304]{0:T(1024)(128)(4,1)S(1)}, s32[]{:S(2)}) async-start(s8[16777216]{0:T(1024)(128)(4,1)} %bitcast.14), calls=%async_computation.6 | async-start | bytes 8388608
  64.5 48.8 %slice-start.3 = ((s8[16777216]{0:T(1024)(128)(4,1)}), s8[4194304]{0:T(1024)(128)(4,1)S(1)}, s32[]{:S(2)}) async-start(s8[16777216]{0:T(1024)(128)(4,1)} %bitcast.14), calls=%async_computation.7 | async-start | bytes 8388608
  89.2 1.9 collective-permute-start.9
  94.3 19.0 %collective-permute-start.10 = (bf16[64,512]{1,0:T(8,128)(2,1)S(1)}, bf16[64,512]{1,0:T(8,128)(2,1)S(1)}, u32[]{:S(2)}, u32[]{:S(2)}) collective-permute-start(bf16[64,512]{1,0:T(8,128)(2,1)S(1)} %get-tuple-element.72), channel_id=1, source_target_pairs={{0,2},{2,0},{4,6},{6,4},{8,10},{10,8},{12,14},{14,12},{16,18},{18,... | collective-permute-start | bytes 196616 | tf_op jit(solution)/shard_map/ppermute | solution.py:502
  94.5 18.8 %collective-permute-start.11 = (bf16[64,512]{1,0:T(8,128)(2,1)S(1)}, bf16[64,512]{1,0:T(8,128)(2,1)S(1)}, u32[]{:S(2)}, u32[]{:S(2)}) collective-permute-start(bf16[64,512]{1,0:T(8,128)(2,1)S(1)} %get-tuple-element.73), channel_id=1, source_target_pairs={{0,126},{2,4},{4,2},{6,8},{8,6},{10,12},{12,10},{14,16},{16,14},{1... | collective-permute-start | bytes 196616 | tf_op jit(solution)/shard_map/ppermute | solution.py:501
  120.6 7.2 %collective-permute-start.12 = (bf16[64,640]{1,0:T(8,128)(2,1)S(1)}, bf16[64,640]{1,0:T(8,128)(2,1)S(1)}, u32[]{:S(2)}, u32[]{:S(2)}) collective-permute-start(bf16[64,640]{1,0:T(8,128)(2,1)S(1)} %get-tuple-element.78.refs_4_), channel_id=1, source_target_pairs={{0,2},{2,0},{4,6},{6,4},{8,10},{10,8},{12,14},{14,12},{16,18},{18,... | collective-permute-start | bytes 245768 | tf_op jit(solution)/shard_map/ppermute | solution.py:502
  121.5 6.4 %collective-permute-start.13 = (bf16[64,640]{1,0:T(8,128)(2,1)S(1)}, bf16[64,640]{1,0:T(8,128)(2,1)S(1)}, u32[]{:S(2)}, u32[]{:S(2)}) collective-permute-start(bf16[64,640]{1,0:T(8,128)(2,1)S(1)} %get-tuple-element.79.refs_5_), channel_id=1, source_target_pairs={{0,126},{2,4},{4,2},{6,8},{8,6},{10,12},{12,10},{14,16},{16,14},{1... | collective-permute-start | bytes 245768 | tf_op jit(solution)/shard_map/ppermute | solution.py:501
  129.7 9.5 %collective-permute-start.14 = (bf16[64,640]{1,0:T(8,128)(2,1)S(1)}, bf16[64,640]{1,0:T(8,128)(2,1)S(1)}, u32[]{:S(2)}, u32[]{:S(2)}) collective-permute-start(bf16[64,640]{1,0:T(8,128)(2,1)S(1)} %get-tuple-element.82.refs_4_), channel_id=1, source_target_pairs={{0,2},{2,0},{4,6},{6,4},{8,10},{10,8},{12,14},{14,12},{16,18},{18,... | collective-permute-start | bytes 245768 | tf_op jit(solution)/shard_map/ppermute | solution.py:502
  133.1 6.2 %collective-permute-start.15 = (bf16[64,640]{1,0:T(8,128)(2,1)S(1)}, bf16[64,640]{1,0:T(8,128)(2,1)S(1)}, u32[]{:S(2)}, u32[]{:S(2)}) collective-permute-start(bf16[64,640]{1,0:T(8,128)(2,1)S(1)} %get-tuple-element.83.refs_5_), channel_id=1, source_target_pairs={{0,126},{2,4},{4,2},{6,8},{8,6},{10,12},{12,10},{14,16},{16,14},{1... | collective-permute-start | bytes 245768 | tf_op jit(solution)/shard_map/ppermute | solution.py:501
  141.1 10.5 %collective-permute-start.16 = (bf16[64,640]{1,0:T(8,128)(2,1)S(1)}, bf16[64,640]{1,0:T(8,128)(2,1)S(1)}, u32[]{:S(2)}, u32[]{:S(2)}) collective-permute-start(bf16[64,640]{1,0:T(8,128)(2,1)S(1)} %get-tuple-element.86.refs_4_), channel_id=1, source_target_pairs={{0,2},{2,0},{4,6},{6,4},{8,10},{10,8},{12,14},{14,12},{16,18},{18,... | collective-permute-start | bytes 245768 | tf_op jit(solution)/shard_map/ppermute | solution.py:502
  145.5 6.2 %collective-permute-start.17 = (bf16[64,640]{1,0:T(8,128)(2,1)S(1)}, bf16[64,640]{1,0:T(8,128)(2,1)S(1)}, u32[]{:S(2)}, u32[]{:S(2)}) collective-permute-start(bf16[64,640]{1,0:T(8,128)(2,1)S(1)} %get-tuple-element.87.refs_5_), channel_id=1, source_target_pairs={{0,126},{2,4},{4,2},{6,8},{8,6},{10,12},{12,10},{14,16},{16,14},{1... | collective-permute-start | bytes 245768 | tf_op jit(solution)/shard_map/ppermute | solution.py:501
  176.1 1.9 collective-permute-start.18
where the time goes:
time: 196 us
  Pallas kernels  78.7 us (40%)
  blocking collectives  73.3 us (37%)
  starting transfers between devices  29.1 us (15%)
  local copies, waits for them, and re-layouts  9.71 us (5%)
  waiting for transfers between devices  3.86 us (2%)
    pallas_call x23, Pallas kernels, call(): pl.pallas_call(kernel, out_shape=outs, in_specs=specs or [pl.BlockSpec(me...  78.7 us
    all_to_all x2, blocking collectives, coarse_step(): lax.all_to_all(chunk, 'sector', 0, 0, axis_index_groups=planes, tiled=True)  42.1 us
    all_to_all x2, blocking collectives, body(): sums = lax.all_to_all(sums, 'sector', 0, 0, tiled=True)  31.2 us
    ppermute x8, starting transfers between devices, exchange(): got_a = lax.ppermute(a, 'sector', chip)  23.4 us
    unnamed x28, local copies, waits for them, and re-layouts  9.71 us
    ppermute x8, starting transfers between devices, exchange(): got_b = lax.ppermute(b, 'sector', side)  5.21 us
  transfers between devices with their start and end apart: 19, of which 2 were waited for; matrix products, arithmetic and copies ran while one was open for 0% of the time, Pallas kernels for 25%

commit v1 on v0

--- a/solution.py
+++ b/solution.py
@@ -11,6 +11,8 @@
 F32, BF16 = jnp.float32, jnp.bfloat16
 CH = 512
 TILE = 128
+EDGE_LIMIT = 57
+FIRST_LIMIT = 20
 
 
 def lane_of(shape):
@@ -37,33 +39,62 @@
     return tile[:, at : at + 1].astype(F32) + tile[:, at + 1 : at + 2].astype(F32)
 
 
-def op_chunk(cur, before, after, dg, cp):
-    width = cur.shape[1]
-    lane = lane_of(cur.shape)
-    left = jnp.where(lane == 0, before, pltpu.roll(cur, 1, 1))
-    right = jnp.where(lane == width - 1, after, pltpu.roll(cur, width - 1, 1))
-    return dg * cur - cp * (left + right)
+GROUP = 16
+
+
+def by_rows(rows, run):
+    def step(g, carry):
+        run(pl.ds(pl.multiple_of(g * GROUP, GROUP), GROUP))
+        return carry
+
+    lax.fori_loop(0, rows // GROUP, step, 0)
+
+
+def operator(read, first, last, total, coefs, before, after, emit):
+    dg_ref, cp_ref = coefs
+    lane = lane_of((GROUP, TILE))
+    cur = read(first)
+    down = pltpu.roll(cur, TILE - 1, 1)
+    prev = before if before is not None else pltpu.roll(read(first - 1), 1, 1)
+    for t in range(first, last):
+        up = pltpu.roll(cur, 1, 1)
+        if t + 1 < last or after is None:
+            ahead = read(t + 1)
+            ahead_down = pltpu.roll(ahead, TILE - 1, 1)
+        else:
+            ahead, ahead_down = None, after
+        left = jnp.where(lane == 0, prev, up)
+        right = jnp.where(lane == TILE - 1, ahead_down, down)
+        cols = slice(total + t * TILE, total + (t + 1) * TILE)
+        emit(t, cur, dg_ref[:, cols] * cur - cp_ref[:, cols] * (left + right))
+        cur, down, prev = ahead, ahead_down, up
 
 
 def parts(v_ref, u0_ref, u3_ref, own):
-    total = v_ref.shape[1]
-
-    def get(lo, hi):
-        if hi <= own:
-            return u0_ref[:, lo:hi]
-        if lo >= total - own:
-            return u3_ref[:, lo - (total - own) : hi - (total - own)]
-        return v_ref[:, lo:hi]
+    tiles, outer = v_ref.shape[1] // TILE, own // TILE
+
+    def get(rows, t):
+        if t < outer:
+            return u0_ref[rows, t * TILE : (t + 1) * TILE]
+        if t >= tiles - outer:
+            t = t - (tiles - outer)
+            return u3_ref[rows, t * TILE : (t + 1) * TILE]
+        return v_ref[rows, t * TILE : (t + 1) * TILE]
 
     return get
 
 
-def chunks_of(get, total):
-    for lo in range(0, total, CH):
-        hi = lo + CH
-        before = get(lo - 1, lo) if lo > 0 else None
-        after = get(hi, hi + 1) if hi < total else None
-        yield lo, hi, get(lo, hi), before, after
+def sweep_residual(r_ref, get, coefs, s_ref):
+    rows, total = r_ref.shape
+
+    def run(group):
+        def emit(t, cur, image):
+            cols = slice(t * TILE, (t + 1) * TILE)
+            s_ref[group, cols] = (r_ref[group, cols] - image).astype(BF16)
+
+        operator(lambda t: get(group, t), 0, total // TILE, 0, coefs, 0.0, 0.0, emit)
+
+    by_rows(rows, run)
 
 
 def pick(core_ref, a_ref, b_ref, left_ref, right_ref):
@@ -117,19 +148,16 @@
         out[:count, CH + TILE :] = jnp.concatenate(
             [line[:, n * TILE : (n + 1) * TILE] for n in range(count)], axis=0
         ).astype(BF16)
-    send_pair(core_ref, left_ref, right_ref, a_ref, b_ref)
-
-
-def send_pair(core_ref, left_ref, right_ref, a_ref, b_ref):
-    @pl.when(core_ref[0] == 0)
-    def _():
-        a_ref[...] = right_ref[...]
-        b_ref[...] = left_ref[...]
-
-    @pl.when(core_ref[0] != 0)
-    def _():
-        a_ref[...] = left_ref[...]
-        b_ref[...] = right_ref[...]
+    def send(even):
+        a_ref[...] = (right_ref if even else left_ref)[...]
+        b_ref[...] = (left_ref if even else right_ref)[...]
+
+    by_side(core_ref, send)
+
+
+def by_side(core_ref, run):
+    pl.when(core_ref[0] == 0)(lambda: run(True))
+    pl.when(core_ref[0] != 0)(lambda: run(False))
 
 
 def lines_of(core_ref, ci_ref, a_ref, b_ref, out_ref, left_ref, right_ref):
@@ -183,10 +211,10 @@
         ).astype(BF16)
         return carry
 
-    lax.fori_loop(0, 2 * half // TILE, step, 0)
-
-
-def products(s_ref, L_ref, own, order, store):
+    lax.fori_loop(0, 2 * half // TILE, step, 0, unroll=min(4, 2 * half // TILE))
+
+
+def products(s_ref, L_ref, own, order, store, ready=None):
     total = s_ref.shape[1]
     margin = (order - own) // 2
     subs = L_ref.shape[0]
@@ -210,126 +238,154 @@
 
     def inner(n, carry):
         j, k = 1 + n // 2, n % 2
+        if ready is not None:
+            pl.when(k == 0)(lambda: ready(j))
         start = pl.multiple_of(j * own - margin, TILE)
         p = dot_t(s_ref[:, pl.ds(start, order)], L_ref[j, rows_at(k), :])
         store(pl.multiple_of(j * own + k * part, part), part, p)
         return carry
 
+    if ready is not None:
+        ready(0)
     lax.fori_loop(0, 2, first, 0)
     lax.fori_loop(0, 2 * (subs - 2), inner, 0)
+    if ready is not None:
+        ready(subs - 1)
     lax.fori_loop(0, 2, last, 0)
 
 
-def middle_first(r_ref, L_ref, v_ref, s_ref):
-    own, order = L_ref.shape[1], L_ref.shape[2]
+def middle_first(r_ref, L_hbm, v_ref, L_ref, s_ref, sem):
+    subs, own, order = L_ref.shape
+
+    def copy(j):
+        return pltpu.make_async_copy(L_hbm.at[j], L_ref.at[j], sem.at[j])
+
+    for j in range(subs):
+        copy(j).start()
     s_ref[...] = r_ref[...].astype(BF16)
 
     def store(at, size, p):
         v_ref[:, pl.ds(at, size)] = p
 
-    products(s_ref, L_ref, own, order, store)
+    products(s_ref, L_ref, own, order, store, lambda j: copy(j).wait())
 
 
 def middle(r_ref, v_ref, u0_ref, u3_ref, dg_ref, cp_ref, L_ref, out_ref, s_ref):
-    own, order = L_ref.shape[1], L_ref.shape[2]
-    get = parts(v_ref, u0_ref, u3_ref, own)
-    for lo, hi, cur, before, after in chunks_of(get, r_ref.shape[1]):
-        before = 0.0 if before is None else before
-        after = 0.0 if after is None else after
-        s = r_ref[:, lo:hi] - op_chunk(cur, before, after, dg_ref[:, lo:hi], cp_ref[:, lo:hi])
-        s_ref[:, lo:hi] = s.astype(BF16)
-        out_ref[:, lo:hi] = cur
-
-    def store(at, size, p):
-        out_ref[:, pl.ds(at, size)] += p
-
-    products(s_ref, L_ref, own, order, store)
-
-
-def edge_sends(r_ref, dg_ref, cp_ref, u0, u3, left_ref, right_ref):
+    subs, own, order = L_ref.shape
     total = r_ref.shape[1]
-    own = u0.shape[1]
-    s = r_ref[:, :CH] - op_chunk(
-        u0[:, :CH], 0.0, u0[:, CH : CH + 1], dg_ref[:, :CH], cp_ref[:, :CH]
-    )
-    left_ref[:, :CH] = s.astype(BF16)
-    left_ref[:, CH : CH + TILE] = spread(u0[:, :1])
-    at = total - CH
-    s = r_ref[:, at:] - op_chunk(
-        u3[:, own - CH :], u3[:, own - CH - 1 : own - CH], 0.0, dg_ref[:, at:], cp_ref[:, at:]
-    )
-    right_ref[:, :CH] = s.astype(BF16)
-    right_ref[:, CH : CH + TILE] = spread(u3[:, own - 1 :])
-
-
-def edges(first, send, *refs):
+    margin = (order - own) // 2
+    sweep_residual(r_ref, parts(v_ref, u0_ref, u3_ref, own), (dg_ref, cp_ref), s_ref)
+
+    def inner(j, carry):
+        at = pl.multiple_of(j * own, own)
+        p = dot_t(s_ref[:, pl.ds(pl.multiple_of(at - margin, TILE), order)], L_ref[j])
+        out_ref[:, pl.ds(at, own)] = v_ref[:, pl.ds(at, own)] + p
+        return carry
+
+    lax.fori_loop(1, subs - 1, inner, 0)
+    for j, u_ref in ((0, u0_ref), (subs - 1, u3_ref)):
+        at = j * own
+        lo = at - margin
+        a, b = max(lo, TILE), min(lo + order, total - TILE)
+        out_ref[:, at : at + own] = u_ref[...] + dot_t(
+            s_ref[:, a:b], L_ref[j, :, a - lo : b - lo]
+        )
+
+
+def edge_sends(r_ref, dg_ref, cp_ref, u0_ref, u3_ref, left_ref, right_ref):
+    rows, total = r_ref.shape
+    own = u0_ref.shape[1]
+    count, tiles = CH // TILE, own // TILE
+    shift = total - own
+
+    def run(group):
+        def left(t, cur, image):
+            cols = slice(t * TILE, (t + 1) * TILE)
+            left_ref[group, cols] = (r_ref[group, cols] - image).astype(BF16)
+
+        def right(t, cur, image):
+            cols = slice(shift + t * TILE, shift + (t + 1) * TILE)
+            k = (t - (tiles - count)) * TILE
+            right_ref[group, k : k + TILE] = (r_ref[group, cols] - image).astype(BF16)
+
+        read = lambda ref: lambda t: ref[group, t * TILE : (t + 1) * TILE]
+        operator(read(u0_ref), 0, count, 0, (dg_ref, cp_ref), 0.0, None, left)
+        operator(
+            read(u3_ref), tiles - count, tiles, shift, (dg_ref, cp_ref), None, 0.0, right
+        )
+
+    by_rows(rows, run)
+    left_ref[:, CH : CH + TILE] = spread(u0_ref[:, :1])
+    right_ref[:, CH : CH + TILE] = spread(u3_ref[:, own - 1 :])
+
+
+def edges(first, *refs):
     (core_ref, v_ref, gota_ref, gotb_ref, owna_ref, ownb_ref, metaa_ref, metab_ref) = refs[:8]
-    (r_ref, dg_ref, cp_ref, L_ref) = refs[8:12]
-    outs = refs[12 : 16 if send else 14]
-    (gotl_ref, gotr_ref, ownl_ref, ownr_ref, metal_ref, metar_ref, sl_ref, sr_ref) = refs[-8:]
+    (r_ref, dg_ref, cp_ref, L_ref, u0_ref, u3_ref, senda_ref, sendb_ref) = refs[8:]
     total = v_ref.shape[1]
     subs, own, order = L_ref.shape
     wide = CH + TILE
-    pick(core_ref, gota_ref, gotb_ref, gotl_ref, gotr_ref)
-    pick(core_ref, owna_ref, ownb_ref, ownl_ref, ownr_ref)
-    tile_l, tile_r = ownl_ref[:, :TILE], ownr_ref[:, CH - TILE : CH]
-    halo_l, halo_r = gotl_ref[:, :CH], gotr_ref[:, :CH]
-    if not first:
-        pick(core_ref, metaa_ref, metab_ref, metal_ref, metar_ref)
-        lane_t = lane_of(tile_l.shape)
-        lane_h = lane_of(halo_l.shape)
-        mine_l = column(ownl_ref[:, CH : CH + TILE], 0)
-        mine_r = column(ownr_ref[:, CH : CH + TILE], 0)
-        rim_l = column(gotl_ref[:, CH : CH + TILE], 0)
-        rim_r = column(gotr_ref[:, CH : CH + TILE], 0)
-        coup_l = column(metal_ref[:, CH : CH + TILE], 0)
-        coup_r = column(metar_ref[:, CH : CH + TILE], 0)
-        add = lambda x, lane, at, y: (x.astype(F32) + jnp.where(lane == at, y, 0.0)).astype(BF16)
-        tile_l = add(tile_l, lane_t, 0, cp_ref[:, :1] * rim_l)
-        tile_r = add(tile_r, lane_t, TILE - 1, cp_ref[:, total - 1 :] * rim_r)
-        halo_l = add(halo_l, lane_h, CH - 1, coup_l * mine_l)
-        halo_r = add(halo_r, lane_h, 0, coup_r * mine_r)
-    u0 = v_ref[:, :own] + (
-        dot_t(halo_l, L_ref[0, :, :CH]) + dot_t(tile_l, L_ref[0, :, CH:wide])
-    )
-    u3 = v_ref[:, total - own :] + (
-        dot_t(halo_r, L_ref[subs - 1, :, order - CH :])
-        + dot_t(tile_r, L_ref[subs - 1, :, order - wide : order - CH])
-    )
-    outs[0][...] = u0
-    outs[1][...] = u3
-    if send:
-        edge_sends(r_ref, dg_ref, cp_ref, u0, u3, sl_ref, sr_ref)
-        send_pair(core_ref, sl_ref, sr_ref, outs[2], outs[3])
+
+    def run(even):
+        order_of = (lambda a, b: (b, a)) if even else (lambda a, b: (a, b))
+        gotl_ref, gotr_ref = order_of(gota_ref, gotb_ref)
+        ownl_ref, ownr_ref = order_of(owna_ref, ownb_ref)
+        metal_ref, metar_ref = order_of(metaa_ref, metab_ref)
+        tile_l, tile_r = ownl_ref[:, :TILE], ownr_ref[:, CH - TILE : CH]
+        halo_l, halo_r = gotl_ref[:, :CH], gotr_ref[:, :CH]
+        if not first:
+            lane_t = lane_of(tile_l.shape)
+            mine_l = column(ownl_ref[:, CH : CH + TILE], 0)
+            mine_r = column(ownr_ref[:, CH : CH + TILE], 0)
+            rim_l = column(gotl_ref[:, CH : CH + TILE], 0)
+            rim_r = column(gotr_ref[:, CH : CH + TILE], 0)
+            coup_l = column(metal_ref[:, CH : CH + TILE], 0)
+            coup_r = column(metar_ref[:, CH : CH + TILE], 0)
+            add = lambda x, at, y: (
+                x.astype(F32) + jnp.where(lane_t == at, y, 0.0)
+            ).astype(BF16)
+            tile_l = add(tile_l, 0, cp_ref[:, :1] * rim_l)
+            tile_r = add(tile_r, TILE - 1, cp_ref[:, total - 1 :] * rim_r)
+            halo_l = jnp.concatenate(
+                [halo_l[:, : CH - TILE], add(halo_l[:, CH - TILE :], TILE - 1, coup_l * mine_l)],
+                axis=1,
+            )
+            halo_r = jnp.concatenate(
+                [add(halo_r[:, :TILE], 0, coup_r * mine_r), halo_r[:, TILE:]], axis=1
+            )
+        u0_ref[...] = v_ref[:, :own] + dot_t(
+            jnp.concatenate([halo_l, tile_l], axis=1), L_ref[0, :, :wide]
+        )
+        u3_ref[...] = v_ref[:, total - own :] + dot_t(
+            jnp.concatenate([tile_r, halo_r], axis=1), L_ref[subs - 1, :, order - wide :]
+        )
+        edge_sends(r_ref, dg_ref, cp_ref, u0_ref, u3_ref, *order_of(senda_ref, sendb_ref))
+
+    by_side(core_ref, run)
 
 
 def project(core_ref, v_ref, u0_ref, u3_ref, r_ref, dg_ref, cp_ref, basis_ref, metaa_ref, metab_ref,
-            out_ref, metal_ref, metar_ref):
+            unused_a, unused_b, out_ref, s_ref, metal_ref, metar_ref):
     rows, total = r_ref.shape
     own = basis_ref.shape[2]
     modes = basis_ref.shape[1]
     get = parts(v_ref, u0_ref, u3_ref, own)
     lane = lane_of((rows, TILE))
-    pick(core_ref, metaa_ref, metab_ref, metal_ref, metar_ref)
-    sums = []
-    for lo, hi, cur, before, after in chunks_of(get, total):
-        before = 0.0 if before is None else before
-        after = 0.0 if after is None else after
-        s = r_ref[:, lo:hi] - op_chunk(cur, before, after, dg_ref[:, lo:hi], cp_ref[:, lo:hi])
-        j, k = lo // own, lo % own
-        sums.append(dot_t(s.astype(BF16), basis_ref[j, :, k : k + CH]))
-    per = own // CH
-    pieces = []
-    for j in range(total // own):
-        p = sums[j * per]
-        for k in range(1, per):
-            p = p + sums[j * per + k]
-        pieces.append(p)
-    first, last = get(0, 1), get(total - 1, total)
+
+    def meta_of(even):
+        metal_ref[...] = (metab_ref if even else metaa_ref)[:modes, CH : CH + TILE]
+        metar_ref[...] = (metaa_ref if even else metab_ref)[:modes, CH : CH + TILE]
+
+    by_side(core_ref, meta_of)
+    sweep_residual(r_ref, get, (dg_ref, cp_ref), s_ref)
+    pieces = [
+        dot_t(s_ref[:, j * own : (j + 1) * own], basis_ref[j]) for j in range(total // own)
+    ]
+    first, last = u0_ref[:, :1], u3_ref[:, own - 1 :]
     chosen = (lane == 2) | (lane == 3)
     for value, meta in ((first, metal_ref), (last, metar_ref)):
         hi, lo = split(value)
-        coef = meta[:modes, CH : CH + TILE]
+        coef = meta[...]
         pieces.append(
             dot_t(jnp.where(chosen, hi.astype(F32), 0.0).astype(BF16), coef)
             + dot_t(jnp.where(chosen, lo.astype(F32), 0.0).astype(BF16), coef)
@@ -345,12 +401,11 @@
         out_ref[d] = chunk
 
 
-def coarse(send, core_ref, mine_ref, other_ref, W_ref, v_ref, u0_ref, u3_ref, r_ref, dg_ref, cp_ref,
-           basis_ref, x_ref, image_ref, sums_ref, *rest):
+def coarse(core_ref, mine_ref, other_ref, W_ref, v_ref, u0_ref, u3_ref, r_ref, dg_ref, cp_ref,
+           basis_ref, x_ref, image_ref, sums_ref, a_ref, b_ref, both_ref, rims_ref):
     rows, total = r_ref.shape
     own = basis_ref.shape[2]
     modes = basis_ref.shape[1]
-    get = parts(v_ref, u0_ref, u3_ref, own)
     count = mine_ref.shape[0]
     group = min(8, count)
     c = None
@@ -366,35 +421,47 @@
     for j in range(subs):
         hi, lo = split(c[:, j * modes : (j + 1) * modes])
         both = jnp.concatenate([hi, lo], axis=1)
-        for k in range(0, own, CH):
-            b = basis_ref[j, :, k : k + CH]
-            at = j * own + k
-            x_ref[:, at : at + CH] = get(at, at + CH) + jnp.dot(
-                both, jnp.concatenate([b, b], axis=0), preferred_element_type=F32
-            )
+        at = j * own
+        b = basis_ref[j]
+        u = u0_ref[...] if j == 0 else u3_ref[...] if j == subs - 1 else v_ref[:, at : at + own]
+        x_ref[:, at : at + own] = u + jnp.dot(
+            both, jnp.concatenate([b, b], axis=0), preferred_element_type=F32
+        )
     n = subs * modes
     before = other_ref[core_ref[1]]
     after = other_ref[core_ref[2]]
     rim_l = column(before, 98) + c[:, n : n + 1]
     rim_r = column(after, 96) + c[:, n + 1 : n + 2]
-    num = jnp.zeros((rows, 1), F32)
-    den = jnp.zeros((rows, 1), F32)
-    read = lambda lo, hi: x_ref[:, lo:hi]
-    for lo, hi, cur, b, a in chunks_of(read, total):
-        b = rim_l if b is None else b
-        a = rim_r if a is None else a
-        image = op_chunk(cur, b, a, dg_ref[:, lo:hi], cp_ref[:, lo:hi])
-        image_ref[:, lo:hi] = image
-        num = num + jnp.sum(r_ref[:, lo:hi] * image, axis=1, keepdims=True)
-        den = den + jnp.sum(image * image, axis=1, keepdims=True)
-    both = jnp.concatenate([num, den], axis=0)
-    flat = jnp.transpose(jnp.broadcast_to(both, (2 * rows, 2 * rows)))
+    rims_ref[0] = jnp.broadcast_to(rim_l, (rows, TILE))
+    rims_ref[1] = jnp.broadcast_to(rim_r, (rows, TILE))
+
+    def run(group):
+        acc = [jnp.zeros((GROUP, TILE), F32)] * 2
+
+        def emit(t, cur, image):
+            cols = slice(t * TILE, (t + 1) * TILE)
+            image_ref[group, cols] = image
+            acc[0] = acc[0] + r_ref[group, cols] * image
+            acc[1] = acc[1] + image * image
+
+        operator(
+            lambda t: x_ref[group, t * TILE : (t + 1) * TILE], 0, total // TILE, 0,
+            (dg_ref, cp_ref), rims_ref[0, group, :], rims_ref[1, group, :], emit,
+        )
+        for k in range(2):
+            both_ref[k, group, :] = jnp.broadcast_to(
+                jnp.sum(acc[k], axis=1, keepdims=True), (GROUP, TILE)
+            )
+
+    by_rows(rows, run)
+    flat = jnp.transpose(jnp.concatenate([both_ref[0], both_ref[1]], axis=0))
     sums_ref[...] = flat[: sums_ref.shape[0]]
-    if send:
-        a_ref, b_ref, left_ref, right_ref = rest
-        left_ref[...] = image_ref[:, :CH].astype(BF16)
-        right_ref[...] = image_ref[:, total - CH :].astype(BF16)
-        send_pair(core_ref, left_ref, right_ref, a_ref, b_ref)
+
+    def send(even):
+        (b_ref if even else a_ref)[...] = image_ref[:, :CH].astype(BF16)
+        (a_ref if even else b_ref)[...] = image_ref[:, total - CH :].astype(BF16)
+
+    by_side(core_ref, send)
 
 
 def step_of(sums_ref, rows):
@@ -405,44 +472,49 @@
 
 def second(core_ref, sums_ref, x_ref, image_ref, r_ref, ha0_ref, hb0_ref, ha_ref, hb_ref,
            dg_ref, cp_ref, L_ref, sol_ref, res_ref, u_ref, u0_ref, u3_ref, a_ref, b_ref,
-           s_ref, sl_ref, sr_ref, hl0_ref, hr0_ref, hl_ref, hr_ref):
+           s_ref, sl_ref, sr_ref):
     rows, total = r_ref.shape
     own, order = L_ref.shape[1], L_ref.shape[2]
     alpha = step_of(sums_ref, rows)
-    pick(core_ref, ha0_ref, hb0_ref, hl0_ref, hr0_ref)
-    pick(core_ref, ha_ref, hb_ref, hl_ref, hr_ref)
-    s_ref[:, :CH] = (hl0_ref[:, :CH].astype(F32) - alpha * hl_ref[...].astype(F32)).astype(BF16)
-    s_ref[:, CH + total :] = (
-        hr0_ref[:, :CH].astype(F32) - alpha * hr_ref[...].astype(F32)
-    ).astype(BF16)
-    for lo in range(0, total, CH):
-        hi = lo + CH
-        r = r_ref[:, lo:hi] - alpha * image_ref[:, lo:hi]
-        res_ref[:, lo:hi] = r
-        sol_ref[:, lo:hi] = alpha * x_ref[:, lo:hi]
-        s_ref[:, CH + lo : CH + hi] = r.astype(BF16)
+
+    def halo(even):
+        for at, one in ((0, even), (CH + total, not even)):
+            old, new = (hb0_ref, hb_ref) if one else (ha0_ref, ha_ref)
+            s_ref[:, at : at + CH] = (
+                old[:, :CH].astype(F32) - alpha * new[...].astype(F32)
+            ).astype(BF16)
+
+    by_side(core_ref, halo)
+
+    def update(k, carry):
+        cols = pl.ds(pl.multiple_of(k * CH, CH), CH)
+        r = r_ref[:, cols] - alpha * image_ref[:, cols]
+        res_ref[:, cols] = r
+        sol_ref[:, cols] = alpha * x_ref[:, cols]
+        s_ref[:, pl.ds(pl.multiple_of((k + 1) * CH, CH), CH)] = r.astype(BF16)
+        return carry
+
+    lax.fori_loop(0, total // CH, update, 0)
     subs = L_ref.shape[0]
-    part = own // 2
-
-    def step(n, carry):
-        j, k = n // 2, n % 2
-        p = dot_t(
-            s_ref[:, pl.ds(pl.multiple_of(j * own, own), order)],
-            L_ref[j, pl.ds(pl.multiple_of(k * part, part), part), :],
-        )
-        u_ref[:, pl.ds(pl.multiple_of(n * part, part), part)] = p
-        return carry
-
-    lax.fori_loop(0, 2 * subs, step, 0)
-    u0 = u_ref[:, :own]
-    u3 = u_ref[:, total - own :]
-    u0_ref[...] = u0
-    u3_ref[...] = u3
-    edge_sends(res_ref, dg_ref, cp_ref, u0, u3, sl_ref, sr_ref)
-    send_pair(core_ref, sl_ref, sr_ref, a_ref, b_ref)
-
-
-def finish(sums_ref, x_ref, image_ref, r_ref, sol_in_ref, sol_ref, res_ref):
+
+    def step(j, carry):
+        at = pl.multiple_of(j * own, own)
+        u_ref[:, pl.ds(at, own)] = dot_t(s_ref[:, pl.ds(at, order)], L_ref[j])
+        return carry
+
+    lax.fori_loop(0, subs, step, 0)
+    u0_ref[...] = u_ref[:, :own]
+    u3_ref[...] = u_ref[:, total - own :]
+    edge_sends(res_ref, dg_ref, cp_ref, u0_ref, u3_ref, sl_ref, sr_ref)
+
+    def send(even):
+        a_ref[...] = (sr_ref if even else sl_ref)[...]
+        b_ref[...] = (sl_ref if even else sr_ref)[...]
+
+    by_side(core_ref, send)
+
+
+def finish(sums_ref, x_ref, image_ref, r_ref, sol_in_ref, unused_a, unused_b, sol_ref, res_ref):
     rows, total = r_ref.shape
     alpha = step_of(sums_ref, rows)
     for lo in range(0, total, CH):
@@ -513,10 +585,15 @@
         ]
         + pair(long)
         + [pltpu.SemaphoreType.DMA((8,))],
+        EDGE_LIMIT,
         specs=[pl.BlockSpec(memory_space=pltpu.SMEM)] + [hbm] * 4,
     )
     got_a0, got_b0 = exchange(sa, sb)
-    v = call(middle_first, "middle_first", full, [r, L], [s_scratch], 8, work, 0)
+    v, L = call(
+        middle_first, "middle_first", [full, shape(L.shape, L.dtype)], [r, L],
+        [s_scratch, pltpu.SemaphoreType.DMA((subs,))],
+        FIRST_LIMIT, work, specs=[pl.BlockSpec(memory_space=pltpu.VMEM), hbm],
+    )
     weights = []
 
     def sweeps(v, u0, u3, sa, sb, start):
@@ -548,25 +625,25 @@
                     )
                 )
             first = sweep == 0
-            outs = call(
-                functools.partial(edges, first, not last), f"edges_{sweep}",
-                [sub, sub] if last else [sub, sub, send, send],
+            if last and start == 0:
+                vv, weights[1] = lax.optimization_barrier((vv, weights[1]))
+            u0, u3, sa, sb = call(
+                functools.partial(edges, first), "edges_first" if first else "edges",
+                [sub, sub, send, send],
                 [core, vv, ga, gb, sa, sb, got_a0, got_b0, r, dg, cp, L],
-                (pair(long) * 2 if first else pair(send) * 2) + pair(long) + pair(send),
-                8, work // 8,
+                flops=work // 8,
             )
-            v, u0, u3 = vv, outs[0], outs[1]
-            if not last:
-                sa, sb = outs[2], outs[3]
-        return v, u0, u3
+            v = vv
+        return v, u0, u3, sa, sb
 
     edge = shape((rows, CH), BF16)
 
-    def coarse_step(v, u0, u3, sending):
+    def coarse_step(v, u0, u3, sa, sb):
         W = weights[1]
         chunk = call(
             project, "project", shape((sectors // 2, rows, TILE), BF16),
-            [core, v, u0, u3, r, dg, cp, basis, got_a0, got_b0], pair(long),
+            [core, v, u0, u3, r, dg, cp, basis, got_a0, got_b0, sa, sb],
+            [s_scratch] + [pltpu.VMEM((modes, TILE), BF16)] * 2,
         )
         chunk, W = lax.optimization_barrier((chunk, W))
         mine = lax.all_to_all(
@@ -574,25 +651,24 @@
         )
         other = lax.ppermute(mine, "sector", chip)
         return call(
-            functools.partial(coarse, sending), "coarse",
-            [full, full, shape((sectors, 2 * rows), F32)] + ([edge, edge] if sending else []),
+            coarse, "coarse", [full, full, shape((sectors, 2 * rows), F32), edge, edge],
             [core, mine, other, W, v, u0, u3, r, dg, cp, basis],
-            pair(edge) if sending else (),
-        )
-
-    v, u0, u3 = sweeps(v, None, None, sa, sb, 0)
-    x, image, sums, ia, ib = coarse_step(v, u0, u3, True)
+            [pltpu.VMEM((2, rows, TILE), F32)] * 2,
+        )
+
+    v, u0, u3, sa, sb = sweeps(v, None, None, sa, sb, 0)
+    x, image, sums, ia, ib = coarse_step(v, u0, u3, sa, sb)
     halo_a, halo_b = exchange(ia, ib)
     sums = lax.all_to_all(sums, "sector", 0, 0, tiled=True)
     sol, r, v, u0, u3, sa, sb = call(
         second, "second", [full, full, full, sub, sub, send, send],
         [core, sums, x, image, r, got_a0, got_b0, halo_a, halo_b, dg, cp, L],
-        [pltpu.VMEM((rows, total + 2 * CH), BF16)] + pair(send) + pair(long) + pair(edge), 8, work,
+        [pltpu.VMEM((rows, total + 2 * CH), BF16)] + pair(send), 8, work,
     )
-    v, u0, u3 = sweeps(v, u0, u3, sa, sb, 1)
-    x, image, sums = coarse_step(v, u0, u3, False)
+    v, u0, u3, sa, sb = sweeps(v, u0, u3, sa, sb, 1)
+    x, image, sums, ia, ib = coarse_step(v, u0, u3, sa, sb)
     sums = lax.all_to_all(sums, "sector", 0, 0, tiled=True)
-    sol, res = call(finish, "finish", [full, full], [sums, x, image, r, sol], smem=0)
+    sol, res = call(finish, "finish", [full, full], [sums, x, image, r, sol, ia, ib], smem=0)
     return sol, res
 
 

time: 196 us -> 190 us (0.969)
  local copies, waits for them, and re-layouts: 9.71 us -> 1.26 us
    unnamed x28 -> x16, local copies, waits for them, and re-layouts: 9.71 us -> 1.26 us
where the time goes in v1:
time: 190 us
  Pallas kernels  79.2 us (42%)
  blocking collectives  74.6 us (39%)
  starting transfers between devices  29.5 us (16%)
  waiting for transfers between devices  3.86 us (2%)
    pallas_call x23, Pallas kernels, call(): pl.pallas_call(kernel, out_shape=outs, in_specs=specs or [pl.BlockSpec(me...  79.2 us
    all_to_all x2, blocking collectives, coarse_step(): lax.all_to_all(chunk, 'sector', 0, 0, axis_index_groups=planes, tiled=True)  43.5 us
    all_to_all x2, blocking collectives, body(): sums = lax.all_to_all(sums, 'sector', 0, 0, tiled=True)  31.2 us
    ppermute x8, starting transfers between devices, exchange(): got_a = lax.ppermute(a, 'sector', chip)  24.5 us
    ppermute x8, starting transfers between devices, exchange(): got_b = lax.ppermute(b, 'sector', side)  4.62 us
    ppermute x2, waiting for transfers between devices, coarse_step(): other = lax.ppermute(mine, 'sector', chip)  3.81 us
  transfers between devices with their start and end apart: 19, of which 2 were waited for; matrix products, arithmetic and copies ran while one was open for 0% of the time, Pallas kernels for 25%

profile of v1, /device:TPU:1, one launch (start us, length us, event | category | flops | bytes accessed | tf_op | source)
XLA Modules:
  0.0 190.1 jit_solution(13359139508796860124)
XLA Ops:
  0.6 0.0 copy-start.1
  0.7 0.6 pad_add_fusion.core_ref.refs_0_
  1.4 2.9 %first_edges.1 = (bf16[64,768]{1,0:T(8,128)(2,1)}, bf16[64,768]{1,0:T(8,128)(2,1)}) custom-call(s32[4]{0:T(128)} %pad_add_fusion.core_ref.refs_0_, f32[64,4096]{1,0:T(8,128)} %r_ref.13, f32[1,4096]{1,0:T(1,128)} %bitcast.14, bf16[4,16,1024]{2,1,0:T(8,128)(2,1)} %basis_ref.7, f32[64,2048]{1,0:T(8,128)} %ci_ref), custom_call_target="tpu_custom_call" | custom-call | bytes 1720336 | tf_op jit(solution)/shard_map/first_edges/pallas_call | solution.py:529
  4.2 1.5 collective-permute-start
  5.7 2.8 %collective-permute-start.1 = (bf16[64,768]{1,0:T(8,128)(2,1)}, bf16[64,768]{1,0:T(8,128)(2,1)S(1)}, u32[]{:S(2)}, u32[]{:S(2)}) collective-permute-start(bf16[64,768]{1,0:T(8,128)(2,1)} %get-tuple-element.61.refs_5_), channel_id=1, source_target_pairs={{0,126},{2,4},{4,2},{6,8},{8,6},{10,12},{12,10},{14,16},{16,14},{1... | collective-permute-start | bytes 294920 | tf_op jit(solution)/shard_map/ppermute | solution.py:573
  8.5 1.2 copy-done
  9.8 7.7 %middle_first.1 = (f32[64,4096]{1,0:T(8,128)S(1)}, bf16[4,1024,2048]{2,1,0:T(8,128)(2,1)S(1)}) custom-call(f32[64,4096]{1,0:T(8,128)S(1)} %copy-done, bf16[4,1024,2048]{2,1,0:T(8,128)(2,1)} %L_hbm.1), custom_call_target="tpu_custom_call" | custom-call | flops 1073741824 | bytes 17825792 | tf_op jit(solution)/shard_map/middle_first/pallas_call | solution.py:529
  17.5 0.0 collective-permute-done.refs_2_.refs_6_.a_ref.metaa_ref.ha0_ref
  17.5 0.0 collective-permute-done.1.refs_3_.refs_7_.b_ref.metab_ref.hb0_ref
  17.5 0.0 copy-start.4
  17.5 2.0 %edges_first.1 = (f32[64,1024]{1,0:T(8,128)S(1)}, f32[64,1024]{1,0:T(8,128)S(1)}, bf16[64,640]{1,0:T(8,128)(2,1)S(1)}, bf16[64,640]{1,0:T(8,128)(2,1)S(1)}) custom-call(s32[4]{0:T(128)S(1)} %copy-done.5, f32[64,4096]{1,0:T(8,128)S(1)} %get-tuple-element.59.refs_1_.v_ref, bf16[64,768]{1,0:T(8,128)(2,1)S(1)} %collective-permute-done.refs_2_.refs_6_.a_ref.metaa_ref.ha0_ref, ...), custom_call_target="tpu_custom_call" | custom-call | flops 134217728 | bytes 19496976 | tf_op jit(solution)/shard_map/edges_first/pallas_call | solution.py:529
  19.6 6.4 %collective-permute-start.2 = (bf16[64,640]{1,0:T(8,128)(2,1)S(1)}, bf16[64,640]{1,0:T(8,128)(2,1)S(1)}, u32[]{:S(2)}, u32[]{:S(2)}) collective-permute-start(bf16[64,640]{1,0:T(8,128)(2,1)S(1)} %get-tuple-element.65.refs_4_), channel_id=1, source_target_pairs={{0,2},{2,0},{4,6},{6,4},{8,10},{10,8},{12,14},{14,12},{16,18},{18,... | collective-permute-start | bytes 245768 | tf_op jit(solution)/shard_map/ppermute | solution.py:574
  26.0 0.0 collective-permute-start.3
  26.0 5.5 %middle.6.refs_1_.v_ref = f32[64,4096]{1,0:T(8,128)S(1)} custom-call(f32[64,4096]{1,0:T(8,128)S(1)} %copy-done, f32[64,4096]{1,0:T(8,128)S(1)} %get-tuple-element.59.refs_1_.v_ref, f32[64,1024]{1,0:T(8,128)S(1)} %get-tuple-element.63.u0_ref, f32[64,1024]{1,0:T(8,128)S(1)} %get-tuple-element.64.u3_ref, f32[1,4096]{1,0:T(1,128)S(1)} %bitcast.34, ...), custom_call_target="tpu_custom_call" | custom-call | flops 1073741824 | bytes 19431424 | tf_op jit(solution)/shard_map/middle/pallas_call | solution.py:529
  31.5 0.6 lines.1.mine_ref
  32.1 0.4 collective-permute-start.6
  32.5 0.0 collective-permute-done.2.refs_2_
  32.5 0.0 collective-permute-done.3.refs_3_
  32.5 2.0 %edges.6 = (f32[64,1024]{1,0:T(8,128)S(1)}, f32[64,1024]{1,0:T(8,128)S(1)}, bf16[64,640]{1,0:T(8,128)(2,1)S(1)}, bf16[64,640]{1,0:T(8,128)(2,1)S(1)}) custom-call(s32[4]{0:T(128)S(1)} %copy-done.5, f32[64,4096]{1,0:T(8,128)S(1)} %middle.6.refs_1_.v_ref, bf16[64,640]{1,0:T(8,128)(2,1)S(1)} %collective-permute-done.2.refs_2_, ...), custom_call_target="tpu_custom_call" | custom-call | flops 134217728 | bytes 19431440 | tf_op jit(solution)/shard_map/edges/pallas_call | solution.py:529
  34.6 3.2 %collective-permute-start.4 = (bf16[64,640]{1,0:T(8,128)(2,1)S(1)}, bf16[64,640]{1,0:T(8,128)(2,1)S(1)}, u32[]{:S(2)}, u32[]{:S(2)}) collective-permute-start(bf16[64,640]{1,0:T(8,128)(2,1)S(1)} %get-tuple-element.69.refs_4_), channel_id=1, source_target_pairs={{0,2},{2,0},{4,6},{6,4},{8,10},{10,8},{12,14},{14,12},{16,18},{18,... | collective-permute-start | bytes 245768 | tf_op jit(solution)/shard_map/ppermute | solution.py:574
  37.8 1.1 collective-permute-start.5
  38.9 5.5 %middle.7.refs_1_.v_ref = f32[64,4096]{1,0:T(8,128)S(1)} custom-call(f32[64,4096]{1,0:T(8,128)S(1)} %copy-done, f32[64,4096]{1,0:T(8,128)S(1)} %middle.6.refs_1_.v_ref, f32[64,1024]{1,0:T(8,128)S(1)} %get-tuple-element.67.u0_ref, f32[64,1024]{1,0:T(8,128)S(1)} %get-tuple-element.68.u3_ref, f32[1,4096]{1,0:T(1,128)S(1)} %bitcast.36, f32[1,4096]{1,0:T(1,128)S(1)} %bitcast.18, ...), custom_call_target="tpu_custom_call" | custom-call | flops 1073741824 | bytes 19431424 | tf_op jit(solution)/shard_map/middle/pallas_call | solution.py:529
  44.4 0.0 collective-permute-done.4.refs_2_
  44.4 0.0 collective-permute-done.5.refs_3_
  44.4 2.0 %edges.7 = (f32[64,1024]{1,0:T(8,128)S(1)}, f32[64,1024]{1,0:T(8,128)S(1)}, bf16[64,640]{1,0:T(8,128)(2,1)S(1)}, bf16[64,640]{1,0:T(8,128)(2,1)S(1)}) custom-call(s32[4]{0:T(128)S(1)} %copy-done.5, f32[64,4096]{1,0:T(8,128)S(1)} %middle.7.refs_1_.v_ref, bf16[64,640]{1,0:T(8,128)(2,1)S(1)} %collective-permute-done.4.refs_2_, ...), custom_call_target="tpu_custom_call" | custom-call | flops 134217728 | bytes 19431440 | tf_op jit(solution)/shard_map/edges/pallas_call | solution.py:529
  46.5 4.1 %collective-permute-start.7 = (bf16[64,640]{1,0:T(8,128)(2,1)S(1)}, bf16[64,640]{1,0:T(8,128)(2,1)S(1)}, u32[]{:S(2)}, u32[]{:S(2)}) collective-permute-start(bf16[64,640]{1,0:T(8,128)(2,1)S(1)} %get-tuple-element.76.refs_4_), channel_id=1, source_target_pairs={{0,2},{2,0},{4,6},{6,4},{8,10},{10,8},{12,14},{14,12},{16,18},{18,... | collective-permute-start | bytes 245768 | tf_op jit(solution)/shard_map/ppermute | solution.py:574
  50.6 0.0 collective-permute-start.8
  50.6 5.5 %middle.8.refs_1_.v_ref = f32[64,4096]{1,0:T(8,128)S(1)} custom-call(f32[64,4096]{1,0:T(8,128)S(1)} %copy-done, f32[64,4096]{1,0:T(8,128)S(1)} %middle.7.refs_1_.v_ref, f32[64,1024]{1,0:T(8,128)S(1)} %get-tuple-element.71.u0_ref, f32[64,1024]{1,0:T(8,128)S(1)} %get-tuple-element.72.u3_ref, f32[1,4096]{1,0:T(1,128)S(1)} %bitcast.38, f32[1,4096]{1,0:T(1,128)S(1)} %bitcast.20, ...), custom_call_target="tpu_custom_call" | custom-call | flops 1073741824 | bytes 19431424 | tf_op jit(solution)/shard_map/middle/pallas_call | solution.py:529
  56.1 0.0 collective-permute-done.6.other_ref
  56.1 1.8 weave.1.W_ref
  57.9 0.0 collective-permute-done.7.refs_2_
  57.9 0.0 collective-permute-done.8.refs_3_
  58.0 2.0 %edges.8 = (f32[64,1024]{1,0:T(8,128)S(1)}, f32[64,1024]{1,0:T(8,128)S(1)}, bf16[64,640]{1,0:T(8,128)(2,1)S(1)}, bf16[64,640]{1,0:T(8,128)(2,1)S(1)}) custom-call(s32[4]{0:T(128)S(1)} %copy-done.5, f32[64,4096]{1,0:T(8,128)S(1)} %middle.8.refs_1_.v_ref, bf16[64,640]{1,0:T(8,128)(2,1)S(1)} %collective-permute-done.7.refs_2_, ...), custom_call_target="tpu_custom_call" | custom-call | flops 134217728 | bytes 19431440 | tf_op jit(solution)/shard_map/edges/pallas_call | solution.py:529
  60.0 1.8 project.2
  61.8 21.8 %all_to_all.32.mine_ref = bf16[32,64,128]{2,1,0:T(8,128)(2,1)S(1)} all-to-all(bf16[32,64,128]{2,1,0:T(8,128)(2,1)S(1)} %project.2), channel_id=1, replica_groups={{0,4,8,12,16,20,24,28,32,36,40,44,48,52,56,60,64,68,72,76,80,84,88,92,9..., dimensions={0} | all-to-all | bytes 1048576 | tf_op jit(solution)/shard_map/all_to_all | solution.py:649
  83.6 0.0 collective-permute-start.9
  83.6 1.9 %collective-permute-done.9.other_ref = bf16[32,64,128]{2,1,0:T(8,128)(2,1)S(1)} collective-permute-done((bf16[32,64,128]{2,1,0:T(8,128)(2,1)S(1)}, bf16[32,64,128]{2,1,0:T(8,128)(2,1)S(1)}, u32[]{:S(2)}, u32[]{:S(2)}) %collective-permute-start.9) | collective-permute-done | bytes 524320 | tf_op jit(solution)/shard_map/ppermute | solution.py:652
  85.6 2.9 %coarse.2 = (f32[64,4096]{1,0:T(8,128)S(1)}, f32[64,4096]{1,0:T(8,128)S(1)}, f32[64,128]{1,0:T(8,128)S(1)}, bf16[64,512]{1,0:T(8,128)(2,1)S(1)}, bf16[64,512]{1,0:T(8,128)(2,1)S(1)}) custom-call(s32[4]{0:T(128)S(1)} %copy-done.5, bf16[32,64,128]{2,1,0:T(8,128)(2,1)S(1)} %all_to_all.32.mine_ref, bf16[32,64,128]{2,1,0:T(8,128)(2,1)S(1)} %collective-permute-done.9.other_ref, ...), custom_call_target="tpu_custom_call" | custom-call | bytes 5013520 | tf_op jit(solution)/shard_map/coarse/pallas_call | solution.py:529
  88.5 0.2 collective-permute-start.10
  88.7 0.5 collective-permute-start.11
  89.1 18.3 %all_to_all.33 = f32[64,1,128]{2,1,0:T(1,128)S(1)} all-to-all(f32[64,1,128]{2,1,0:T(1,128)S(1)} %bitcast.53), channel_id=1, replica_groups=mesh['sector'=64,'lift'=2] {'sector'}, dimensions={0} | all-to-all | bytes 65536 | tf_op jit(solution)/shard_map/all_to_all | solution.py:662
  107.4 7.7 %second.1 = (f32[64,4096]{1,0:T(8,128)S(1)}, f32[64,4096]{1,0:T(8,128)S(1)}, f32[64,4096]{1,0:T(8,128)S(1)}, f32[64,1024]{1,0:T(8,128)S(1)}, f32[64,1024]{1,0:T(...) custom-call(s32[4]{0:T(128)S(1)} %copy-done.5, f32[64,128]{1,0:T(8,128)S(1)} %bitcast.51, ...), custom_call_target="tpu_custom_call" | custom-call | flops 1073741824 | bytes 20316176 | tf_op jit(solution)/shard_map/second/pallas_call | solution.py:529
  115.1 0.8 collective-permute-start.12
  115.9 0.2 collective-permute-start.13
  116.2 5.5 %middle.9.refs_1_.v_ref = f32[64,4096]{1,0:T(8,128)S(1)} custom-call(f32[64,4096]{1,0:T(8,128)S(1)} %get-tuple-element.90.r_ref.refs_8_, f32[64,4096]{1,0:T(8,128)S(1)} %get-tuple-element.91.v_ref, f32[64,1024]{1,0:T(8,128)S(1)} %get-tuple-element.92.u0_ref, f32[64,1024]{1,0:T(8,128)S(1)} %get-tuple-element.93.u3_ref, f32[1,4096]{1,0:T(1,128)S(1)} %bitcast.43, ...), custom_call_target="tpu_custom_call" | custom-call | flops 1073741824 | bytes 19431424 | tf_op jit(solution)/shard_map/middle/pallas_call | solution.py:529
  121.7 0.0 collective-permute-done.12.refs_2_
  121.7 0.0 collective-permute-done.13.refs_3_
  121.7 2.2 %edges.9 = (f32[64,1024]{1,0:T(8,128)S(1)}, f32[64,1024]{1,0:T(8,128)S(1)}, bf16[64,640]{1,0:T(8,128)(2,1)S(1)}, bf16[64,640]{1,0:T(8,128)(2,1)S(1)}) custom-call(s32[4]{0:T(128)S(1)} %copy-done.5, f32[64,4096]{1,0:T(8,128)S(1)} %middle.9.refs_1_.v_ref, bf16[64,640]{1,0:T(8,128)(2,1)S(1)} %collective-permute-done.12.refs_2_, ...), custom_call_target="tpu_custom_call" | custom-call | flops 134217728 | bytes 19431440 | tf_op jit(solution)/shard_map/edges/pallas_call | solution.py:529
  123.9 4.0 %collective-permute-start.14 = (bf16[64,640]{1,0:T(8,128)(2,1)S(1)}, bf16[64,640]{1,0:T(8,128)(2,1)S(1)}, u32[]{:S(2)}, u32[]{:S(2)}) collective-permute-start(bf16[64,640]{1,0:T(8,128)(2,1)S(1)} %get-tuple-element.98.refs_4_), channel_id=1, source_target_pairs={{0,2},{2,0},{4,6},{6,4},{8,10},{10,8},{12,14},{14,12},{16,18},{18,... | collective-permute-start | bytes 245768 | tf_op jit(solution)/shard_map/ppermute | solution.py:574
  127.9 0.0 collective-permute-start.15
  127.9 5.5 %middle.10.refs_1_.v_ref = f32[64,4096]{1,0:T(8,128)S(1)} custom-call(f32[64,4096]{1,0:T(8,128)S(1)} %get-tuple-element.90.r_ref.refs_8_, f32[64,4096]{1,0:T(8,128)S(1)} %middle.9.refs_1_.v_ref, f32[64,1024]{1,0:T(8,128)S(1)} %get-tuple-element.96.u0_ref, f32[64,1024]{1,0:T(8,128)S(1)} %get-tuple-element.97.u3_ref, f32[1,4096]{1,0:T(1,128)S(1)} %bitcast.45, ...), custom_call_target="tpu_custom_call" | custom-call | flops 1073741824 | bytes 19431424 | tf_op jit(solution)/shard_map/middle/pallas_call | solution.py:529
  133.4 0.0 collective-permute-done.15.refs_3_
  133.5 2.0 %edges.10 = (f32[64,1024]{1,0:T(8,128)S(1)}, f32[64,1024]{1,0:T(8,128)S(1)}, bf16[64,640]{1,0:T(8,128)(2,1)S(1)}, bf16[64,640]{1,0:T(8,128)(2,1)S(1)}) custom-call(s32[4]{0:T(128)S(1)} %copy-done.5, f32[64,4096]{1,0:T(8,128)S(1)} %middle.10.refs_1_.v_ref, bf16[64,640]{1,0:T(8,128)(2,1)S(1)} %collective-permute-done.14.refs_2_, ...), custom_call_target="tpu_custom_call" | custom-call | flops 134217728 | bytes 19431440 | tf_op jit(solution)/shard_map/edges/pallas_call | solution.py:529
  135.5 4.2 %collective-permute-start.16 = (bf16[64,640]{1,0:T(8,128)(2,1)S(1)}, bf16[64,640]{1,0:T(8,128)(2,1)S(1)}, u32[]{:S(2)}, u32[]{:S(2)}) collective-permute-start(bf16[64,640]{1,0:T(8,128)(2,1)S(1)} %get-tuple-element.102.refs_4_), channel_id=1, source_target_pairs={{0,2},{2,0},{4,6},{6,4},{8,10},{10,8},{12,14},{14,12},{16,18},{18,... | collective-permute-start | bytes 245768 | tf_op jit(solution)/shard_map/ppermute | solution.py:574
  139.7 0.0 collective-permute-start.17
  139.7 5.5 %middle.11.refs_1_.v_ref = f32[64,4096]{1,0:T(8,128)S(1)} custom-call(f32[64,4096]{1,0:T(8,128)S(1)} %get-tuple-element.90.r_ref.refs_8_, f32[64,4096]{1,0:T(8,128)S(1)} %middle.10.refs_1_.v_ref, f32[64,1024]{1,0:T(8,128)S(1)} %get-tuple-element.100.u0_ref, f32[64,1024]{1,0:T(8,128)S(1)} %get-tuple-element.101.u3_ref, f32[1,4096]{1,0:T(1,128)S(1)} %bitcast.47, ...), custom_call_target="tpu_custom_call" | custom-call | flops 1073741824 | bytes 19431424 | tf_op jit(solution)/shard_map/middle/pallas_call | solution.py:529
  145.3 2.0 %edges.11 = (f32[64,1024]{1,0:T(8,128)S(1)}, f32[64,1024]{1,0:T(8,128)S(1)}, bf16[64,640]{1,0:T(8,128)(2,1)S(1)}, bf16[64,640]{1,0:T(8,128)(2,1)S(1)}) custom-call(s32[4]{0:T(128)S(1)} %copy-done.5, f32[64,4096]{1,0:T(8,128)S(1)} %middle.11.refs_1_.v_ref, bf16[64,640]{1,0:T(8,128)(2,1)S(1)} %collective-permute-done.16.refs_2_, ...), custom_call_target="tpu_custom_call" | custom-call | flops 134217728 | bytes 19431440 | tf_op jit(solution)/shard_map/edges/pallas_call | solution.py:529
  147.3 1.8 project.3
  149.1 21.6 %all_to_all.34.mine_ref = bf16[32,64,128]{2,1,0:T(8,128)(2,1)S(1)} all-to-all(bf16[32,64,128]{2,1,0:T(8,128)(2,1)S(1)} %project.3), channel_id=1, replica_groups={{0,4,8,12,16,20,24,28,32,36,40,44,48,52,56,60,64,68,72,76,80,84,88,92,9..., dimensions={0} | all-to-all | bytes 1048576 | tf_op jit(solution)/shard_map/all_to_all | solution.py:649
  170.8 0.0 collective-permute-start.18
  170.8 1.9 %collective-permute-done.18.other_ref = bf16[32,64,128]{2,1,0:T(8,128)(2,1)S(1)} collective-permute-done((bf16[32,64,128]{2,1,0:T(8,128)(2,1)S(1)}, bf16[32,64,128]{2,1,0:T(8,128)(2,1)S(1)}, u32[]{:S(2)}, u32[]{:S(2)}) %collective-permute-start.18) | collective-permute-done | bytes 524320 | tf_op jit(solution)/shard_map/ppermute | solution.py:652
  172.7 2.9 %coarse.3 = (f32[64,4096]{1,0:T(8,128)S(1)}, f32[64,4096]{1,0:T(8,128)S(1)}, f32[64,128]{1,0:T(8,128)S(1)}, bf16[64,512]{1,0:T(8,128)(2,1)S(1)}, bf16[64,512]{1,0:T(8,128)(2,1)S(1)}) custom-call(s32[4]{0:T(128)S(1)} %copy-done.5, bf16[32,64,128]{2,1,0:T(8,128)(2,1)S(1)} %all_to_all.34.mine_ref, bf16[32,64,128]{2,1,0:T(8,128)(2,1)S(1)} %collective-permute-done.18.other_ref, ...), custom_call_target="tpu_custom_call" | custom-call | bytes 5013520 | tf_op jit(solution)/shard_map/coarse/pallas_call | solution.py:529
  175.6 12.9 %all_to_all.35 = f32[64,1,128]{2,1,0:T(1,128)S(1)} all-to-all(f32[64,1,128]{2,1,0:T(1,128)S(1)} %bitcast.54), channel_id=1, replica_groups=mesh['sector'=64,'lift'=2] {'sector'}, dimensions={0} | all-to-all | bytes 65536 | tf_op jit(solution)/shard_map/all_to_all | solution.py:670
  188.5 1.7 finish.1
  (18 shorter events, 0.0 us)
Async XLA Ops:
  0.6 16.9 %copy-start.1 = (f32[4096]{0:T(1024)S(1)}, f32[4096]{0:T(1024)}, u32[]{:S(2)}) copy-start(f32[4096]{0:T(1024)} %param.8) | copy-start | bytes 49156
  0.6 16.9 %copy-start.2 = (f32[4096]{0:T(1024)S(1)}, f32[4096]{0:T(1024)}, u32[]{:S(2)}) copy-start(f32[4096]{0:T(1024)} %param.7) | copy-start | bytes 49156
  1.4 16.1 %copy-start.5 = (s32[4]{0:T(128)S(1)}, s32[4]{0:T(128)}, u32[]{:S(2)}) copy-start(s32[4]{0:T(128)} %pad_add_fusion.core_ref.refs_0_) | copy-start | bytes 52
  4.2 13.2 %collective-permute-start = (bf16[64,768]{1,0:T(8,128)(2,1)}, bf16[64,768]{1,0:T(8,128)(2,1)S(1)}, u32[]{:S(2)}, u32[]{:S(2)}) collective-permute-start(bf16[64,768]{1,0:T(8,128)(2,1)} %get-tuple-element.60.refs_4_), channel_id=1, source_target_pairs={{0,2},{2,0},{4,6},{6,4},{8,10},{10,8},{12,14},{14,12},{16,18},{18,... | collective-permute-start | bytes 294920 | tf_op jit(solution)/shard_map/ppermute | solution.py:574
  5.7 11.8 %collective-permute-start.1 = (bf16[64,768]{1,0:T(8,128)(2,1)}, bf16[64,768]{1,0:T(8,128)(2,1)S(1)}, u32[]{:S(2)}, u32[]{:S(2)}) collective-permute-start(bf16[64,768]{1,0:T(8,128)(2,1)} %get-tuple-element.61.refs_5_), channel_id=1, source_target_pairs={{0,126},{2,4},{4,2},{6,8},{8,6},{10,12},{12,10},{14,16},{16,14},{1... | collective-permute-start | bytes 294920 | tf_op jit(solution)/shard_map/ppermute | solution.py:573
  8.5 1.2 copy-start
  9.8 7.8 %copy-start.6 = (bf16[64,768]{1,0:T(8,128)(2,1)S(1)}, bf16[64,768]{1,0:T(8,128)(2,1)}, u32[]{:S(2)}) copy-start(bf16[64,768]{1,0:T(8,128)(2,1)} %get-tuple-element.60.refs_4_) | copy-start | bytes 294916
  9.8 7.8 %copy-start.7 = (bf16[64,768]{1,0:T(8,128)(2,1)S(1)}, bf16[64,768]{1,0:T(8,128)(2,1)}, u32[]{:S(2)}) copy-start(bf16[64,768]{1,0:T(8,128)(2,1)} %get-tuple-element.61.refs_5_) | copy-start | bytes 294916
  17.5 14.0 %copy-start.4 = (f32[64,2048]{1,0:T(8,128)S(1)}, f32[64,2048]{1,0:T(8,128)}, u32[]{:S(2)}) copy-start(f32[64,2048]{1,0:T(8,128)} %ci_ref) | copy-start | bytes 1572868
  19.6 13.0 %collective-permute-start.2 = (bf16[64,640]{1,0:T(8,128)(2,1)S(1)}, bf16[64,640]{1,0:T(8,128)(2,1)S(1)}, u32[]{:S(2)}, u32[]{:S(2)}) collective-permute-start(bf16[64,640]{1,0:T(8,128)(2,1)S(1)} %get-tuple-element.65.refs_4_), channel_id=1, source_target_pairs={{0,2},{2,0},{4,6},{6,4},{8,10},{10,8},{12,14},{14,12},{16,18},{18,... | collective-permute-start | bytes 245768 | tf_op jit(solution)/shard_map/ppermute | solution.py:574
  26.0 6.5 %collective-permute-start.3 = (bf16[64,640]{1,0:T(8,128)(2,1)S(1)}, bf16[64,640]{1,0:T(8,128)(2,1)S(1)}, u32[]{:S(2)}, u32[]{:S(2)}) collective-permute-start(bf16[64,640]{1,0:T(8,128)(2,1)S(1)} %get-tuple-element.66.refs_5_), channel_id=1, source_target_pairs={{0,126},{2,4},{4,2},{6,8},{8,6},{10,12},{12,10},{14,16},{16,14},{1... | collective-permute-start | bytes 245768 | tf_op jit(solution)/shard_map/ppermute | solution.py:573
  32.1 24.0 %collective-permute-start.6 = (bf16[72,2048]{1,0:T(8,128)(2,1)S(1)}, bf16[72,2048]{1,0:T(8,128)(2,1)S(1)}, u32[]{:S(2)}, u32[]{:S(2)}) collective-permute-start(bf16[72,2048]{1,0:T(8,128)(2,1)S(1)} %lines.1.mine_ref), channel_id=1, source_target_pairs={{0,1},{1,0},{2,3},{3,2},{4,5},{5,4},{6,7},{7,6},{8,9},{9,8},{10,11... | collective-permute-start | bytes 884744 | tf_op jit(solution)/shard_map/ppermute | solution.py:615
  34.6 9.8 %collective-permute-start.4 = (bf16[64,640]{1,0:T(8,128)(2,1)S(1)}, bf16[64,640]{1,0:T(8,128)(2,1)S(1)}, u32[]{:S(2)}, u32[]{:S(2)}) collective-permute-start(bf16[64,640]{1,0:T(8,128)(2,1)S(1)} %get-tuple-element.69.refs_4_), channel_id=1, source_target_pairs={{0,2},{2,0},{4,6},{6,4},{8,10},{10,8},{12,14},{14,12},{16,18},{18,... | collective-permute-start | bytes 245768 | tf_op jit(solution)/shard_map/ppermute | solution.py:574
  37.8 6.6 %collective-permute-start.5 = (bf16[64,640]{1,0:T(8,128)(2,1)S(1)}, bf16[64,640]{1,0:T(8,128)(2,1)S(1)}, u32[]{:S(2)}, u32[]{:S(2)}) collective-permute-start(bf16[64,640]{1,0:T(8,128)(2,1)S(1)} %get-tuple-element.70.refs_5_), channel_id=1, source_target_pairs={{0,126},{2,4},{4,2},{6,8},{8,6},{10,12},{12,10},{14,16},{16,14},{1... | collective-permute-start | bytes 245768 | tf_op jit(solution)/shard_map/ppermute | solution.py:573
  46.5 11.5 %collective-permute-start.7 = (bf16[64,640]{1,0:T(8,128)(2,1)S(1)}, bf16[64,640]{1,0:T(8,128)(2,1)S(1)}, u32[]{:S(2)}, u32[]{:S(2)}) collective-permute-start(bf16[64,640]{1,0:T(8,128)(2,1)S(1)} %get-tuple-element.76.refs_4_), channel_id=1, source_target_pairs={{0,2},{2,0},{4,6},{6,4},{8,10},{10,8},{12,14},{14,12},{16,18},{18,... | collective-permute-start | bytes 245768 | tf_op jit(solution)/shard_map/ppermute | solution.py:574
  50.6 7.4 %collective-permute-start.8 = (bf16[64,640]{1,0:T(8,128)(2,1)S(1)}, bf16[64,640]{1,0:T(8,128)(2,1)S(1)}, u32[]{:S(2)}, u32[]{:S(2)}) collective-permute-start(bf16[64,640]{1,0:T(8,128)(2,1)S(1)} %get-tuple-element.77.refs_5_), channel_id=1, source_target_pairs={{0,126},{2,4},{4,2},{6,8},{8,6},{10,12},{12,10},{14,16},{16,14},{1... | collective-permute-start | bytes 245768 | tf_op jit(solution)/shard_map/ppermute | solution.py:573
  50.6 9.4 %copy-start.3 = (bf16[4,16,1024]{2,1,0:T(8,128)(2,1)S(1)}, bf16[4,16,1024]{2,1,0:T(8,128)(2,1)}, u32[]{:S(2)}) copy-start(bf16[4,16,1024]{2,1,0:T(8,128)(2,1)} %basis_ref.7) | copy-start | bytes 393220
  83.6 1.9 %collective-permute-start.9 = (bf16[32,64,128]{2,1,0:T(8,128)(2,1)S(1)}, bf16[32,64,128]{2,1,0:T(8,128)(2,1)S(1)}, u32[]{:S(2)}, u32[]{:S(2)}) collective-permute-start(bf16[32,64,128]{2,1,0:T(8,128)(2,1)S(1)} %all_to_all.32.mine_ref), channel_id=1, source_target_pairs={{0,2},{2,0},{4,6},{6,4},{8,10},{10,8},{12,14},{14,12},{16,18},{18,... | collective-permute-start | bytes 1572872 | tf_op jit(solution)/shard_map/ppermute | solution.py:652
  88.5 19.0 %collective-permute-start.10 = (bf16[64,512]{1,0:T(8,128)(2,1)S(1)}, bf16[64,512]{1,0:T(8,128)(2,1)S(1)}, u32[]{:S(2)}, u32[]{:S(2)}) collective-permute-start(bf16[64,512]{1,0:T(8,128)(2,1)S(1)} %get-tuple-element.88), channel_id=1, source_target_pairs={{0,2},{2,0},{4,6},{6,4},{8,10},{10,8},{12,14},{14,12},{16,18},{18,... | collective-permute-start | bytes 196616 | tf_op jit(solution)/shard_map/ppermute | solution.py:574
  88.7 18.8 %collective-permute-start.11 = (bf16[64,512]{1,0:T(8,128)(2,1)S(1)}, bf16[64,512]{1,0:T(8,128)(2,1)S(1)}, u32[]{:S(2)}, u32[]{:S(2)}) collective-permute-start(bf16[64,512]{1,0:T(8,128)(2,1)S(1)} %get-tuple-element.89), channel_id=1, source_target_pairs={{0,126},{2,4},{4,2},{6,8},{8,6},{10,12},{12,10},{14,16},{16,14},{1... | collective-permute-start | bytes 196616 | tf_op jit(solution)/shard_map/ppermute | solution.py:573
  115.1 6.6 %collective-permute-start.12 = (bf16[64,640]{1,0:T(8,128)(2,1)S(1)}, bf16[64,640]{1,0:T(8,128)(2,1)S(1)}, u32[]{:S(2)}, u32[]{:S(2)}) collective-permute-start(bf16[64,640]{1,0:T(8,128)(2,1)S(1)} %get-tuple-element.94.refs_4_), channel_id=1, source_target_pairs={{0,2},{2,0},{4,6},{6,4},{8,10},{10,8},{12,14},{14,12},{16,18},{18,... | collective-permute-start | bytes 245768 | tf_op jit(solution)/shard_map/ppermute | solution.py:574
  115.9 5.7 %collective-permute-start.13 = (bf16[64,640]{1,0:T(8,128)(2,1)S(1)}, bf16[64,640]{1,0:T(8,128)(2,1)S(1)}, u32[]{:S(2)}, u32[]{:S(2)}) collective-permute-start(bf16[64,640]{1,0:T(8,128)(2,1)S(1)} %get-tuple-element.95.refs_5_), channel_id=1, source_target_pairs={{0,126},{2,4},{4,2},{6,8},{8,6},{10,12},{12,10},{14,16},{16,14},{1... | collective-permute-start | bytes 245768 | tf_op jit(solution)/shard_map/ppermute | solution.py:573
  123.9 9.5 %collective-permute-start.14 = (bf16[64,640]{1,0:T(8,128)(2,1)S(1)}, bf16[64,640]{1,0:T(8,128)(2,1)S(1)}, u32[]{:S(2)}, u32[]{:S(2)}) collective-permute-start(bf16[64,640]{1,0:T(8,128)(2,1)S(1)} %get-tuple-element.98.refs_4_), channel_id=1, source_target_pairs={{0,2},{2,0},{4,6},{6,4},{8,10},{10,8},{12,14},{14,12},{16,18},{18,... | collective-permute-start | bytes 245768 | tf_op jit(solution)/shard_map/ppermute | solution.py:574
  127.9 5.5 %collective-permute-start.15 = (bf16[64,640]{1,0:T(8,128)(2,1)S(1)}, bf16[64,640]{1,0:T(8,128)(2,1)S(1)}, u32[]{:S(2)}, u32[]{:S(2)}) collective-permute-start(bf16[64,640]{1,0:T(8,128)(2,1)S(1)} %get-tuple-element.99.refs_5_), channel_id=1, source_target_pairs={{0,126},{2,4},{4,2},{6,8},{8,6},{10,12},{12,10},{14,16},{16,14},{1... | collective-permute-start | bytes 245768 | tf_op jit(solution)/shard_map/ppermute | solution.py:573
  135.5 9.7 %collective-permute-start.16 = (bf16[64,640]{1,0:T(8,128)(2,1)S(1)}, bf16[64,640]{1,0:T(8,128)(2,1)S(1)}, u32[]{:S(2)}, u32[]{:S(2)}) collective-permute-start(bf16[64,640]{1,0:T(8,128)(2,1)S(1)} %get-tuple-element.102.refs_4_), channel_id=1, source_target_pairs={{0,2},{2,0},{4,6},{6,4},{8,10},{10,8},{12,14},{14,12},{16,18},{18,... | collective-permute-start | bytes 245768 | tf_op jit(solution)/shard_map/ppermute | solution.py:574
  139.7 5.5 %collective-permute-start.17 = (bf16[64,640]{1,0:T(8,128)(2,1)S(1)}, bf16[64,640]{1,0:T(8,128)(2,1)S(1)}, u32[]{:S(2)}, u32[]{:S(2)}) collective-permute-start(bf16[64,640]{1,0:T(8,128)(2,1)S(1)} %get-tuple-element.103.refs_5_), channel_id=1, source_target_pairs={{0,126},{2,4},{4,2},{6,8},{8,6},{10,12},{12,10},{14,16},{16,14},{1... | collective-permute-start | bytes 245768 | tf_op jit(solution)/shard_map/ppermute | solution.py:573
  170.8 1.9 %collective-permute-start.18 = (bf16[32,64,128]{2,1,0:T(8,128)(2,1)S(1)}, bf16[32,64,128]{2,1,0:T(8,128)(2,1)S(1)}, u32[]{:S(2)}, u32[]{:S(2)}) collective-permute-start(bf16[32,64,128]{2,1,0:T(8,128)(2,1)S(1)} %all_to_all.34.mine_ref), channel_id=1, source_target_pairs={{0,2},{2,0},{4,6},{6,4},{8,10},{10,8},{12,14},{14,12},{16,18},{18,... | collective-permute-start | bytes 1572872 | tf_op jit(solution)/shard_map/ppermute | solution.py:652

commit v2 on v1

--- a/solution.py
+++ b/solution.py
@@ -43,11 +43,8 @@
 
 
 def by_rows(rows, run):
-    def step(g, carry):
-        run(pl.ds(pl.multiple_of(g * GROUP, GROUP), GROUP))
-        return carry
-
-    lax.fori_loop(0, rows // GROUP, step, 0)
+    for at in range(0, rows, GROUP):
+        run(slice(at, at + GROUP))
 
 
 def operator(read, first, last, total, coefs, before, after, emit):
@@ -276,13 +273,6 @@
     margin = (order - own) // 2
     sweep_residual(r_ref, parts(v_ref, u0_ref, u3_ref, own), (dg_ref, cp_ref), s_ref)
 
-    def inner(j, carry):
-        at = pl.multiple_of(j * own, own)
-        p = dot_t(s_ref[:, pl.ds(pl.multiple_of(at - margin, TILE), order)], L_ref[j])
-        out_ref[:, pl.ds(at, own)] = v_ref[:, pl.ds(at, own)] + p
-        return carry
-
-    lax.fori_loop(1, subs - 1, inner, 0)
     for j, u_ref in ((0, u0_ref), (subs - 1, u3_ref)):
         at = j * own
         lo = at - margin
@@ -291,6 +281,14 @@
             s_ref[:, a:b], L_ref[j, :, a - lo : b - lo]
         )
 
+    def inner(j, carry):
+        at = pl.multiple_of(j * own, own)
+        p = dot_t(s_ref[:, pl.ds(pl.multiple_of(at - margin, TILE), order)], L_ref[j])
+        out_ref[:, pl.ds(at, own)] = v_ref[:, pl.ds(at, own)] + p
+        return carry
+
+    lax.fori_loop(1, subs - 1, inner, 0)
+
 
 def edge_sends(r_ref, dg_ref, cp_ref, u0_ref, u3_ref, left_ref, right_ref):
     rows, total = r_ref.shape
@@ -321,47 +319,49 @@
 
 def edges(first, *refs):
     (core_ref, v_ref, gota_ref, gotb_ref, owna_ref, ownb_ref, metaa_ref, metab_ref) = refs[:8]
-    (r_ref, dg_ref, cp_ref, L_ref, u0_ref, u3_ref, senda_ref, sendb_ref) = refs[8:]
+    (r_ref, dg_ref, cp_ref, L_ref, u0_ref, u3_ref, senda_ref, sendb_ref) = refs[8:16]
+    (wl_ref, wr_ref, info_ref, sl_ref, sr_ref) = refs[16:]
     total = v_ref.shape[1]
     subs, own, order = L_ref.shape
     wide = CH + TILE
-
-    def run(even):
-        order_of = (lambda a, b: (b, a)) if even else (lambda a, b: (a, b))
-        gotl_ref, gotr_ref = order_of(gota_ref, gotb_ref)
-        ownl_ref, ownr_ref = order_of(owna_ref, ownb_ref)
-        metal_ref, metar_ref = order_of(metaa_ref, metab_ref)
-        tile_l, tile_r = ownl_ref[:, :TILE], ownr_ref[:, CH - TILE : CH]
-        halo_l, halo_r = gotl_ref[:, :CH], gotr_ref[:, :CH]
+    spreads = slice(CH, wide)
+
+    def gather(even):
+        a, b = (gota_ref, owna_ref, metaa_ref), (gotb_ref, ownb_ref, metab_ref)
+        (gl, ol, ml), (gr, orr, mr) = (b, a) if even else (a, b)
+        wl_ref[:, :CH] = gl[:, :CH]
+        wl_ref[:, CH:] = ol[:, :TILE]
+        wr_ref[:, :TILE] = orr[:, CH - TILE : CH]
+        wr_ref[:, TILE:] = gr[:, :CH]
         if not first:
-            lane_t = lane_of(tile_l.shape)
-            mine_l = column(ownl_ref[:, CH : CH + TILE], 0)
-            mine_r = column(ownr_ref[:, CH : CH + TILE], 0)
-            rim_l = column(gotl_ref[:, CH : CH + TILE], 0)
-            rim_r = column(gotr_ref[:, CH : CH + TILE], 0)
-            coup_l = column(metal_ref[:, CH : CH + TILE], 0)
-            coup_r = column(metar_ref[:, CH : CH + TILE], 0)
-            add = lambda x, at, y: (
-                x.astype(F32) + jnp.where(lane_t == at, y, 0.0)
-            ).astype(BF16)
-            tile_l = add(tile_l, 0, cp_ref[:, :1] * rim_l)
-            tile_r = add(tile_r, TILE - 1, cp_ref[:, total - 1 :] * rim_r)
-            halo_l = jnp.concatenate(
-                [halo_l[:, : CH - TILE], add(halo_l[:, CH - TILE :], TILE - 1, coup_l * mine_l)],
-                axis=1,
-            )
-            halo_r = jnp.concatenate(
-                [add(halo_r[:, :TILE], 0, coup_r * mine_r), halo_r[:, TILE:]], axis=1
-            )
-        u0_ref[...] = v_ref[:, :own] + dot_t(
-            jnp.concatenate([halo_l, tile_l], axis=1), L_ref[0, :, :wide]
-        )
-        u3_ref[...] = v_ref[:, total - own :] + dot_t(
-            jnp.concatenate([tile_r, halo_r], axis=1), L_ref[subs - 1, :, order - wide :]
-        )
-        edge_sends(r_ref, dg_ref, cp_ref, u0_ref, u3_ref, *order_of(senda_ref, sendb_ref))
-
-    by_side(core_ref, run)
+            for k, ref in enumerate((gl, gr, ol, orr, ml, mr)):
+                info_ref[k] = ref[:, spreads]
+
+    by_side(core_ref, gather)
+    if not first:
+        rim_l, rim_r, mine_l, mine_r, coup_l, coup_r = (
+            column(info_ref[k], 0) for k in range(6)
+        )
+        lane = lane_of((v_ref.shape[0], TILE))
+        for ref, lo, at, y in (
+            (wl_ref, CH, 0, cp_ref[:, :1] * rim_l),
+            (wr_ref, 0, TILE - 1, cp_ref[:, total - 1 :] * rim_r),
+            (wl_ref, CH - TILE, TILE - 1, coup_l * mine_l),
+            (wr_ref, TILE, 0, coup_r * mine_r),
+        ):
+            x = ref[:, lo : lo + TILE].astype(F32)
+            ref[:, lo : lo + TILE] = (x + jnp.where(lane == at, y, 0.0)).astype(BF16)
+    u0_ref[...] = v_ref[:, :own] + dot_t(wl_ref[...], L_ref[0, :, :wide])
+    u3_ref[...] = v_ref[:, total - own :] + dot_t(
+        wr_ref[...], L_ref[subs - 1, :, order - wide :]
+    )
+    edge_sends(r_ref, dg_ref, cp_ref, u0_ref, u3_ref, sl_ref, sr_ref)
+
+    def send(even):
+        senda_ref[...] = (sr_ref if even else sl_ref)[...]
+        sendb_ref[...] = (sl_ref if even else sr_ref)[...]
+
+    by_side(core_ref, send)
 
 
 def project(core_ref, v_ref, u0_ref, u3_ref, r_ref, dg_ref, cp_ref, basis_ref, metaa_ref, metab_ref,
@@ -485,26 +485,25 @@
             ).astype(BF16)
 
     by_side(core_ref, halo)
-
-    def update(k, carry):
-        cols = pl.ds(pl.multiple_of(k * CH, CH), CH)
+    for lo in range(0, total, TILE):
+        cols = slice(lo, lo + TILE)
         r = r_ref[:, cols] - alpha * image_ref[:, cols]
         res_ref[:, cols] = r
         sol_ref[:, cols] = alpha * x_ref[:, cols]
-        s_ref[:, pl.ds(pl.multiple_of((k + 1) * CH, CH), CH)] = r.astype(BF16)
-        return carry
-
-    lax.fori_loop(0, total // CH, update, 0)
+        s_ref[:, CH + lo : CH + lo + TILE] = r.astype(BF16)
     subs = L_ref.shape[0]
+
+    u0_ref[...] = dot_t(s_ref[:, :order], L_ref[0])
+    u3_ref[...] = dot_t(s_ref[:, total - own :], L_ref[subs - 1])
+    u_ref[:, :own] = u0_ref[...]
+    u_ref[:, total - own :] = u3_ref[...]
 
     def step(j, carry):
         at = pl.multiple_of(j * own, own)
         u_ref[:, pl.ds(at, own)] = dot_t(s_ref[:, pl.ds(at, order)], L_ref[j])
         return carry
 
-    lax.fori_loop(0, subs, step, 0)
-    u0_ref[...] = u_ref[:, :own]
-    u3_ref[...] = u_ref[:, total - own :]
+    lax.fori_loop(1, subs - 1, step, 0)
     edge_sends(res_ref, dg_ref, cp_ref, u0_ref, u3_ref, sl_ref, sr_ref)
 
     def send(even):
@@ -631,6 +630,7 @@
                 functools.partial(edges, first), "edges_first" if first else "edges",
                 [sub, sub, send, send],
                 [core, vv, ga, gb, sa, sb, got_a0, got_b0, r, dg, cp, L],
+                pair(send) + [pltpu.VMEM((6, rows, TILE), BF16)] + pair(send),
                 flops=work // 8,
             )
             v = vv

time: 190 us -> 184 us (0.968)
  Pallas kernels: 79.2 us -> 69 us
    pallas_call x23, Pallas kernels: 79.2 us -> 69 us  [call(): pl.pallas_call(kernel, out_shape=outs, in_specs=specs or [pl.BlockSpec(me...]
    ppermute x8, waiting for transfers between devices: 0.02 us -> 2.15 us  [exchange(): got_b = lax.ppermute(b, 'sector', side)]
  transfers between devices with their start and end apart: 19 -> 19, of which waited for: 2 -> 6; matrix products, arithmetic and copies ran while one was open for 0% -> 0% of each run, Pallas kernels for 25% -> 23%
where the time goes in v2:
time: 184 us; the launch traced here: 183 us
  blocking collectives  75.1 us (41%)
  Pallas kernels  69 us (38%)
  starting transfers between devices  30.6 us (17%)
  waiting for transfers between devices  5.62 us (3%)
    pallas_call x23, Pallas kernels, call(): pl.pallas_call(kernel, out_shape=outs, in_specs=specs or [pl.BlockSpec(me...  69 us
    all_to_all x2, blocking collectives, coarse_step(): lax.all_to_all(chunk, 'sector', 0, 0, axis_index_groups=planes, tiled=True)  43.8 us
    all_to_all x2, blocking collectives, body(): sums = lax.all_to_all(sums, 'sector', 0, 0, tiled=True)  31.4 us
    ppermute x8, starting transfers between devices, exchange(): got_a = lax.ppermute(a, 'sector', chip)  25.7 us
    ppermute x8, starting transfers between devices, exchange(): got_b = lax.ppermute(b, 'sector', side)  4.09 us
  transfers between devices with their start and end apart: 19, of which 6 were waited for; matrix products, arithmetic and copies ran while one was open for 0% of the time, Pallas kernels for 23%

profile of v2, /device:TPU:1, one launch (start us, length us, event | category | flops | bytes accessed | tf_op | source)
XLA Modules:
  0.0 183.3 jit_solution(18183040174885786732)
XLA Ops:
  0.6 0.0 copy-start.1
  0.7 0.6 pad_add_fusion.core_ref.refs_0_
  1.4 2.9 %first_edges.1 = (bf16[64,768]{1,0:T(8,128)(2,1)}, bf16[64,768]{1,0:T(8,128)(2,1)}) custom-call(s32[4]{0:T(128)} %pad_add_fusion.core_ref.refs_0_, f32[64,4096]{1,0:T(8,128)} %r_ref.13, f32[1,4096]{1,0:T(1,128)} %bitcast.14, bf16[4,16,1024]{2,1,0:T(8,128)(2,1)} %basis_ref.7, f32[64,2048]{1,0:T(8,128)} %ci_ref), custom_call_target="tpu_custom_call" | custom-call | bytes 1720336 | tf_op jit(solution)/shard_map/first_edges/pallas_call | solution.py:528
  4.2 1.5 collective-permute-start
  5.7 2.8 %collective-permute-start.1 = (bf16[64,768]{1,0:T(8,128)(2,1)}, bf16[64,768]{1,0:T(8,128)(2,1)S(1)}, u32[]{:S(2)}, u32[]{:S(2)}) collective-permute-start(bf16[64,768]{1,0:T(8,128)(2,1)} %get-tuple-element.61.refs_5_), channel_id=1, source_target_pairs={{0,126},{2,4},{4,2},{6,8},{8,6},{10,12},{12,10},{14,16},{16,14},{1... | collective-permute-start | bytes 294920 | tf_op jit(solution)/shard_map/ppermute | solution.py:572
  8.5 1.2 copy-done
  9.8 7.7 %middle_first.1 = (f32[64,4096]{1,0:T(8,128)S(1)}, bf16[4,1024,2048]{2,1,0:T(8,128)(2,1)S(1)}) custom-call(f32[64,4096]{1,0:T(8,128)S(1)} %copy-done, bf16[4,1024,2048]{2,1,0:T(8,128)(2,1)} %L_hbm.1), custom_call_target="tpu_custom_call" | custom-call | flops 1073741824 | bytes 17825792 | tf_op jit(solution)/shard_map/middle_first/pallas_call | solution.py:528
  17.5 0.0 collective-permute-done.refs_2_.refs_6_.a_ref.metaa_ref.ha0_ref
  17.5 0.0 collective-permute-done.1.refs_3_.refs_7_.b_ref.metab_ref.hb0_ref
  17.5 0.0 copy-start.4
  17.5 1.7 edges_first.1
  19.2 6.4 %collective-permute-start.2 = (bf16[64,640]{1,0:T(8,128)(2,1)S(1)}, bf16[64,640]{1,0:T(8,128)(2,1)S(1)}, u32[]{:S(2)}, u32[]{:S(2)}) collective-permute-start(bf16[64,640]{1,0:T(8,128)(2,1)S(1)} %get-tuple-element.65.refs_4_), channel_id=1, source_target_pairs={{0,2},{2,0},{4,6},{6,4},{8,10},{10,8},{12,14},{14,12},{16,18},{18,... | collective-permute-start | bytes 245768 | tf_op jit(solution)/shard_map/ppermute | solution.py:573
  25.6 0.0 collective-permute-start.3
  25.6 4.8 %middle.6.refs_1_.v_ref = f32[64,4096]{1,0:T(8,128)S(1)} custom-call(f32[64,4096]{1,0:T(8,128)S(1)} %copy-done, f32[64,4096]{1,0:T(8,128)S(1)} %get-tuple-element.59.refs_1_.v_ref, f32[64,1024]{1,0:T(8,128)S(1)} %get-tuple-element.63.u0_ref, f32[64,1024]{1,0:T(8,128)S(1)} %get-tuple-element.64.u3_ref, f32[1,4096]{1,0:T(1,128)S(1)} %bitcast.34, ...), custom_call_target="tpu_custom_call" | custom-call | flops 1073741824 | bytes 19431424 | tf_op jit(solution)/shard_map/middle/pallas_call | solution.py:528
  30.4 0.6 lines.1.mine_ref
  31.0 0.4 collective-permute-start.6
  31.4 0.0 collective-permute-done.2.refs_2_
  31.4 0.0 collective-permute-done.3.refs_3_
  31.4 1.7 edges.6
  33.1 4.0 %collective-permute-start.4 = (bf16[64,640]{1,0:T(8,128)(2,1)S(1)}, bf16[64,640]{1,0:T(8,128)(2,1)S(1)}, u32[]{:S(2)}, u32[]{:S(2)}) collective-permute-start(bf16[64,640]{1,0:T(8,128)(2,1)S(1)} %get-tuple-element.69.refs_4_), channel_id=1, source_target_pairs={{0,2},{2,0},{4,6},{6,4},{8,10},{10,8},{12,14},{14,12},{16,18},{18,... | collective-permute-start | bytes 245768 | tf_op jit(solution)/shard_map/ppermute | solution.py:573
  37.1 0.3 collective-permute-start.5
  37.4 4.8 %middle.7.refs_1_.v_ref = f32[64,4096]{1,0:T(8,128)S(1)} custom-call(f32[64,4096]{1,0:T(8,128)S(1)} %copy-done, f32[64,4096]{1,0:T(8,128)S(1)} %middle.6.refs_1_.v_ref, f32[64,1024]{1,0:T(8,128)S(1)} %get-tuple-element.67.u0_ref, f32[64,1024]{1,0:T(8,128)S(1)} %get-tuple-element.68.u3_ref, f32[1,4096]{1,0:T(1,128)S(1)} %bitcast.36, f32[1,4096]{1,0:T(1,128)S(1)} %bitcast.18, ...), custom_call_target="tpu_custom_call" | custom-call | flops 1073741824 | bytes 19431424 | tf_op jit(solution)/shard_map/middle/pallas_call | solution.py:528
  42.2 0.0 collective-permute-done.4.refs_2_
  42.2 0.2 collective-permute-done.5.refs_3_
  42.5 1.7 edges.7
  44.2 4.4 %collective-permute-start.7 = (bf16[64,640]{1,0:T(8,128)(2,1)S(1)}, bf16[64,640]{1,0:T(8,128)(2,1)S(1)}, u32[]{:S(2)}, u32[]{:S(2)}) collective-permute-start(bf16[64,640]{1,0:T(8,128)(2,1)S(1)} %get-tuple-element.76.refs_4_), channel_id=1, source_target_pairs={{0,2},{2,0},{4,6},{6,4},{8,10},{10,8},{12,14},{14,12},{16,18},{18,... | collective-permute-start | bytes 245768 | tf_op jit(solution)/shard_map/ppermute | solution.py:573
  48.6 0.0 collective-permute-start.8
  48.6 4.8 %middle.8.refs_1_.v_ref = f32[64,4096]{1,0:T(8,128)S(1)} custom-call(f32[64,4096]{1,0:T(8,128)S(1)} %copy-done, f32[64,4096]{1,0:T(8,128)S(1)} %middle.7.refs_1_.v_ref, f32[64,1024]{1,0:T(8,128)S(1)} %get-tuple-element.71.u0_ref, f32[64,1024]{1,0:T(8,128)S(1)} %get-tuple-element.72.u3_ref, f32[1,4096]{1,0:T(1,128)S(1)} %bitcast.38, f32[1,4096]{1,0:T(1,128)S(1)} %bitcast.20, ...), custom_call_target="tpu_custom_call" | custom-call | flops 1073741824 | bytes 19431424 | tf_op jit(solution)/shard_map/middle/pallas_call | solution.py:528
  53.4 0.0 collective-permute-done.6.other_ref
  53.4 1.8 weave.1.W_ref
  55.2 0.0 collective-permute-done.7.refs_2_
  55.2 1.7 edges.8
  57.0 1.5 project.2
  58.5 22.0 %all_to_all.32.mine_ref = bf16[32,64,128]{2,1,0:T(8,128)(2,1)S(1)} all-to-all(bf16[32,64,128]{2,1,0:T(8,128)(2,1)S(1)} %project.2), channel_id=1, replica_groups={{0,4,8,12,16,20,24,28,32,36,40,44,48,52,56,60,64,68,72,76,80,84,88,92,9..., dimensions={0} | all-to-all | bytes 1048576 | tf_op jit(solution)/shard_map/all_to_all | solution.py:649
  80.5 0.0 collective-permute-start.9
  80.5 1.9 %collective-permute-done.9.other_ref = bf16[32,64,128]{2,1,0:T(8,128)(2,1)S(1)} collective-permute-done((bf16[32,64,128]{2,1,0:T(8,128)(2,1)S(1)}, bf16[32,64,128]{2,1,0:T(8,128)(2,1)S(1)}, u32[]{:S(2)}, u32[]{:S(2)}) %collective-permute-start.9) | collective-permute-done | bytes 524320 | tf_op jit(solution)/shard_map/ppermute | solution.py:652
  82.4 2.2 %coarse.2 = (f32[64,4096]{1,0:T(8,128)S(1)}, f32[64,4096]{1,0:T(8,128)S(1)}, f32[64,128]{1,0:T(8,128)S(1)}, bf16[64,512]{1,0:T(8,128)(2,1)S(1)}, bf16[64,512]{1,0:T(8,128)(2,1)S(1)}) custom-call(s32[4]{0:T(128)S(1)} %copy-done.5, bf16[32,64,128]{2,1,0:T(8,128)(2,1)S(1)} %all_to_all.32.mine_ref, bf16[32,64,128]{2,1,0:T(8,128)(2,1)S(1)} %collective-permute-done.9.other_ref, ...), custom_call_target="tpu_custom_call" | custom-call | bytes 5013520 | tf_op jit(solution)/shard_map/coarse/pallas_call | solution.py:528
  84.6 0.2 collective-permute-start.10
  84.8 0.5 collective-permute-start.11
  85.3 18.3 %all_to_all.33 = f32[64,1,128]{2,1,0:T(1,128)S(1)} all-to-all(f32[64,1,128]{2,1,0:T(1,128)S(1)} %bitcast.53), channel_id=1, replica_groups=mesh['sector'=64,'lift'=2] {'sector'}, dimensions={0} | all-to-all | bytes 65536 | tf_op jit(solution)/shard_map/all_to_all | solution.py:662
  103.6 0.0 collective-permute-done.10.ha_ref
  103.6 0.0 collective-permute-done.11.hb_ref
  103.6 6.5 %second.1 = (f32[64,4096]{1,0:T(8,128)S(1)}, f32[64,4096]{1,0:T(8,128)S(1)}, f32[64,4096]{1,0:T(8,128)S(1)}, f32[64,1024]{1,0:T(8,128)S(1)}, f32[64,1024]{1,0:T(...) custom-call(s32[4]{0:T(128)S(1)} %copy-done.5, f32[64,128]{1,0:T(8,128)S(1)} %bitcast.51, ...), custom_call_target="tpu_custom_call" | custom-call | flops 1073741824 | bytes 20316176 | tf_op jit(solution)/shard_map/second/pallas_call | solution.py:528
  110.1 0.8 collective-permute-start.12
  110.9 0.5 collective-permute-start.13
  111.4 4.7 %middle.9.refs_1_.v_ref = f32[64,4096]{1,0:T(8,128)S(1)} custom-call(f32[64,4096]{1,0:T(8,128)S(1)} %get-tuple-element.90.r_ref.refs_8_, f32[64,4096]{1,0:T(8,128)S(1)} %get-tuple-element.91.v_ref, f32[64,1024]{1,0:T(8,128)S(1)} %get-tuple-element.92.u0_ref, f32[64,1024]{1,0:T(8,128)S(1)} %get-tuple-element.93.u3_ref, f32[1,4096]{1,0:T(1,128)S(1)} %bitcast.43, ...), custom_call_target="tpu_custom_call" | custom-call | flops 1073741824 | bytes 19431424 | tf_op jit(solution)/shard_map/middle/pallas_call | solution.py:528
  116.1 0.7 collective-permute-done.13.refs_3_
  116.8 1.7 edges.9
  118.5 4.1 %collective-permute-start.14 = (bf16[64,640]{1,0:T(8,128)(2,1)S(1)}, bf16[64,640]{1,0:T(8,128)(2,1)S(1)}, u32[]{:S(2)}, u32[]{:S(2)}) collective-permute-start(bf16[64,640]{1,0:T(8,128)(2,1)S(1)} %get-tuple-element.98.refs_4_), channel_id=1, source_target_pairs={{0,2},{2,0},{4,6},{6,4},{8,10},{10,8},{12,14},{14,12},{16,18},{18,... | collective-permute-start | bytes 245768 | tf_op jit(solution)/shard_map/ppermute | solution.py:573
  122.6 0.0 collective-permute-start.15
  122.6 4.7 %middle.10.refs_1_.v_ref = f32[64,4096]{1,0:T(8,128)S(1)} custom-call(f32[64,4096]{1,0:T(8,128)S(1)} %get-tuple-element.90.r_ref.refs_8_, f32[64,4096]{1,0:T(8,128)S(1)} %middle.9.refs_1_.v_ref, f32[64,1024]{1,0:T(8,128)S(1)} %get-tuple-element.96.u0_ref, f32[64,1024]{1,0:T(8,128)S(1)} %get-tuple-element.97.u3_ref, f32[1,4096]{1,0:T(1,128)S(1)} %bitcast.45, ...), custom_call_target="tpu_custom_call" | custom-call | flops 1073741824 | bytes 19431424 | tf_op jit(solution)/shard_map/middle/pallas_call | solution.py:528
  127.4 0.6 collective-permute-done.15.refs_3_
  128.0 1.7 edges.10
  129.7 4.4 %collective-permute-start.16 = (bf16[64,640]{1,0:T(8,128)(2,1)S(1)}, bf16[64,640]{1,0:T(8,128)(2,1)S(1)}, u32[]{:S(2)}, u32[]{:S(2)}) collective-permute-start(bf16[64,640]{1,0:T(8,128)(2,1)S(1)} %get-tuple-element.102.refs_4_), channel_id=1, source_target_pairs={{0,2},{2,0},{4,6},{6,4},{8,10},{10,8},{12,14},{14,12},{16,18},{18,... | collective-permute-start | bytes 245768 | tf_op jit(solution)/shard_map/ppermute | solution.py:573
  134.1 4.8 %middle.11.refs_1_.v_ref = f32[64,4096]{1,0:T(8,128)S(1)} custom-call(f32[64,4096]{1,0:T(8,128)S(1)} %get-tuple-element.90.r_ref.refs_8_, f32[64,4096]{1,0:T(8,128)S(1)} %middle.10.refs_1_.v_ref, f32[64,1024]{1,0:T(8,128)S(1)} %get-tuple-element.100.u0_ref, f32[64,1024]{1,0:T(8,128)S(1)} %get-tuple-element.101.u3_ref, f32[1,4096]{1,0:T(1,128)S(1)} %bitcast.47, ...), custom_call_target="tpu_custom_call" | custom-call | flops 1073741824 | bytes 19431424 | tf_op jit(solution)/shard_map/middle/pallas_call | solution.py:528
  138.9 0.6 collective-permute-done.17.refs_3_
  139.5 1.7 edges.11
  141.2 1.5 project.3
  142.7 21.8 %all_to_all.34.mine_ref = bf16[32,64,128]{2,1,0:T(8,128)(2,1)S(1)} all-to-all(bf16[32,64,128]{2,1,0:T(8,128)(2,1)S(1)} %project.3), channel_id=1, replica_groups={{0,4,8,12,16,20,24,28,32,36,40,44,48,52,56,60,64,68,72,76,80,84,88,92,9..., dimensions={0} | all-to-all | bytes 1048576 | tf_op jit(solution)/shard_map/all_to_all | solution.py:649
  164.4 0.4 collective-permute-start.18
  164.8 1.5 collective-permute-done.18.other_ref
  166.4 2.2 %coarse.3 = (f32[64,4096]{1,0:T(8,128)S(1)}, f32[64,4096]{1,0:T(8,128)S(1)}, f32[64,128]{1,0:T(8,128)S(1)}, bf16[64,512]{1,0:T(8,128)(2,1)S(1)}, bf16[64,512]{1,0:T(8,128)(2,1)S(1)}) custom-call(s32[4]{0:T(128)S(1)} %copy-done.5, bf16[32,64,128]{2,1,0:T(8,128)(2,1)S(1)} %all_to_all.34.mine_ref, bf16[32,64,128]{2,1,0:T(8,128)(2,1)S(1)} %collective-permute-done.18.other_ref, ...), custom_call_target="tpu_custom_call" | custom-call | bytes 5013520 | tf_op jit(solution)/shard_map/coarse/pallas_call | solution.py:528
  168.5 13.1 %all_to_all.35 = f32[64,1,128]{2,1,0:T(1,128)S(1)} all-to-all(f32[64,1,128]{2,1,0:T(1,128)S(1)} %bitcast.54), channel_id=1, replica_groups=mesh['sector'=64,'lift'=2] {'sector'}, dimensions={0} | all-to-all | bytes 65536 | tf_op jit(solution)/shard_map/all_to_all | solution.py:670
  181.6 1.7 finish.1
  (18 shorter events, 0.0 us)
Async XLA Ops:
  0.6 16.9 %copy-start.1 = (f32[4096]{0:T(1024)S(1)}, f32[4096]{0:T(1024)}, u32[]{:S(2)}) copy-start(f32[4096]{0:T(1024)} %param.8) | copy-start | bytes 49156
  0.6 16.9 %copy-start.2 = (f32[4096]{0:T(1024)S(1)}, f32[4096]{0:T(1024)}, u32[]{:S(2)}) copy-start(f32[4096]{0:T(1024)} %param.7) | copy-start | bytes 49156
  1.4 16.1 %copy-start.5 = (s32[4]{0:T(128)S(1)}, s32[4]{0:T(128)}, u32[]{:S(2)}) copy-start(s32[4]{0:T(128)} %pad_add_fusion.core_ref.refs_0_) | copy-start | bytes 52
  4.2 13.2 %collective-permute-start = (bf16[64,768]{1,0:T(8,128)(2,1)}, bf16[64,768]{1,0:T(8,128)(2,1)S(1)}, u32[]{:S(2)}, u32[]{:S(2)}) collective-permute-start(bf16[64,768]{1,0:T(8,128)(2,1)} %get-tuple-element.60.refs_4_), channel_id=1, source_target_pairs={{0,2},{2,0},{4,6},{6,4},{8,10},{10,8},{12,14},{14,12},{16,18},{18,... | collective-permute-start | bytes 294920 | tf_op jit(solution)/shard_map/ppermute | solution.py:573
  5.7 11.8 %collective-permute-start.1 = (bf16[64,768]{1,0:T(8,128)(2,1)}, bf16[64,768]{1,0:T(8,128)(2,1)S(1)}, u32[]{:S(2)}, u32[]{:S(2)}) collective-permute-start(bf16[64,768]{1,0:T(8,128)(2,1)} %get-tuple-element.61.refs_5_), channel_id=1, source_target_pairs={{0,126},{2,4},{4,2},{6,8},{8,6},{10,12},{12,10},{14,16},{16,14},{1... | collective-permute-start | bytes 294920 | tf_op jit(solution)/shard_map/ppermute | solution.py:572
  8.5 1.2 copy-start
  9.8 7.8 %copy-start.6 = (bf16[64,768]{1,0:T(8,128)(2,1)S(1)}, bf16[64,768]{1,0:T(8,128)(2,1)}, u32[]{:S(2)}) copy-start(bf16[64,768]{1,0:T(8,128)(2,1)} %get-tuple-element.60.refs_4_) | copy-start | bytes 294916
  9.8 7.8 %copy-start.7 = (bf16[64,768]{1,0:T(8,128)(2,1)S(1)}, bf16[64,768]{1,0:T(8,128)(2,1)}, u32[]{:S(2)}) copy-start(bf16[64,768]{1,0:T(8,128)(2,1)} %get-tuple-element.61.refs_5_) | copy-start | bytes 294916
  17.5 12.9 %copy-start.4 = (f32[64,2048]{1,0:T(8,128)S(1)}, f32[64,2048]{1,0:T(8,128)}, u32[]{:S(2)}) copy-start(f32[64,2048]{1,0:T(8,128)} %ci_ref) | copy-start | bytes 1572868
  19.2 12.2 %collective-permute-start.2 = (bf16[64,640]{1,0:T(8,128)(2,1)S(1)}, bf16[64,640]{1,0:T(8,128)(2,1)S(1)}, u32[]{:S(2)}, u32[]{:S(2)}) collective-permute-start(bf16[64,640]{1,0:T(8,128)(2,1)S(1)} %get-tuple-element.65.refs_4_), channel_id=1, source_target_pairs={{0,2},{2,0},{4,6},{6,4},{8,10},{10,8},{12,14},{14,12},{16,18},{18,... | collective-permute-start | bytes 245768 | tf_op jit(solution)/shard_map/ppermute | solution.py:573
  25.6 5.8 %collective-permute-start.3 = (bf16[64,640]{1,0:T(8,128)(2,1)S(1)}, bf16[64,640]{1,0:T(8,128)(2,1)S(1)}, u32[]{:S(2)}, u32[]{:S(2)}) collective-permute-start(bf16[64,640]{1,0:T(8,128)(2,1)S(1)} %get-tuple-element.66.refs_5_), channel_id=1, source_target_pairs={{0,126},{2,4},{4,2},{6,8},{8,6},{10,12},{12,10},{14,16},{16,14},{1... | collective-permute-start | bytes 245768 | tf_op jit(solution)/shard_map/ppermute | solution.py:572
  31.0 22.4 %collective-permute-start.6 = (bf16[72,2048]{1,0:T(8,128)(2,1)S(1)}, bf16[72,2048]{1,0:T(8,128)(2,1)S(1)}, u32[]{:S(2)}, u32[]{:S(2)}) collective-permute-start(bf16[72,2048]{1,0:T(8,128)(2,1)S(1)} %lines.1.mine_ref), channel_id=1, source_target_pairs={{0,1},{1,0},{2,3},{3,2},{4,5},{5,4},{6,7},{7,6},{8,9},{9,8},{10,11... | collective-permute-start | bytes 884744 | tf_op jit(solution)/shard_map/ppermute | solution.py:614
  33.1 9.1 %collective-permute-start.4 = (bf16[64,640]{1,0:T(8,128)(2,1)S(1)}, bf16[64,640]{1,0:T(8,128)(2,1)S(1)}, u32[]{:S(2)}, u32[]{:S(2)}) collective-permute-start(bf16[64,640]{1,0:T(8,128)(2,1)S(1)} %get-tuple-element.69.refs_4_), channel_id=1, source_target_pairs={{0,2},{2,0},{4,6},{6,4},{8,10},{10,8},{12,14},{14,12},{16,18},{18,... | collective-permute-start | bytes 245768 | tf_op jit(solution)/shard_map/ppermute | solution.py:573
  37.1 5.4 %collective-permute-start.5 = (bf16[64,640]{1,0:T(8,128)(2,1)S(1)}, bf16[64,640]{1,0:T(8,128)(2,1)S(1)}, u32[]{:S(2)}, u32[]{:S(2)}) collective-permute-start(bf16[64,640]{1,0:T(8,128)(2,1)S(1)} %get-tuple-element.70.refs_5_), channel_id=1, source_target_pairs={{0,126},{2,4},{4,2},{6,8},{8,6},{10,12},{12,10},{14,16},{16,14},{1... | collective-permute-start | bytes 245768 | tf_op jit(solution)/shard_map/ppermute | solution.py:572
  44.2 11.0 %collective-permute-start.7 = (bf16[64,640]{1,0:T(8,128)(2,1)S(1)}, bf16[64,640]{1,0:T(8,128)(2,1)S(1)}, u32[]{:S(2)}, u32[]{:S(2)}) collective-permute-start(bf16[64,640]{1,0:T(8,128)(2,1)S(1)} %get-tuple-element.76.refs_4_), channel_id=1, source_target_pairs={{0,2},{2,0},{4,6},{6,4},{8,10},{10,8},{12,14},{14,12},{16,18},{18,... | collective-permute-start | bytes 245768 | tf_op jit(solution)/shard_map/ppermute | solution.py:573
  48.6 6.7 %collective-permute-start.8 = (bf16[64,640]{1,0:T(8,128)(2,1)S(1)}, bf16[64,640]{1,0:T(8,128)(2,1)S(1)}, u32[]{:S(2)}, u32[]{:S(2)}) collective-permute-start(bf16[64,640]{1,0:T(8,128)(2,1)S(1)} %get-tuple-element.77.refs_5_), channel_id=1, source_target_pairs={{0,126},{2,4},{4,2},{6,8},{8,6},{10,12},{12,10},{14,16},{16,14},{1... | collective-permute-start | bytes 245768 | tf_op jit(solution)/shard_map/ppermute | solution.py:572
  48.6 8.4 %copy-start.3 = (bf16[4,16,1024]{2,1,0:T(8,128)(2,1)S(1)}, bf16[4,16,1024]{2,1,0:T(8,128)(2,1)}, u32[]{:S(2)}) copy-start(bf16[4,16,1024]{2,1,0:T(8,128)(2,1)} %basis_ref.7) | copy-start | bytes 393220
  80.5 1.9 %collective-permute-start.9 = (bf16[32,64,128]{2,1,0:T(8,128)(2,1)S(1)}, bf16[32,64,128]{2,1,0:T(8,128)(2,1)S(1)}, u32[]{:S(2)}, u32[]{:S(2)}) collective-permute-start(bf16[32,64,128]{2,1,0:T(8,128)(2,1)S(1)} %all_to_all.32.mine_ref), channel_id=1, source_target_pairs={{0,2},{2,0},{4,6},{6,4},{8,10},{10,8},{12,14},{14,12},{16,18},{18,... | collective-permute-start | bytes 1572872 | tf_op jit(solution)/shard_map/ppermute | solution.py:652
  84.6 19.0 %collective-permute-start.10 = (bf16[64,512]{1,0:T(8,128)(2,1)S(1)}, bf16[64,512]{1,0:T(8,128)(2,1)S(1)}, u32[]{:S(2)}, u32[]{:S(2)}) collective-permute-start(bf16[64,512]{1,0:T(8,128)(2,1)S(1)} %get-tuple-element.88), channel_id=1, source_target_pairs={{0,2},{2,0},{4,6},{6,4},{8,10},{10,8},{12,14},{14,12},{16,18},{18,... | collective-permute-start | bytes 196616 | tf_op jit(solution)/shard_map/ppermute | solution.py:573
  84.8 18.8 %collective-permute-start.11 = (bf16[64,512]{1,0:T(8,128)(2,1)S(1)}, bf16[64,512]{1,0:T(8,128)(2,1)S(1)}, u32[]{:S(2)}, u32[]{:S(2)}) collective-permute-start(bf16[64,512]{1,0:T(8,128)(2,1)S(1)} %get-tuple-element.89), channel_id=1, source_target_pairs={{0,126},{2,4},{4,2},{6,8},{8,6},{10,12},{12,10},{14,16},{16,14},{1... | collective-permute-start | bytes 196616 | tf_op jit(solution)/shard_map/ppermute | solution.py:572
  110.1 6.0 %collective-permute-start.12 = (bf16[64,640]{1,0:T(8,128)(2,1)S(1)}, bf16[64,640]{1,0:T(8,128)(2,1)S(1)}, u32[]{:S(2)}, u32[]{:S(2)}) collective-permute-start(bf16[64,640]{1,0:T(8,128)(2,1)S(1)} %get-tuple-element.94.refs_4_), channel_id=1, source_target_pairs={{0,2},{2,0},{4,6},{6,4},{8,10},{10,8},{12,14},{14,12},{16,18},{18,... | collective-permute-start | bytes 245768 | tf_op jit(solution)/shard_map/ppermute | solution.py:573
  110.9 5.9 %collective-permute-start.13 = (bf16[64,640]{1,0:T(8,128)(2,1)S(1)}, bf16[64,640]{1,0:T(8,128)(2,1)S(1)}, u32[]{:S(2)}, u32[]{:S(2)}) collective-permute-start(bf16[64,640]{1,0:T(8,128)(2,1)S(1)} %get-tuple-element.95.refs_5_), channel_id=1, source_target_pairs={{0,126},{2,4},{4,2},{6,8},{8,6},{10,12},{12,10},{14,16},{16,14},{1... | collective-permute-start | bytes 245768 | tf_op jit(solution)/shard_map/ppermute | solution.py:572
  118.5 8.8 %collective-permute-start.14 = (bf16[64,640]{1,0:T(8,128)(2,1)S(1)}, bf16[64,640]{1,0:T(8,128)(2,1)S(1)}, u32[]{:S(2)}, u32[]{:S(2)}) collective-permute-start(bf16[64,640]{1,0:T(8,128)(2,1)S(1)} %get-tuple-element.98.refs_4_), channel_id=1, source_target_pairs={{0,2},{2,0},{4,6},{6,4},{8,10},{10,8},{12,14},{14,12},{16,18},{18,... | collective-permute-start | bytes 245768 | tf_op jit(solution)/shard_map/ppermute | solution.py:573
  122.6 5.4 %collective-permute-start.15 = (bf16[64,640]{1,0:T(8,128)(2,1)S(1)}, bf16[64,640]{1,0:T(8,128)(2,1)S(1)}, u32[]{:S(2)}, u32[]{:S(2)}) collective-permute-start(bf16[64,640]{1,0:T(8,128)(2,1)S(1)} %get-tuple-element.99.refs_5_), channel_id=1, source_target_pairs={{0,126},{2,4},{4,2},{6,8},{8,6},{10,12},{12,10},{14,16},{16,14},{1... | collective-permute-start | bytes 245768 | tf_op jit(solution)/shard_map/ppermute | solution.py:572
  129.7 9.2 %collective-permute-start.16 = (bf16[64,640]{1,0:T(8,128)(2,1)S(1)}, bf16[64,640]{1,0:T(8,128)(2,1)S(1)}, u32[]{:S(2)}, u32[]{:S(2)}) collective-permute-start(bf16[64,640]{1,0:T(8,128)(2,1)S(1)} %get-tuple-element.102.refs_4_), channel_id=1, source_target_pairs={{0,2},{2,0},{4,6},{6,4},{8,10},{10,8},{12,14},{14,12},{16,18},{18,... | collective-permute-start | bytes 245768 | tf_op jit(solution)/shard_map/ppermute | solution.py:573
  134.1 5.4 %collective-permute-start.17 = (bf16[64,640]{1,0:T(8,128)(2,1)S(1)}, bf16[64,640]{1,0:T(8,128)(2,1)S(1)}, u32[]{:S(2)}, u32[]{:S(2)}) collective-permute-start(bf16[64,640]{1,0:T(8,128)(2,1)S(1)} %get-tuple-element.103.refs_5_), channel_id=1, source_target_pairs={{0,126},{2,4},{4,2},{6,8},{8,6},{10,12},{12,10},{14,16},{16,14},{1... | collective-permute-start | bytes 245768 | tf_op jit(solution)/shard_map/ppermute | solution.py:572
  164.4 1.9 %collective-permute-start.18 = (bf16[32,64,128]{2,1,0:T(8,128)(2,1)S(1)}, bf16[32,64,128]{2,1,0:T(8,128)(2,1)S(1)}, u32[]{:S(2)}, u32[]{:S(2)}) collective-permute-start(bf16[32,64,128]{2,1,0:T(8,128)(2,1)S(1)} %all_to_all.34.mine_ref), channel_id=1, source_target_pairs={{0,2},{2,0},{4,6},{6,4},{8,10},{10,8},{12,14},{14,12},{16,18},{18,... | collective-permute-start | bytes 1572872 | tf_op jit(solution)/shard_map/ppermute | solution.py:652

commit v3 on v2

--- a/solution.py
+++ b/solution.py
@@ -216,21 +216,23 @@
     margin = (order - own) // 2
     subs = L_ref.shape[0]
     part = own // 2
-
-    def rows_at(k):
+    quarter = own // 4
+
+    def rows_at(k, part=part):
         return pl.ds(pl.multiple_of(k * part, part), part)
 
     def first(k, carry):
-        p = dot_t(s_ref[:, TILE : order - margin], L_ref[0, rows_at(k), margin + TILE :])
-        store(pl.multiple_of(k * part, part), part, p)
+        p = dot_t(s_ref[:, TILE : order - margin], L_ref[0, rows_at(k, quarter), margin + TILE :])
+        store(pl.multiple_of(k * quarter, quarter), quarter, p)
         return carry
 
     def last(k, carry):
         start = (subs - 1) * own - margin
         p = dot_t(
-            s_ref[:, start : total - TILE], L_ref[subs - 1, rows_at(k), : total - TILE - start]
-        )
-        store(pl.multiple_of((subs - 1) * own + k * part, part), part, p)
+            s_ref[:, start : total - TILE],
+            L_ref[subs - 1, rows_at(k, quarter), : total - TILE - start],
+        )
+        store(pl.multiple_of((subs - 1) * own + k * quarter, quarter), quarter, p)
         return carry
 
     def inner(n, carry):
@@ -244,11 +246,11 @@
 
     if ready is not None:
         ready(0)
-    lax.fori_loop(0, 2, first, 0)
+    lax.fori_loop(0, 4, first, 0)
     lax.fori_loop(0, 2 * (subs - 2), inner, 0)
     if ready is not None:
         ready(subs - 1)
-    lax.fori_loop(0, 2, last, 0)
+    lax.fori_loop(0, 4, last, 0)
 
 
 def middle_first(r_ref, L_hbm, v_ref, L_ref, s_ref, sem):
@@ -265,6 +267,23 @@
         v_ref[:, pl.ds(at, size)] = p
 
     products(s_ref, L_ref, own, order, store, lambda j: copy(j).wait())
+
+
+def complete(v_ref, near_l_ref, near_r_ref, wl_ref, wr_ref, L_ref, u0_ref, u3_ref):
+    subs, own, order = L_ref.shape
+    total, wide = v_ref.shape[1], wl_ref.shape[1]
+    u0_ref[:, :wide] = near_l_ref[...]
+    u0_ref[:, wide:] = v_ref[:, wide:own] + dot_t(wl_ref[...], L_ref[0, wide:, :wide])
+    u3_ref[:, own - wide :] = near_r_ref[...]
+    u3_ref[:, : own - wide] = v_ref[:, total - own : total - wide] + dot_t(
+        wr_ref[...], L_ref[subs - 1, : own - wide, order - wide :]
+    )
+
+
+def middle_near(r_ref, v_ref, near_l_ref, near_r_ref, wl_ref, wr_ref, dg_ref, cp_ref, L_ref,
+                out_ref, s_ref, u0_ref, u3_ref):
+    complete(v_ref, near_l_ref, near_r_ref, wl_ref, wr_ref, L_ref, u0_ref, u3_ref)
+    middle(r_ref, v_ref, u0_ref, u3_ref, dg_ref, cp_ref, L_ref, out_ref, s_ref)
 
 
 def middle(r_ref, v_ref, u0_ref, u3_ref, dg_ref, cp_ref, L_ref, out_ref, s_ref):
@@ -319,8 +338,8 @@
 
 def edges(first, *refs):
     (core_ref, v_ref, gota_ref, gotb_ref, owna_ref, ownb_ref, metaa_ref, metab_ref) = refs[:8]
-    (r_ref, dg_ref, cp_ref, L_ref, u0_ref, u3_ref, senda_ref, sendb_ref) = refs[8:16]
-    (wl_ref, wr_ref, info_ref, sl_ref, sr_ref) = refs[16:]
+    (r_ref, dg_ref, cp_ref, L_ref, u0_ref, u3_ref, wl_ref, wr_ref) = refs[8:16]
+    (senda_ref, sendb_ref, info_ref, sl_ref, sr_ref) = refs[16:]
     total = v_ref.shape[1]
     subs, own, order = L_ref.shape
     wide = CH + TILE
@@ -351,9 +370,9 @@
         ):
             x = ref[:, lo : lo + TILE].astype(F32)
             ref[:, lo : lo + TILE] = (x + jnp.where(lane == at, y, 0.0)).astype(BF16)
-    u0_ref[...] = v_ref[:, :own] + dot_t(wl_ref[...], L_ref[0, :, :wide])
-    u3_ref[...] = v_ref[:, total - own :] + dot_t(
-        wr_ref[...], L_ref[subs - 1, :, order - wide :]
+    u0_ref[...] = v_ref[:, :wide] + dot_t(wl_ref[...], L_ref[0, :wide, :wide])
+    u3_ref[...] = v_ref[:, total - wide :] + dot_t(
+        wr_ref[...], L_ref[subs - 1, own - wide :, order - wide :]
     )
     edge_sends(r_ref, dg_ref, cp_ref, u0_ref, u3_ref, sl_ref, sr_ref)
 
@@ -364,8 +383,10 @@
     by_side(core_ref, send)
 
 
-def project(core_ref, v_ref, u0_ref, u3_ref, r_ref, dg_ref, cp_ref, basis_ref, metaa_ref, metab_ref,
-            unused_a, unused_b, out_ref, s_ref, metal_ref, metar_ref):
+def project(core_ref, v_ref, near_l_ref, near_r_ref, wl_ref, wr_ref, L_ref, r_ref, dg_ref, cp_ref,
+            basis_ref, metaa_ref, metab_ref, unused_a, unused_b, out_ref, u0_ref, u3_ref,
+            s_ref, metal_ref, metar_ref):
+    complete(v_ref, near_l_ref, near_r_ref, wl_ref, wr_ref, L_ref, u0_ref, u3_ref)
     rows, total = r_ref.shape
     own = basis_ref.shape[2]
     modes = basis_ref.shape[1]
@@ -516,10 +537,15 @@
 def finish(sums_ref, x_ref, image_ref, r_ref, sol_in_ref, unused_a, unused_b, sol_ref, res_ref):
     rows, total = r_ref.shape
     alpha = step_of(sums_ref, rows)
-    for lo in range(0, total, CH):
-        hi = lo + CH
-        res_ref[:, lo:hi] = r_ref[:, lo:hi] - alpha * image_ref[:, lo:hi]
-        sol_ref[:, lo:hi] = sol_in_ref[:, lo:hi] + alpha * x_ref[:, lo:hi]
+    width = total // 2
+
+    def half(k, carry):
+        cols = pl.ds(pl.multiple_of(k * width, width), width)
+        res_ref[:, cols] = r_ref[:, cols] - alpha * image_ref[:, cols]
+        sol_ref[:, cols] = sol_in_ref[:, cols] + alpha * x_ref[:, cols]
+        return carry
+
+    lax.fori_loop(0, 2, half, 0)
 
 
 def call(kernel, name, outs, args, scratch=(), limit=8, flops=0, smem=1, specs=None):
@@ -562,6 +588,7 @@
     shape = jax.ShapeDtypeStruct
     full = shape((rows, total), F32)
     sub = shape((rows, own), F32)
+    near = shape((rows, wide), F32)
     send = shape((rows, wide), BF16)
     long = shape((rows, wide + TILE), BF16)
     s_scratch = pltpu.VMEM((rows, total), BF16)
@@ -595,16 +622,22 @@
     )
     weights = []
 
-    def sweeps(v, u0, u3, sa, sb, start):
+    def sweeps(v, u, sa, sb, start):
         for sweep in range(start, SWEEPS):
             last = sweep == SWEEPS - 1
             if sweep == 0:
                 vv, ga, gb = v, got_a0, got_b0
             else:
                 ga, gb = exchange(sa, sb)
-                vv = call(
-                    middle, "middle", full, [r, v, u0, u3, dg, cp, L], [s_scratch], 8, work, 0
-                )
+                if len(u) == 2:
+                    vv = call(
+                        middle, "middle", full, [r, v, *u, dg, cp, L], [s_scratch], 8, work, 0
+                    )
+                else:
+                    vv = call(
+                        middle_near, "middle_near", full, [r, v, *u, dg, cp, L],
+                        [s_scratch] + pair(sub), 8, work, 0,
+                    )
             if sweep == 1 and not weights:
                 ci, _ = lax.optimization_barrier((coarse_inverse, vv))
                 lines = call(
@@ -612,52 +645,52 @@
                     [core, ci, got_a0, got_b0], pair(long),
                 )
                 other = lax.ppermute(lines, "lift", [(0, 1), (1, 0)])
-                weights.append((lines, other))
+                weights.append([lines, other])
             if sweep == 2 and len(weights) == 1:
-                lines, other = weights[0]
-                other, _ = lax.optimization_barrier((other, vv))
-                weights.append(
-                    call(
-                        weave, "weave", shape((lines.shape[0], sectors * TILE), BF16),
-                        [core, lines, other],
-                        [pltpu.VMEM((lines.shape[0], 2 * lines.shape[1] + 2 * TILE), F32)],
-                    )
-                )
+                vv, *weights[0] = lax.optimization_barrier((vv, *weights[0]))
             first = sweep == 0
-            if last and start == 0:
-                vv, weights[1] = lax.optimization_barrier((vv, weights[1]))
-            u0, u3, sa, sb = call(
+            *u, sa, sb = call(
                 functools.partial(edges, first), "edges_first" if first else "edges",
-                [sub, sub, send, send],
+                [near, near, send, send, send, send],
                 [core, vv, ga, gb, sa, sb, got_a0, got_b0, r, dg, cp, L],
-                pair(send) + [pltpu.VMEM((6, rows, TILE), BF16)] + pair(send),
+                [pltpu.VMEM((6, rows, TILE), BF16)] + pair(send),
                 flops=work // 8,
             )
             v = vv
-        return v, u0, u3, sa, sb
+        return v, u, sa, sb
 
     edge = shape((rows, CH), BF16)
 
-    def coarse_step(v, u0, u3, sa, sb):
-        W = weights[1]
-        chunk = call(
-            project, "project", shape((sectors // 2, rows, TILE), BF16),
-            [core, v, u0, u3, r, dg, cp, basis, got_a0, got_b0, sa, sb],
+    def coarse_step(v, u, sa, sb):
+        chunk, u0, u3 = call(
+            project, "project", [shape((sectors // 2, rows, TILE), BF16), sub, sub],
+            [core, v, *u, L, r, dg, cp, basis, got_a0, got_b0, sa, sb],
             [s_scratch] + [pltpu.VMEM((modes, TILE), BF16)] * 2,
         )
-        chunk, W = lax.optimization_barrier((chunk, W))
         mine = lax.all_to_all(
             chunk, "sector", 0, 0, axis_index_groups=planes, tiled=True
         )
         other = lax.ppermute(mine, "sector", chip)
+        if len(weights) == 1:
+            lines, swapped = weights[0]
+            lines, swapped, _ = lax.optimization_barrier((lines, swapped, mine))
+            weights.append(
+                call(
+                    weave, "weave", shape((lines.shape[0], sectors * TILE), BF16),
+                    [core, lines, swapped],
+                    [pltpu.VMEM((lines.shape[0], 2 * lines.shape[1] + 2 * TILE), F32)],
+                    flops=1 << 26,
+                )
+            )
+        W = weights[1]
         return call(
             coarse, "coarse", [full, full, shape((sectors, 2 * rows), F32), edge, edge],
             [core, mine, other, W, v, u0, u3, r, dg, cp, basis],
             [pltpu.VMEM((2, rows, TILE), F32)] * 2,
         )
 
-    v, u0, u3, sa, sb = sweeps(v, None, None, sa, sb, 0)
-    x, image, sums, ia, ib = coarse_step(v, u0, u3, sa, sb)
+    v, u, sa, sb = sweeps(v, None, sa, sb, 0)
+    x, image, sums, ia, ib = coarse_step(v, u, sa, sb)
     halo_a, halo_b = exchange(ia, ib)
     sums = lax.all_to_all(sums, "sector", 0, 0, tiled=True)
     sol, r, v, u0, u3, sa, sb = call(
@@ -665,8 +698,8 @@
         [core, sums, x, image, r, got_a0, got_b0, halo_a, halo_b, dg, cp, L],
         [pltpu.VMEM((rows, total + 2 * CH), BF16)] + pair(send), 8, work,
     )
-    v, u0, u3, sa, sb = sweeps(v, u0, u3, sa, sb, 1)
-    x, image, sums, ia, ib = coarse_step(v, u0, u3, sa, sb)
+    v, u, sa, sb = sweeps(v, (u0, u3), sa, sb, 1)
+    x, image, sums, ia, ib = coarse_step(v, u, sa, sb)
     sums = lax.all_to_all(sums, "sector", 0, 0, tiled=True)
     sol, res = call(finish, "finish", [full, full], [sums, x, image, r, sol, ia, ib], smem=0)
     return sol, res

time: 184 us -> 189 us (1.027)
  waiting for transfers between devices: 5.62 us -> 9.13 us
    ppermute x8, waiting for transfers between devices: 2.15 us -> 6.22 us  [exchange(): got_b = lax.ppermute(b, 'sector', side)]
  transfers between devices with their start and end apart: 19 -> 19, of which waited for: 6 -> 9; matrix products, arithmetic and copies ran while one was open for 0% -> 0% of each run, Pallas kernels for 23% -> 19%
where the time goes in v3:
time: 189 us; the launch traced here: 188 us
  blocking collectives  75 us (40%)
  Pallas kernels  70.5 us (37%)
  starting transfers between devices  31.1 us (16%)
  waiting for transfers between devices  9.13 us (5%)
    pallas_call x23, Pallas kernels, call(): pl.pallas_call(kernel, out_shape=outs, in_specs=specs or [pl.BlockSpec(me...  70.5 us
    all_to_all x2, blocking collectives, coarse_step(): lax.all_to_all(chunk, 'sector', 0, 0, axis_index_groups=planes, tiled=True)  43.8 us
    all_to_all x2, blocking collectives, body(): sums = lax.all_to_all(sums, 'sector', 0, 0, tiled=True)  31.2 us
    ppermute x8, starting transfers between devices, exchange(): got_a = lax.ppermute(a, 'sector', chip)  27.2 us
    ppermute x8, waiting for transfers between devices, exchange(): got_b = lax.ppermute(b, 'sector', side)  6.22 us
  transfers between devices with their start and end apart: 19, of which 9 were waited for; matrix products, arithmetic and copies ran while one was open for 0% of the time, Pallas kernels for 19%

profile of v3, /device:TPU:1, one launch (start us, length us, event | category | flops | bytes accessed | tf_op | source)
XLA Modules:
  0.0 188.5 jit_solution(1984374744181366414)
XLA Ops:
  0.6 0.0 copy-start.1
  0.7 0.6 pad_add_fusion.core_ref.refs_0_
  1.3 2.9 %first_edges.1 = (bf16[64,768]{1,0:T(8,128)(2,1)}, bf16[64,768]{1,0:T(8,128)(2,1)}) custom-call(s32[4]{0:T(128)} %pad_add_fusion.core_ref.refs_0_, f32[64,4096]{1,0:T(8,128)} %r_ref.13, f32[1,4096]{1,0:T(1,128)} %bitcast.14, bf16[4,16,1024]{2,1,0:T(8,128)(2,1)} %basis_ref.7, f32[64,2048]{1,0:T(8,128)} %ci_ref), custom_call_target="tpu_custom_call" | custom-call | bytes 1720336 | tf_op jit(solution)/shard_map/first_edges/pallas_call | solution.py:554
  4.2 1.5 collective-permute-start
  5.7 2.8 %collective-permute-start.1 = (bf16[64,768]{1,0:T(8,128)(2,1)}, bf16[64,768]{1,0:T(8,128)(2,1)S(1)}, u32[]{:S(2)}, u32[]{:S(2)}) collective-permute-start(bf16[64,768]{1,0:T(8,128)(2,1)} %get-tuple-element.79.refs_5_), channel_id=1, source_target_pairs={{0,126},{2,4},{4,2},{6,8},{8,6},{10,12},{12,10},{14,16},{16,14},{1... | collective-permute-start | bytes 294920 | tf_op jit(solution)/shard_map/ppermute | solution.py:599
  8.5 1.2 copy-done
  9.7 8.2 %middle_first.1 = (f32[64,4096]{1,0:T(8,128)S(1)}, bf16[4,1024,2048]{2,1,0:T(8,128)(2,1)S(1)}) custom-call(f32[64,4096]{1,0:T(8,128)S(1)} %copy-done, bf16[4,1024,2048]{2,1,0:T(8,128)(2,1)} %L_hbm.1), custom_call_target="tpu_custom_call" | custom-call | flops 1073741824 | bytes 17825792 | tf_op jit(solution)/shard_map/middle_first/pallas_call | solution.py:554
  17.9 0.0 collective-permute-done.refs_2_.refs_6_.a_ref.metaa_ref.ha0_ref
  17.9 0.0 collective-permute-done.1.refs_3_.refs_7_.b_ref.metab_ref.hb0_ref
  18.0 0.0 copy-start.4
  18.0 1.3 edges_first.1
  19.3 5.1 %middle_near.5.refs_1_.v_ref = f32[64,4096]{1,0:T(8,128)S(1)} custom-call(f32[64,4096]{1,0:T(8,128)S(1)} %copy-done, f32[64,4096]{1,0:T(8,128)S(1)} %get-tuple-element.77.refs_1_.v_ref, f32[64,640]{1,0:T(8,128)S(1)} %get-tuple-element.81.near_l_ref, f32[64,640]{1,0:T(8,128)S(1)} %get-tuple-element.82.near_r_ref, ...), custom_call_target="tpu_custom_call" | custom-call | flops 1073741824 | bytes 19398656 | tf_op jit(solution)/shard_map/middle_near/pallas_call | solution.py:554
  24.4 0.6 lines.1.mine_ref
  25.0 0.4 collective-permute-start.4
  25.4 6.6 %collective-permute-start.2 = (bf16[64,640]{1,0:T(8,128)(2,1)S(1)}, bf16[64,640]{1,0:T(8,128)(2,1)S(1)}, u32[]{:S(2)}, u32[]{:S(2)}) collective-permute-start(bf16[64,640]{1,0:T(8,128)(2,1)S(1)} %get-tuple-element.85.refs_4_), channel_id=1, source_target_pairs={{0,2},{2,0},{4,6},{6,4},{8,10},{10,8},{12,14},{14,12},{16,18},{18,... | collective-permute-start | bytes 245768 | tf_op jit(solution)/shard_map/ppermute | solution.py:600
  32.1 0.0 collective-permute-start.3
  32.1 0.9 collective-permute-done.2.refs_2_
  33.0 4.4 %collective-permute-done.3.refs_3_ = bf16[64,640]{1,0:T(8,128)(2,1)S(1)} collective-permute-done((bf16[64,640]{1,0:T(8,128)(2,1)S(1)}, bf16[64,640]{1,0:T(8,128)(2,1)S(1)}, u32[]{:S(2)}, u32[]{:S(2)}) %collective-permute-start.3) | collective-permute-done | bytes 81952 | tf_op jit(solution)/shard_map/ppermute | solution.py:599
  37.4 1.5 edges.6
  38.9 4.9 %collective-permute-start.5 = (bf16[64,640]{1,0:T(8,128)(2,1)S(1)}, bf16[64,640]{1,0:T(8,128)(2,1)S(1)}, u32[]{:S(2)}, u32[]{:S(2)}) collective-permute-start(bf16[64,640]{1,0:T(8,128)(2,1)S(1)} %get-tuple-element.93.refs_4_), channel_id=1, source_target_pairs={{0,2},{2,0},{4,6},{6,4},{8,10},{10,8},{12,14},{14,12},{16,18},{18,... | collective-permute-start | bytes 245768 | tf_op jit(solution)/shard_map/ppermute | solution.py:600
  43.8 0.0 collective-permute-start.6
  43.8 5.1 %middle_near.6.refs_1_.v_ref = f32[64,4096]{1,0:T(8,128)S(1)} custom-call(f32[64,4096]{1,0:T(8,128)S(1)} %copy-done, f32[64,4096]{1,0:T(8,128)S(1)} %middle_near.5.refs_1_.v_ref, f32[64,640]{1,0:T(8,128)S(1)} %get-tuple-element.87.near_l_ref, f32[64,640]{1,0:T(8,128)S(1)} %get-tuple-element.88.near_r_ref, bf16[64,640]{1,0:T(8,128)(2,1)S(1)} %get-tuple-element.89.wl_ref, ...), custom_call_target="tpu_custom_call" | custom-call | flops 1073741824 | bytes 19398656 | tf_op jit(solution)/shard_map/middle_near/pallas_call | solution.py:554
  48.9 0.0 collective-permute-done.4.other_ref
  48.9 0.0 collective-permute-done.5.refs_2_
  48.9 0.3 collective-permute-done.6.refs_3_
  49.2 1.5 edges.7
  50.6 4.4 %collective-permute-start.7 = (bf16[64,640]{1,0:T(8,128)(2,1)S(1)}, bf16[64,640]{1,0:T(8,128)(2,1)S(1)}, u32[]{:S(2)}, u32[]{:S(2)}) collective-permute-start(bf16[64,640]{1,0:T(8,128)(2,1)S(1)} %get-tuple-element.99.refs_4_), channel_id=1, source_target_pairs={{0,2},{2,0},{4,6},{6,4},{8,10},{10,8},{12,14},{14,12},{16,18},{18,... | collective-permute-start | bytes 245768 | tf_op jit(solution)/shard_map/ppermute | solution.py:600
  55.0 0.0 collective-permute-start.8
  55.0 5.1 %middle_near.7.refs_1_.v_ref = f32[64,4096]{1,0:T(8,128)S(1)} custom-call(f32[64,4096]{1,0:T(8,128)S(1)} %copy-done, f32[64,4096]{1,0:T(8,128)S(1)} %middle_near.6.refs_1_.v_ref, f32[64,640]{1,0:T(8,128)S(1)} %get-tuple-element.95.near_l_ref, f32[64,640]{1,0:T(8,128)S(1)} %get-tuple-element.96.near_r_ref, bf16[64,640]{1,0:T(8,128)(2,1)S(1)} %get-tuple-element.97.wl_ref, ...), custom_call_target="tpu_custom_call" | custom-call | flops 1073741824 | bytes 19398656 | tf_op jit(solution)/shard_map/middle_near/pallas_call | solution.py:554
  60.1 0.0 collective-permute-done.7.refs_2_
  60.1 0.3 collective-permute-done.8.refs_3_
  60.4 1.5 edges.8
  61.9 2.0 %project.2 = (bf16[32,64,128]{2,1,0:T(8,128)(2,1)S(1)}, f32[64,1024]{1,0:T(8,128)S(1)}, f32[64,1024]{1,0:T(8,128)S(1)}) custom-call(s32[4]{0:T(128)S(1)} %copy-done.5, f32[64,4096]{1,0:T(8,128)S(1)} %middle_near.7.refs_1_.v_ref, f32[64,640]{1,0:T(8,128)S(1)} %get-tuple-element.101.near_l_ref, f32[64,640]{1,0:T(8,128)S(1)} %get-tuple-element.102.near_r_ref, ...), custom_call_target="tpu_custom_call" | custom-call | bytes 19890192 | tf_op jit(solution)/shard_map/project/pallas_call | solution.py:554
  63.8 22.0 %all_to_all.32.mine_ref = bf16[32,64,128]{2,1,0:T(8,128)(2,1)S(1)} all-to-all(bf16[32,64,128]{2,1,0:T(8,128)(2,1)S(1)} %get-tuple-element.107), channel_id=1, replica_groups={{0,4,8,12,16,20,24,28,32,36,40,44,48,52,56,60,64,68,72,76,80,84,88,92,9..., dimensions={0} | all-to-all | bytes 1048576 | tf_op jit(solution)/shard_map/all_to_all | solution.py:670
  85.8 0.0 collective-permute-start.9
  85.8 1.8 weave.1.W_ref
  87.7 0.1 collective-permute-done.9.other_ref
  87.7 2.2 %coarse.2 = (f32[64,4096]{1,0:T(8,128)S(1)}, f32[64,4096]{1,0:T(8,128)S(1)}, f32[64,128]{1,0:T(8,128)S(1)}, bf16[64,512]{1,0:T(8,128)(2,1)S(1)}, bf16[64,512]{1,0:T(8,128)(2,1)S(1)}) custom-call(s32[4]{0:T(128)S(1)} %copy-done.5, bf16[32,64,128]{2,1,0:T(8,128)(2,1)S(1)} %all_to_all.32.mine_ref, bf16[32,64,128]{2,1,0:T(8,128)(2,1)S(1)} %collective-permute-done.9.other_ref, ...), custom_call_target="tpu_custom_call" | custom-call | bytes 5013520 | tf_op jit(solution)/shard_map/coarse/pallas_call | solution.py:554
  89.9 0.5 collective-permute-start.10
  90.4 0.2 collective-permute-start.11
  90.6 18.3 %all_to_all.33 = f32[64,1,128]{2,1,0:T(1,128)S(1)} all-to-all(f32[64,1,128]{2,1,0:T(1,128)S(1)} %bitcast.53), channel_id=1, replica_groups=mesh['sector'=64,'lift'=2] {'sector'}, dimensions={0} | all-to-all | bytes 65536 | tf_op jit(solution)/shard_map/all_to_all | solution.py:695
  108.9 0.0 collective-permute-done.10.ha_ref
  108.9 0.0 collective-permute-done.11.hb_ref
  108.9 6.5 %second.1 = (f32[64,4096]{1,0:T(8,128)S(1)}, f32[64,4096]{1,0:T(8,128)S(1)}, f32[64,4096]{1,0:T(8,128)S(1)}, f32[64,1024]{1,0:T(8,128)S(1)}, f32[64,1024]{1,0:T(...) custom-call(s32[4]{0:T(128)S(1)} %copy-done.5, f32[64,128]{1,0:T(8,128)S(1)} %bitcast.51, ...), custom_call_target="tpu_custom_call" | custom-call | flops 1073741824 | bytes 20316176 | tf_op jit(solution)/shard_map/second/pallas_call | solution.py:554
  115.4 0.8 collective-permute-start.12
  116.3 0.4 collective-permute-start.13
  116.7 4.7 %middle.1.refs_1_.v_ref = f32[64,4096]{1,0:T(8,128)S(1)} custom-call(f32[64,4096]{1,0:T(8,128)S(1)} %get-tuple-element.119.r_ref.refs_8_, f32[64,4096]{1,0:T(8,128)S(1)} %get-tuple-element.120.v_ref, f32[64,1024]{1,0:T(8,128)S(1)} %get-tuple-element.121.u0_ref, f32[64,1024]{1,0:T(8,128)S(1)} %get-tuple-element.122.u3_ref, f32[1,4096]{1,0:T(1,128)S(1)} %bitcast.43, ...), custom_call_target="tpu_custom_call" | custom-call | flops 1073741824 | bytes 19431424 | tf_op jit(solution)/shard_map/middle/pallas_call | solution.py:554
  121.5 0.7 collective-permute-done.13.refs_3_
  122.2 1.5 edges.9
  123.6 4.1 %collective-permute-start.14 = (bf16[64,640]{1,0:T(8,128)(2,1)S(1)}, bf16[64,640]{1,0:T(8,128)(2,1)S(1)}, u32[]{:S(2)}, u32[]{:S(2)}) collective-permute-start(bf16[64,640]{1,0:T(8,128)(2,1)S(1)} %get-tuple-element.129.refs_4_), channel_id=1, source_target_pairs={{0,2},{2,0},{4,6},{6,4},{8,10},{10,8},{12,14},{14,12},{16,18},{18,... | collective-permute-start | bytes 245768 | tf_op jit(solution)/shard_map/ppermute | solution.py:600
  127.7 5.1 %middle_near.8.refs_1_.v_ref = f32[64,4096]{1,0:T(8,128)S(1)} custom-call(f32[64,4096]{1,0:T(8,128)S(1)} %get-tuple-element.119.r_ref.refs_8_, f32[64,4096]{1,0:T(8,128)S(1)} %middle.1.refs_1_.v_ref, f32[64,640]{1,0:T(8,128)S(1)} %get-tuple-element.125.near_l_ref, f32[64,640]{1,0:T(8,128)S(1)} %get-tuple-element.126.near_r_ref, ...), custom_call_target="tpu_custom_call" | custom-call | flops 1073741824 | bytes 19398656 | tf_op jit(solution)/shard_map/middle_near/pallas_call | solution.py:554
  132.8 0.3 collective-permute-done.15.refs_3_
  133.1 1.5 edges.10
  134.6 4.4 %collective-permute-start.16 = (bf16[64,640]{1,0:T(8,128)(2,1)S(1)}, bf16[64,640]{1,0:T(8,128)(2,1)S(1)}, u32[]{:S(2)}, u32[]{:S(2)}) collective-permute-start(bf16[64,640]{1,0:T(8,128)(2,1)S(1)} %get-tuple-element.135.refs_4_), channel_id=1, source_target_pairs={{0,2},{2,0},{4,6},{6,4},{8,10},{10,8},{12,14},{14,12},{16,18},{18,... | collective-permute-start | bytes 245768 | tf_op jit(solution)/shard_map/ppermute | solution.py:600
  139.0 5.1 %middle_near.9.refs_1_.v_ref = f32[64,4096]{1,0:T(8,128)S(1)} custom-call(f32[64,4096]{1,0:T(8,128)S(1)} %get-tuple-element.119.r_ref.refs_8_, f32[64,4096]{1,0:T(8,128)S(1)} %middle_near.8.refs_1_.v_ref, f32[64,640]{1,0:T(8,128)S(1)} %get-tuple-element.131.near_l_ref, f32[64,640]{1,0:T(8,128)S(1)} %get-tuple-element.132.near_r_ref, ...), custom_call_target="tpu_custom_call" | custom-call | flops 1073741824 | bytes 19398656 | tf_op jit(solution)/shard_map/middle_near/pallas_call | solution.py:554
  144.0 0.3 collective-permute-done.17.refs_3_
  144.3 1.5 edges.11
  145.8 2.0 %project.3 = (bf16[32,64,128]{2,1,0:T(8,128)(2,1)S(1)}, f32[64,1024]{1,0:T(8,128)S(1)}, f32[64,1024]{1,0:T(8,128)S(1)}) custom-call(s32[4]{0:T(128)S(1)} %copy-done.5, f32[64,4096]{1,0:T(8,128)S(1)} %middle_near.9.refs_1_.v_ref, f32[64,640]{1,0:T(8,128)S(1)} %get-tuple-element.137.near_l_ref, f32[64,640]{1,0:T(8,128)S(1)} %get-tuple-element.138.near_r_ref, ...), custom_call_target="tpu_custom_call" | custom-call | bytes 19890192 | tf_op jit(solution)/shard_map/project/pallas_call | solution.py:554
  147.8 21.8 %all_to_all.34.mine_ref = bf16[32,64,128]{2,1,0:T(8,128)(2,1)S(1)} all-to-all(bf16[32,64,128]{2,1,0:T(8,128)(2,1)S(1)} %get-tuple-element.143), channel_id=1, replica_groups={{0,4,8,12,16,20,24,28,32,36,40,44,48,52,56,60,64,68,72,76,80,84,88,92,9..., dimensions={0} | all-to-all | bytes 1048576 | tf_op jit(solution)/shard_map/all_to_all | solution.py:670
  169.6 0.0 collective-permute-start.18
  169.6 1.9 %collective-permute-done.18.other_ref = bf16[32,64,128]{2,1,0:T(8,128)(2,1)S(1)} collective-permute-done((bf16[32,64,128]{2,1,0:T(8,128)(2,1)S(1)}, bf16[32,64,128]{2,1,0:T(8,128)(2,1)S(1)}, u32[]{:S(2)}, u32[]{:S(2)}) %collective-permute-start.18) | collective-permute-done | bytes 524320 | tf_op jit(solution)/shard_map/ppermute | solution.py:673
  171.5 2.2 %coarse.3 = (f32[64,4096]{1,0:T(8,128)S(1)}, f32[64,4096]{1,0:T(8,128)S(1)}, f32[64,128]{1,0:T(8,128)S(1)}, bf16[64,512]{1,0:T(8,128)(2,1)S(1)}, bf16[64,512]{1,0:T(8,128)(2,1)S(1)}) custom-call(s32[4]{0:T(128)S(1)} %copy-done.5, bf16[32,64,128]{2,1,0:T(8,128)(2,1)S(1)} %all_to_all.34.mine_ref, bf16[32,64,128]{2,1,0:T(8,128)(2,1)S(1)} %collective-permute-done.18.other_ref, ...), custom_call_target="tpu_custom_call" | custom-call | bytes 5013520 | tf_op jit(solution)/shard_map/coarse/pallas_call | solution.py:554
  173.7 12.9 %all_to_all.35 = f32[64,1,128]{2,1,0:T(1,128)S(1)} all-to-all(f32[64,1,128]{2,1,0:T(1,128)S(1)} %bitcast.54), channel_id=1, replica_groups=mesh['sector'=64,'lift'=2] {'sector'}, dimensions={0} | all-to-all | bytes 65536 | tf_op jit(solution)/shard_map/all_to_all | solution.py:703
  186.6 1.9 %finish.1 = (f32[64,4096]{1,0:T(8,128)}, f32[64,4096]{1,0:T(8,128)}) custom-call(f32[64,128]{1,0:T(8,128)S(1)} %bitcast.52, f32[64,4096]{1,0:T(8,128)S(1)} %get-tuple-element.147.x_ref, f32[64,4096]{1,0:T(8,128)S(1)} %get-tuple-element.148.image_ref, f32[64,4096]{1,0:T(8,128)S(1)} %get-tuple-element.119.r_ref.refs_8_, ...), custom_call_target="tpu_custom_call" | custom-call | bytes 4358144 | tf_op jit(solution)/shard_map/finish/pallas_call | solution.py:554
  (18 shorter events, 0.0 us)
Async XLA Ops:
  0.6 17.3 %copy-start.1 = (f32[4096]{0:T(1024)S(1)}, f32[4096]{0:T(1024)}, u32[]{:S(2)}) copy-start(f32[4096]{0:T(1024)} %param.8) | copy-start | bytes 49156
  0.6 17.3 %copy-start.2 = (f32[4096]{0:T(1024)S(1)}, f32[4096]{0:T(1024)}, u32[]{:S(2)}) copy-start(f32[4096]{0:T(1024)} %param.7) | copy-start | bytes 49156
  1.3 16.6 %copy-start.5 = (s32[4]{0:T(128)S(1)}, s32[4]{0:T(128)}, u32[]{:S(2)}) copy-start(s32[4]{0:T(128)} %pad_add_fusion.core_ref.refs_0_) | copy-start | bytes 52
  4.2 13.7 %collective-permute-start = (bf16[64,768]{1,0:T(8,128)(2,1)}, bf16[64,768]{1,0:T(8,128)(2,1)S(1)}, u32[]{:S(2)}, u32[]{:S(2)}) collective-permute-start(bf16[64,768]{1,0:T(8,128)(2,1)} %get-tuple-element.78.refs_4_), channel_id=1, source_target_pairs={{0,2},{2,0},{4,6},{6,4},{8,10},{10,8},{12,14},{14,12},{16,18},{18,... | collective-permute-start | bytes 294920 | tf_op jit(solution)/shard_map/ppermute | solution.py:600
  5.7 12.3 %collective-permute-start.1 = (bf16[64,768]{1,0:T(8,128)(2,1)}, bf16[64,768]{1,0:T(8,128)(2,1)S(1)}, u32[]{:S(2)}, u32[]{:S(2)}) collective-permute-start(bf16[64,768]{1,0:T(8,128)(2,1)} %get-tuple-element.79.refs_5_), channel_id=1, source_target_pairs={{0,126},{2,4},{4,2},{6,8},{8,6},{10,12},{12,10},{14,16},{16,14},{1... | collective-permute-start | bytes 294920 | tf_op jit(solution)/shard_map/ppermute | solution.py:599
  8.5 1.2 copy-start
  9.7 8.2 %copy-start.6 = (bf16[64,768]{1,0:T(8,128)(2,1)S(1)}, bf16[64,768]{1,0:T(8,128)(2,1)}, u32[]{:S(2)}) copy-start(bf16[64,768]{1,0:T(8,128)(2,1)} %get-tuple-element.78.refs_4_) | copy-start | bytes 294916
  9.7 8.2 %copy-start.7 = (bf16[64,768]{1,0:T(8,128)(2,1)S(1)}, bf16[64,768]{1,0:T(8,128)(2,1)}, u32[]{:S(2)}) copy-start(bf16[64,768]{1,0:T(8,128)(2,1)} %get-tuple-element.79.refs_5_) | copy-start | bytes 294916
  18.0 6.5 %copy-start.4 = (f32[64,2048]{1,0:T(8,128)S(1)}, f32[64,2048]{1,0:T(8,128)}, u32[]{:S(2)}) copy-start(f32[64,2048]{1,0:T(8,128)} %ci_ref) | copy-start | bytes 1572868
  25.0 23.8 %collective-permute-start.4 = (bf16[72,2048]{1,0:T(8,128)(2,1)S(1)}, bf16[72,2048]{1,0:T(8,128)(2,1)S(1)}, u32[]{:S(2)}, u32[]{:S(2)}) collective-permute-start(bf16[72,2048]{1,0:T(8,128)(2,1)S(1)} %lines.1.mine_ref), channel_id=1, source_target_pairs={{0,1},{1,0},{2,3},{3,2},{4,5},{5,4},{6,7},{7,6},{8,9},{9,8},{10,11... | collective-permute-start | bytes 884744 | tf_op jit(solution)/shard_map/ppermute | solution.py:647
  25.4 7.6 %collective-permute-start.2 = (bf16[64,640]{1,0:T(8,128)(2,1)S(1)}, bf16[64,640]{1,0:T(8,128)(2,1)S(1)}, u32[]{:S(2)}, u32[]{:S(2)}) collective-permute-start(bf16[64,640]{1,0:T(8,128)(2,1)S(1)} %get-tuple-element.85.refs_4_), channel_id=1, source_target_pairs={{0,2},{2,0},{4,6},{6,4},{8,10},{10,8},{12,14},{14,12},{16,18},{18,... | collective-permute-start | bytes 245768 | tf_op jit(solution)/shard_map/ppermute | solution.py:600
  32.1 5.4 %collective-permute-start.3 = (bf16[64,640]{1,0:T(8,128)(2,1)S(1)}, bf16[64,640]{1,0:T(8,128)(2,1)S(1)}, u32[]{:S(2)}, u32[]{:S(2)}) collective-permute-start(bf16[64,640]{1,0:T(8,128)(2,1)S(1)} %get-tuple-element.86.refs_5_), channel_id=1, source_target_pairs={{0,126},{2,4},{4,2},{6,8},{8,6},{10,12},{12,10},{14,16},{16,14},{1... | collective-permute-start | bytes 245768 | tf_op jit(solution)/shard_map/ppermute | solution.py:599
  38.9 10.0 %collective-permute-start.5 = (bf16[64,640]{1,0:T(8,128)(2,1)S(1)}, bf16[64,640]{1,0:T(8,128)(2,1)S(1)}, u32[]{:S(2)}, u32[]{:S(2)}) collective-permute-start(bf16[64,640]{1,0:T(8,128)(2,1)S(1)} %get-tuple-element.93.refs_4_), channel_id=1, source_target_pairs={{0,2},{2,0},{4,6},{6,4},{8,10},{10,8},{12,14},{14,12},{16,18},{18,... | collective-permute-start | bytes 245768 | tf_op jit(solution)/shard_map/ppermute | solution.py:600
  43.8 5.4 %collective-permute-start.6 = (bf16[64,640]{1,0:T(8,128)(2,1)S(1)}, bf16[64,640]{1,0:T(8,128)(2,1)S(1)}, u32[]{:S(2)}, u32[]{:S(2)}) collective-permute-start(bf16[64,640]{1,0:T(8,128)(2,1)S(1)} %get-tuple-element.94.refs_5_), channel_id=1, source_target_pairs={{0,126},{2,4},{4,2},{6,8},{8,6},{10,12},{12,10},{14,16},{16,14},{1... | collective-permute-start | bytes 245768 | tf_op jit(solution)/shard_map/ppermute | solution.py:599
  50.6 9.5 %collective-permute-start.7 = (bf16[64,640]{1,0:T(8,128)(2,1)S(1)}, bf16[64,640]{1,0:T(8,128)(2,1)S(1)}, u32[]{:S(2)}, u32[]{:S(2)}) collective-permute-start(bf16[64,640]{1,0:T(8,128)(2,1)S(1)} %get-tuple-element.99.refs_4_), channel_id=1, source_target_pairs={{0,2},{2,0},{4,6},{6,4},{8,10},{10,8},{12,14},{14,12},{16,18},{18,... | collective-permute-start | bytes 245768 | tf_op jit(solution)/shard_map/ppermute | solution.py:600
  55.0 5.4 %collective-permute-start.8 = (bf16[64,640]{1,0:T(8,128)(2,1)S(1)}, bf16[64,640]{1,0:T(8,128)(2,1)S(1)}, u32[]{:S(2)}, u32[]{:S(2)}) collective-permute-start(bf16[64,640]{1,0:T(8,128)(2,1)S(1)} %get-tuple-element.100.refs_5_), channel_id=1, source_target_pairs={{0,126},{2,4},{4,2},{6,8},{8,6},{10,12},{12,10},{14,16},{16,14},{1... | collective-permute-start | bytes 245768 | tf_op jit(solution)/shard_map/ppermute | solution.py:599
  55.0 6.8 %copy-start.3 = (bf16[4,16,1024]{2,1,0:T(8,128)(2,1)S(1)}, bf16[4,16,1024]{2,1,0:T(8,128)(2,1)}, u32[]{:S(2)}) copy-start(bf16[4,16,1024]{2,1,0:T(8,128)(2,1)} %basis_ref.7) | copy-start | bytes 393220
  85.8 1.9 %collective-permute-start.9 = (bf16[32,64,128]{2,1,0:T(8,128)(2,1)S(1)}, bf16[32,64,128]{2,1,0:T(8,128)(2,1)S(1)}, u32[]{:S(2)}, u32[]{:S(2)}) collective-permute-start(bf16[32,64,128]{2,1,0:T(8,128)(2,1)S(1)} %all_to_all.32.mine_ref), channel_id=1, source_target_pairs={{0,2},{2,0},{4,6},{6,4},{8,10},{10,8},{12,14},{14,12},{16,18},{18,... | collective-permute-start | bytes 1572872 | tf_op jit(solution)/shard_map/ppermute | solution.py:673
  89.9 19.0 %collective-permute-start.10 = (bf16[64,512]{1,0:T(8,128)(2,1)S(1)}, bf16[64,512]{1,0:T(8,128)(2,1)S(1)}, u32[]{:S(2)}, u32[]{:S(2)}) collective-permute-start(bf16[64,512]{1,0:T(8,128)(2,1)S(1)} %get-tuple-element.117), channel_id=1, source_target_pairs={{0,2},{2,0},{4,6},{6,4},{8,10},{10,8},{12,14},{14,12},{16,18},{18,... | collective-permute-start | bytes 196616 | tf_op jit(solution)/shard_map/ppermute | solution.py:600
  90.4 18.5 %collective-permute-start.11 = (bf16[64,512]{1,0:T(8,128)(2,1)S(1)}, bf16[64,512]{1,0:T(8,128)(2,1)S(1)}, u32[]{:S(2)}, u32[]{:S(2)}) collective-permute-start(bf16[64,512]{1,0:T(8,128)(2,1)S(1)} %get-tuple-element.118), channel_id=1, source_target_pairs={{0,126},{2,4},{4,2},{6,8},{8,6},{10,12},{12,10},{14,16},{16,14},{1... | collective-permute-start | bytes 196616 | tf_op jit(solution)/shard_map/ppermute | solution.py:599
  115.4 6.0 %collective-permute-start.12 = (bf16[64,640]{1,0:T(8,128)(2,1)S(1)}, bf16[64,640]{1,0:T(8,128)(2,1)S(1)}, u32[]{:S(2)}, u32[]{:S(2)}) collective-permute-start(bf16[64,640]{1,0:T(8,128)(2,1)S(1)} %get-tuple-element.123.refs_4_), channel_id=1, source_target_pairs={{0,2},{2,0},{4,6},{6,4},{8,10},{10,8},{12,14},{14,12},{16,18},{18,... | collective-permute-start | bytes 245768 | tf_op jit(solution)/shard_map/ppermute | solution.py:600
  116.3 5.9 %collective-permute-start.13 = (bf16[64,640]{1,0:T(8,128)(2,1)S(1)}, bf16[64,640]{1,0:T(8,128)(2,1)S(1)}, u32[]{:S(2)}, u32[]{:S(2)}) collective-permute-start(bf16[64,640]{1,0:T(8,128)(2,1)S(1)} %get-tuple-element.124.refs_5_), channel_id=1, source_target_pairs={{0,126},{2,4},{4,2},{6,8},{8,6},{10,12},{12,10},{14,16},{16,14},{1... | collective-permute-start | bytes 245768 | tf_op jit(solution)/shard_map/ppermute | solution.py:599
  123.6 9.2 %collective-permute-start.14 = (bf16[64,640]{1,0:T(8,128)(2,1)S(1)}, bf16[64,640]{1,0:T(8,128)(2,1)S(1)}, u32[]{:S(2)}, u32[]{:S(2)}) collective-permute-start(bf16[64,640]{1,0:T(8,128)(2,1)S(1)} %get-tuple-element.129.refs_4_), channel_id=1, source_target_pairs={{0,2},{2,0},{4,6},{6,4},{8,10},{10,8},{12,14},{14,12},{16,18},{18,... | collective-permute-start | bytes 245768 | tf_op jit(solution)/shard_map/ppermute | solution.py:600
  127.7 5.4 %collective-permute-start.15 = (bf16[64,640]{1,0:T(8,128)(2,1)S(1)}, bf16[64,640]{1,0:T(8,128)(2,1)S(1)}, u32[]{:S(2)}, u32[]{:S(2)}) collective-permute-start(bf16[64,640]{1,0:T(8,128)(2,1)S(1)} %get-tuple-element.130.refs_5_), channel_id=1, source_target_pairs={{0,126},{2,4},{4,2},{6,8},{8,6},{10,12},{12,10},{14,16},{16,14},{1... | collective-permute-start | bytes 245768 | tf_op jit(solution)/shard_map/ppermute | solution.py:599
  134.6 9.5 %collective-permute-start.16 = (bf16[64,640]{1,0:T(8,128)(2,1)S(1)}, bf16[64,640]{1,0:T(8,128)(2,1)S(1)}, u32[]{:S(2)}, u32[]{:S(2)}) collective-permute-start(bf16[64,640]{1,0:T(8,128)(2,1)S(1)} %get-tuple-element.135.refs_4_), channel_id=1, source_target_pairs={{0,2},{2,0},{4,6},{6,4},{8,10},{10,8},{12,14},{14,12},{16,18},{18,... | collective-permute-start | bytes 245768 | tf_op jit(solution)/shard_map/ppermute | solution.py:600
  139.0 5.4 %collective-permute-start.17 = (bf16[64,640]{1,0:T(8,128)(2,1)S(1)}, bf16[64,640]{1,0:T(8,128)(2,1)S(1)}, u32[]{:S(2)}, u32[]{:S(2)}) collective-permute-start(bf16[64,640]{1,0:T(8,128)(2,1)S(1)} %get-tuple-element.136.refs_5_), channel_id=1, source_target_pairs={{0,126},{2,4},{4,2},{6,8},{8,6},{10,12},{12,10},{14,16},{16,14},{1... | collective-permute-start | bytes 245768 | tf_op jit(solution)/shard_map/ppermute | solution.py:599
  169.6 1.9 %collective-permute-start.18 = (bf16[32,64,128]{2,1,0:T(8,128)(2,1)S(1)}, bf16[32,64,128]{2,1,0:T(8,128)(2,1)S(1)}, u32[]{:S(2)}, u32[]{:S(2)}) collective-permute-start(bf16[32,64,128]{2,1,0:T(8,128)(2,1)S(1)} %all_to_all.34.mine_ref), channel_id=1, source_target_pairs={{0,2},{2,0},{4,6},{6,4},{8,10},{10,8},{12,14},{14,12},{16,18},{18,... | collective-permute-start | bytes 1572872 | tf_op jit(solution)/shard_map/ppermute | solution.py:673

commit v4 on v3

--- a/solution.py
+++ b/solution.py
@@ -230,9 +230,9 @@
         start = (subs - 1) * own - margin
         p = dot_t(
             s_ref[:, start : total - TILE],
-            L_ref[subs - 1, rows_at(k, quarter), : total - TILE - start],
-        )
-        store(pl.multiple_of((subs - 1) * own + k * quarter, quarter), quarter, p)
+            L_ref[subs - 1, rows_at(k), : total - TILE - start],
+        )
+        store(pl.multiple_of((subs - 1) * own + k * part, part), part, p)
         return carry
 
     def inner(n, carry):
@@ -250,7 +250,7 @@
     lax.fori_loop(0, 2 * (subs - 2), inner, 0)
     if ready is not None:
         ready(subs - 1)
-    lax.fori_loop(0, 4, last, 0)
+    lax.fori_loop(0, 2, last, 0)
 
 
 def middle_first(r_ref, L_hbm, v_ref, L_ref, s_ref, sem):
@@ -537,7 +537,7 @@
 def finish(sums_ref, x_ref, image_ref, r_ref, sol_in_ref, unused_a, unused_b, sol_ref, res_ref):
     rows, total = r_ref.shape
     alpha = step_of(sums_ref, rows)
-    width = total // 2
+    width = total // 4
 
     def half(k, carry):
         cols = pl.ds(pl.multiple_of(k * width, width), width)
@@ -545,7 +545,7 @@
         sol_ref[:, cols] = sol_in_ref[:, cols] + alpha * x_ref[:, cols]
         return carry
 
-    lax.fori_loop(0, 2, half, 0)
+    lax.fori_loop(0, 4, half, 0)
 
 
 def call(kernel, name, outs, args, scratch=(), limit=8, flops=0, smem=1, specs=None):
@@ -646,7 +646,7 @@
                 )
                 other = lax.ppermute(lines, "lift", [(0, 1), (1, 0)])
                 weights.append([lines, other])
-            if sweep == 2 and len(weights) == 1:
+            if last and len(weights) == 1:
                 vv, *weights[0] = lax.optimization_barrier((vv, *weights[0]))
             first = sweep == 0
             *u, sa, sb = call(

time: 189 us -> 182 us (0.963)
  waiting for transfers between devices: 9.13 us -> 3.51 us
    ppermute x8, waiting for transfers between devices: 6.22 us -> 1.52 us  [exchange(): got_b = lax.ppermute(b, 'sector', side)]
  transfers between devices with their start and end apart: 19 -> 19, of which waited for: 9 -> 6; matrix products, arithmetic and copies ran while one was open for 0% -> 0% of each run, Pallas kernels for 19% -> 24%
where the time goes in v4:
time: 182 us
  blocking collectives  75 us (41%)
  Pallas kernels  70.2 us (39%)
  starting transfers between devices  30 us (16%)
  waiting for transfers between devices  3.51 us (2%)
    pallas_call x23, Pallas kernels, call(): pl.pallas_call(kernel, out_shape=outs, in_specs=specs or [pl.BlockSpec(me...  70.2 us
    all_to_all x2, blocking collectives, coarse_step(): lax.all_to_all(chunk, 'sector', 0, 0, axis_index_groups=planes, tiled=True)  43.8 us
    all_to_all x2, blocking collectives, body(): sums = lax.all_to_all(sums, 'sector', 0, 0, tiled=True)  31.2 us
    ppermute x8, starting transfers between devices, exchange(): got_a = lax.ppermute(a, 'sector', chip)  25.4 us
    ppermute x8, starting transfers between devices, exchange(): got_b = lax.ppermute(b, 'sector', side)  4.14 us
  transfers between devices with their start and end apart: 19, of which 6 were waited for; matrix products, arithmetic and copies ran while one was open for 0% of the time, Pallas kernels for 24%

profile of v4, /device:TPU:1, one launch (start us, length us, event | category | flops | bytes accessed | tf_op | source)
XLA Modules:
  0.0 181.5 jit_solution(11234895443191858080)
XLA Ops:
  0.6 0.0 copy-start.1
  0.7 0.6 pad_add_fusion.core_ref.refs_0_
  1.3 2.9 %first_edges.1 = (bf16[64,768]{1,0:T(8,128)(2,1)}, bf16[64,768]{1,0:T(8,128)(2,1)}) custom-call(s32[4]{0:T(128)} %pad_add_fusion.core_ref.refs_0_, f32[64,4096]{1,0:T(8,128)} %r_ref.13, f32[1,4096]{1,0:T(1,128)} %bitcast.14, bf16[4,16,1024]{2,1,0:T(8,128)(2,1)} %basis_ref.7, f32[64,2048]{1,0:T(8,128)} %ci_ref), custom_call_target="tpu_custom_call" | custom-call | bytes 1720336 | tf_op jit(solution)/shard_map/first_edges/pallas_call | solution.py:554
  4.2 1.5 collective-permute-start
  5.7 2.8 %collective-permute-start.1 = (bf16[64,768]{1,0:T(8,128)(2,1)}, bf16[64,768]{1,0:T(8,128)(2,1)S(1)}, u32[]{:S(2)}, u32[]{:S(2)}) collective-permute-start(bf16[64,768]{1,0:T(8,128)(2,1)} %get-tuple-element.79.refs_5_), channel_id=1, source_target_pairs={{0,126},{2,4},{4,2},{6,8},{8,6},{10,12},{12,10},{14,16},{16,14},{1... | collective-permute-start | bytes 294920 | tf_op jit(solution)/shard_map/ppermute | solution.py:599
  8.5 1.2 copy-done
  9.7 7.9 %middle_first.1 = (f32[64,4096]{1,0:T(8,128)S(1)}, bf16[4,1024,2048]{2,1,0:T(8,128)(2,1)S(1)}) custom-call(f32[64,4096]{1,0:T(8,128)S(1)} %copy-done, bf16[4,1024,2048]{2,1,0:T(8,128)(2,1)} %L_hbm.1), custom_call_target="tpu_custom_call" | custom-call | flops 1073741824 | bytes 17825792 | tf_op jit(solution)/shard_map/middle_first/pallas_call | solution.py:554
  17.6 0.0 collective-permute-done.refs_2_.refs_6_.a_ref.metaa_ref.ha0_ref
  17.7 0.0 copy-start.4
  17.7 1.3 edges_first.1
  19.0 6.4 %collective-permute-start.2 = (bf16[64,640]{1,0:T(8,128)(2,1)S(1)}, bf16[64,640]{1,0:T(8,128)(2,1)S(1)}, u32[]{:S(2)}, u32[]{:S(2)}) collective-permute-start(bf16[64,640]{1,0:T(8,128)(2,1)S(1)} %get-tuple-element.85.refs_4_), channel_id=1, source_target_pairs={{0,2},{2,0},{4,6},{6,4},{8,10},{10,8},{12,14},{14,12},{16,18},{18,... | collective-permute-start | bytes 245768 | tf_op jit(solution)/shard_map/ppermute | solution.py:600
  25.4 0.0 collective-permute-start.3
  25.4 5.1 %middle_near.5.refs_1_.v_ref = f32[64,4096]{1,0:T(8,128)S(1)} custom-call(f32[64,4096]{1,0:T(8,128)S(1)} %copy-done, f32[64,4096]{1,0:T(8,128)S(1)} %get-tuple-element.77.refs_1_.v_ref, f32[64,640]{1,0:T(8,128)S(1)} %get-tuple-element.81.near_l_ref, f32[64,640]{1,0:T(8,128)S(1)} %get-tuple-element.82.near_r_ref, ...), custom_call_target="tpu_custom_call" | custom-call | flops 1073741824 | bytes 19398656 | tf_op jit(solution)/shard_map/middle_near/pallas_call | solution.py:554
  30.5 0.6 lines.1.mine_ref
  31.1 0.4 collective-permute-start.6
  31.5 1.5 edges.6
  33.0 3.6 %collective-permute-start.4 = (bf16[64,640]{1,0:T(8,128)(2,1)S(1)}, bf16[64,640]{1,0:T(8,128)(2,1)S(1)}, u32[]{:S(2)}, u32[]{:S(2)}) collective-permute-start(bf16[64,640]{1,0:T(8,128)(2,1)S(1)} %get-tuple-element.91.refs_4_), channel_id=1, source_target_pairs={{0,2},{2,0},{4,6},{6,4},{8,10},{10,8},{12,14},{14,12},{16,18},{18,... | collective-permute-start | bytes 245768 | tf_op jit(solution)/shard_map/ppermute | solution.py:600
  36.7 0.7 collective-permute-start.5
  37.3 5.1 %middle_near.6.refs_1_.v_ref = f32[64,4096]{1,0:T(8,128)S(1)} custom-call(f32[64,4096]{1,0:T(8,128)S(1)} %copy-done, f32[64,4096]{1,0:T(8,128)S(1)} %middle_near.5.refs_1_.v_ref, f32[64,640]{1,0:T(8,128)S(1)} %get-tuple-element.87.near_l_ref, f32[64,640]{1,0:T(8,128)S(1)} %get-tuple-element.88.near_r_ref, bf16[64,640]{1,0:T(8,128)(2,1)S(1)} %get-tuple-element.89.wl_ref, ...), custom_call_target="tpu_custom_call" | custom-call | flops 1073741824 | bytes 19398656 | tf_op jit(solution)/shard_map/middle_near/pallas_call | solution.py:554
  42.4 0.0 collective-permute-done.5.refs_3_
  42.4 1.5 edges.7
  43.9 4.1 %collective-permute-start.7 = (bf16[64,640]{1,0:T(8,128)(2,1)S(1)}, bf16[64,640]{1,0:T(8,128)(2,1)S(1)}, u32[]{:S(2)}, u32[]{:S(2)}) collective-permute-start(bf16[64,640]{1,0:T(8,128)(2,1)S(1)} %get-tuple-element.99.refs_4_), channel_id=1, source_target_pairs={{0,2},{2,0},{4,6},{6,4},{8,10},{10,8},{12,14},{14,12},{16,18},{18,... | collective-permute-start | bytes 245768 | tf_op jit(solution)/shard_map/ppermute | solution.py:600
  48.0 0.0 collective-permute-start.8
  48.0 5.1 %middle_near.7.refs_1_.v_ref = f32[64,4096]{1,0:T(8,128)S(1)} custom-call(f32[64,4096]{1,0:T(8,128)S(1)} %copy-done, f32[64,4096]{1,0:T(8,128)S(1)} %middle_near.6.refs_1_.v_ref, f32[64,640]{1,0:T(8,128)S(1)} %get-tuple-element.93.near_l_ref, f32[64,640]{1,0:T(8,128)S(1)} %get-tuple-element.94.near_r_ref, bf16[64,640]{1,0:T(8,128)(2,1)S(1)} %get-tuple-element.95.wl_ref, ...), custom_call_target="tpu_custom_call" | custom-call | flops 1073741824 | bytes 19398656 | tf_op jit(solution)/shard_map/middle_near/pallas_call | solution.py:554
  53.1 0.0 collective-permute-done.6.other_ref
  53.2 0.2 collective-permute-done.8.refs_3_
  53.4 1.5 edges.8
  54.9 2.0 %project.2 = (bf16[32,64,128]{2,1,0:T(8,128)(2,1)S(1)}, f32[64,1024]{1,0:T(8,128)S(1)}, f32[64,1024]{1,0:T(8,128)S(1)}) custom-call(s32[4]{0:T(128)S(1)} %copy-done.5, f32[64,4096]{1,0:T(8,128)S(1)} %middle_near.7.refs_1_.v_ref, f32[64,640]{1,0:T(8,128)S(1)} %get-tuple-element.101.near_l_ref, f32[64,640]{1,0:T(8,128)S(1)} %get-tuple-element.102.near_r_ref, ...), custom_call_target="tpu_custom_call" | custom-call | bytes 19890192 | tf_op jit(solution)/shard_map/project/pallas_call | solution.py:554
  56.9 22.0 %all_to_all.32.mine_ref = bf16[32,64,128]{2,1,0:T(8,128)(2,1)S(1)} all-to-all(bf16[32,64,128]{2,1,0:T(8,128)(2,1)S(1)} %get-tuple-element.107), channel_id=1, replica_groups={{0,4,8,12,16,20,24,28,32,36,40,44,48,52,56,60,64,68,72,76,80,84,88,92,9..., dimensions={0} | all-to-all | bytes 1048576 | tf_op jit(solution)/shard_map/all_to_all | solution.py:670
  78.9 0.0 collective-permute-start.9
  78.9 1.8 %weave.1.W_ref = bf16[72,8192]{1,0:T(8,128)(2,1)S(1)} custom-call(s32[4]{0:T(128)S(1)} %copy-done.5, bf16[72,2048]{1,0:T(8,128)(2,1)S(1)} %lines.1.mine_ref, bf16[72,2048]{1,0:T(8,128)(2,1)S(1)} %collective-permute-done.6.other_ref), custom_call_target="tpu_custom_call" | custom-call | flops 67108864 | bytes 589840 | tf_op jit(solution)/shard_map/weave/pallas_call | solution.py:554
  80.7 0.1 collective-permute-done.9.other_ref
  80.8 2.2 %coarse.2 = (f32[64,4096]{1,0:T(8,128)S(1)}, f32[64,4096]{1,0:T(8,128)S(1)}, f32[64,128]{1,0:T(8,128)S(1)}, bf16[64,512]{1,0:T(8,128)(2,1)S(1)}, bf16[64,512]{1,0:T(8,128)(2,1)S(1)}) custom-call(s32[4]{0:T(128)S(1)} %copy-done.5, bf16[32,64,128]{2,1,0:T(8,128)(2,1)S(1)} %all_to_all.32.mine_ref, bf16[32,64,128]{2,1,0:T(8,128)(2,1)S(1)} %collective-permute-done.9.other_ref, ...), custom_call_target="tpu_custom_call" | custom-call | bytes 5013520 | tf_op jit(solution)/shard_map/coarse/pallas_call | solution.py:554
  83.0 0.5 collective-permute-start.10
  83.5 0.2 collective-permute-start.11
  83.7 18.3 %all_to_all.33 = f32[64,1,128]{2,1,0:T(1,128)S(1)} all-to-all(f32[64,1,128]{2,1,0:T(1,128)S(1)} %bitcast.53), channel_id=1, replica_groups=mesh['sector'=64,'lift'=2] {'sector'}, dimensions={0} | all-to-all | bytes 65536 | tf_op jit(solution)/shard_map/all_to_all | solution.py:695
  101.9 0.0 collective-permute-done.10.ha_ref
  101.9 0.0 collective-permute-done.11.hb_ref
  101.9 6.5 %second.1 = (f32[64,4096]{1,0:T(8,128)S(1)}, f32[64,4096]{1,0:T(8,128)S(1)}, f32[64,4096]{1,0:T(8,128)S(1)}, f32[64,1024]{1,0:T(8,128)S(1)}, f32[64,1024]{1,0:T(...) custom-call(s32[4]{0:T(128)S(1)} %copy-done.5, f32[64,128]{1,0:T(8,128)S(1)} %bitcast.51, ...), custom_call_target="tpu_custom_call" | custom-call | flops 1073741824 | bytes 20316176 | tf_op jit(solution)/shard_map/second/pallas_call | solution.py:554
  108.5 0.8 collective-permute-start.12
  109.3 0.5 collective-permute-start.13
  109.8 4.7 %middle.1.refs_1_.v_ref = f32[64,4096]{1,0:T(8,128)S(1)} custom-call(f32[64,4096]{1,0:T(8,128)S(1)} %get-tuple-element.119.r_ref.refs_8_, f32[64,4096]{1,0:T(8,128)S(1)} %get-tuple-element.120.v_ref, f32[64,1024]{1,0:T(8,128)S(1)} %get-tuple-element.121.u0_ref, f32[64,1024]{1,0:T(8,128)S(1)} %get-tuple-element.122.u3_ref, f32[1,4096]{1,0:T(1,128)S(1)} %bitcast.43, ...), custom_call_target="tpu_custom_call" | custom-call | flops 1073741824 | bytes 19431424 | tf_op jit(solution)/shard_map/middle/pallas_call | solution.py:554
  114.5 0.0 collective-permute-done.12.refs_2_
  114.5 0.7 collective-permute-done.13.refs_3_
  115.2 1.5 edges.9
  116.7 4.1 %collective-permute-start.14 = (bf16[64,640]{1,0:T(8,128)(2,1)S(1)}, bf16[64,640]{1,0:T(8,128)(2,1)S(1)}, u32[]{:S(2)}, u32[]{:S(2)}) collective-permute-start(bf16[64,640]{1,0:T(8,128)(2,1)S(1)} %get-tuple-element.129.refs_4_), channel_id=1, source_target_pairs={{0,2},{2,0},{4,6},{6,4},{8,10},{10,8},{12,14},{14,12},{16,18},{18,... | collective-permute-start | bytes 245768 | tf_op jit(solution)/shard_map/ppermute | solution.py:600
  120.7 0.0 collective-permute-start.15
  120.8 5.1 %middle_near.8.refs_1_.v_ref = f32[64,4096]{1,0:T(8,128)S(1)} custom-call(f32[64,4096]{1,0:T(8,128)S(1)} %get-tuple-element.119.r_ref.refs_8_, f32[64,4096]{1,0:T(8,128)S(1)} %middle.1.refs_1_.v_ref, f32[64,640]{1,0:T(8,128)S(1)} %get-tuple-element.125.near_l_ref, f32[64,640]{1,0:T(8,128)S(1)} %get-tuple-element.126.near_r_ref, ...), custom_call_target="tpu_custom_call" | custom-call | flops 1073741824 | bytes 19398656 | tf_op jit(solution)/shard_map/middle_near/pallas_call | solution.py:554
  125.8 0.0 collective-permute-done.14.refs_2_
  125.8 0.3 collective-permute-done.15.refs_3_
  126.1 1.5 edges.10
  127.6 4.4 %collective-permute-start.16 = (bf16[64,640]{1,0:T(8,128)(2,1)S(1)}, bf16[64,640]{1,0:T(8,128)(2,1)S(1)}, u32[]{:S(2)}, u32[]{:S(2)}) collective-permute-start(bf16[64,640]{1,0:T(8,128)(2,1)S(1)} %get-tuple-element.135.refs_4_), channel_id=1, source_target_pairs={{0,2},{2,0},{4,6},{6,4},{8,10},{10,8},{12,14},{14,12},{16,18},{18,... | collective-permute-start | bytes 245768 | tf_op jit(solution)/shard_map/ppermute | solution.py:600
  132.0 0.0 collective-permute-start.17
  132.0 5.1 %middle_near.9.refs_1_.v_ref = f32[64,4096]{1,0:T(8,128)S(1)} custom-call(f32[64,4096]{1,0:T(8,128)S(1)} %get-tuple-element.119.r_ref.refs_8_, f32[64,4096]{1,0:T(8,128)S(1)} %middle_near.8.refs_1_.v_ref, f32[64,640]{1,0:T(8,128)S(1)} %get-tuple-element.131.near_l_ref, f32[64,640]{1,0:T(8,128)S(1)} %get-tuple-element.132.near_r_ref, ...), custom_call_target="tpu_custom_call" | custom-call | flops 1073741824 | bytes 19398656 | tf_op jit(solution)/shard_map/middle_near/pallas_call | solution.py:554
  137.1 0.0 collective-permute-done.16.refs_2_
  137.1 0.3 collective-permute-done.17.refs_3_
  137.4 1.5 edges.11
  138.8 2.0 %project.3 = (bf16[32,64,128]{2,1,0:T(8,128)(2,1)S(1)}, f32[64,1024]{1,0:T(8,128)S(1)}, f32[64,1024]{1,0:T(8,128)S(1)}) custom-call(s32[4]{0:T(128)S(1)} %copy-done.5, f32[64,4096]{1,0:T(8,128)S(1)} %middle_near.9.refs_1_.v_ref, f32[64,640]{1,0:T(8,128)S(1)} %get-tuple-element.137.near_l_ref, f32[64,640]{1,0:T(8,128)S(1)} %get-tuple-element.138.near_r_ref, ...), custom_call_target="tpu_custom_call" | custom-call | bytes 19890192 | tf_op jit(solution)/shard_map/project/pallas_call | solution.py:554
  140.8 21.8 %all_to_all.34.mine_ref = bf16[32,64,128]{2,1,0:T(8,128)(2,1)S(1)} all-to-all(bf16[32,64,128]{2,1,0:T(8,128)(2,1)S(1)} %get-tuple-element.143), channel_id=1, replica_groups={{0,4,8,12,16,20,24,28,32,36,40,44,48,52,56,60,64,68,72,76,80,84,88,92,9..., dimensions={0} | all-to-all | bytes 1048576 | tf_op jit(solution)/shard_map/all_to_all | solution.py:670
  162.6 0.0 collective-permute-start.18
  162.6 1.9 %collective-permute-done.18.other_ref = bf16[32,64,128]{2,1,0:T(8,128)(2,1)S(1)} collective-permute-done((bf16[32,64,128]{2,1,0:T(8,128)(2,1)S(1)}, bf16[32,64,128]{2,1,0:T(8,128)(2,1)S(1)}, u32[]{:S(2)}, u32[]{:S(2)}) %collective-permute-start.18) | collective-permute-done | bytes 524320 | tf_op jit(solution)/shard_map/ppermute | solution.py:673
  164.5 2.2 %coarse.3 = (f32[64,4096]{1,0:T(8,128)S(1)}, f32[64,4096]{1,0:T(8,128)S(1)}, f32[64,128]{1,0:T(8,128)S(1)}, bf16[64,512]{1,0:T(8,128)(2,1)S(1)}, bf16[64,512]{1,0:T(8,128)(2,1)S(1)}) custom-call(s32[4]{0:T(128)S(1)} %copy-done.5, bf16[32,64,128]{2,1,0:T(8,128)(2,1)S(1)} %all_to_all.34.mine_ref, bf16[32,64,128]{2,1,0:T(8,128)(2,1)S(1)} %collective-permute-done.18.other_ref, ...), custom_call_target="tpu_custom_call" | custom-call | bytes 5013520 | tf_op jit(solution)/shard_map/coarse/pallas_call | solution.py:554
  166.7 12.9 %all_to_all.35 = f32[64,1,128]{2,1,0:T(1,128)S(1)} all-to-all(f32[64,1,128]{2,1,0:T(1,128)S(1)} %bitcast.54), channel_id=1, replica_groups=mesh['sector'=64,'lift'=2] {'sector'}, dimensions={0} | all-to-all | bytes 65536 | tf_op jit(solution)/shard_map/all_to_all | solution.py:703
  179.6 1.9 %finish.1 = (f32[64,4096]{1,0:T(8,128)}, f32[64,4096]{1,0:T(8,128)}) custom-call(f32[64,128]{1,0:T(8,128)S(1)} %bitcast.52, f32[64,4096]{1,0:T(8,128)S(1)} %get-tuple-element.147.x_ref, f32[64,4096]{1,0:T(8,128)S(1)} %get-tuple-element.148.image_ref, f32[64,4096]{1,0:T(8,128)S(1)} %get-tuple-element.119.r_ref.refs_8_, ...), custom_call_target="tpu_custom_call" | custom-call | bytes 4358144 | tf_op jit(solution)/shard_map/finish/pallas_call | solution.py:554
  (18 shorter events, 0.0 us)
Async XLA Ops:
  0.6 17.0 %copy-start.1 = (f32[4096]{0:T(1024)S(1)}, f32[4096]{0:T(1024)}, u32[]{:S(2)}) copy-start(f32[4096]{0:T(1024)} %param.8) | copy-start | bytes 49156
  0.6 17.0 %copy-start.2 = (f32[4096]{0:T(1024)S(1)}, f32[4096]{0:T(1024)}, u32[]{:S(2)}) copy-start(f32[4096]{0:T(1024)} %param.7) | copy-start | bytes 49156
  1.3 16.3 %copy-start.5 = (s32[4]{0:T(128)S(1)}, s32[4]{0:T(128)}, u32[]{:S(2)}) copy-start(s32[4]{0:T(128)} %pad_add_fusion.core_ref.refs_0_) | copy-start | bytes 52
  4.2 13.4 %collective-permute-start = (bf16[64,768]{1,0:T(8,128)(2,1)}, bf16[64,768]{1,0:T(8,128)(2,1)S(1)}, u32[]{:S(2)}, u32[]{:S(2)}) collective-permute-start(bf16[64,768]{1,0:T(8,128)(2,1)} %get-tuple-element.78.refs_4_), channel_id=1, source_target_pairs={{0,2},{2,0},{4,6},{6,4},{8,10},{10,8},{12,14},{14,12},{16,18},{18,... | collective-permute-start | bytes 294920 | tf_op jit(solution)/shard_map/ppermute | solution.py:600
  5.7 11.9 %collective-permute-start.1 = (bf16[64,768]{1,0:T(8,128)(2,1)}, bf16[64,768]{1,0:T(8,128)(2,1)S(1)}, u32[]{:S(2)}, u32[]{:S(2)}) collective-permute-start(bf16[64,768]{1,0:T(8,128)(2,1)} %get-tuple-element.79.refs_5_), channel_id=1, source_target_pairs={{0,126},{2,4},{4,2},{6,8},{8,6},{10,12},{12,10},{14,16},{16,14},{1... | collective-permute-start | bytes 294920 | tf_op jit(solution)/shard_map/ppermute | solution.py:599
  8.5 1.2 copy-start
  9.7 7.9 %copy-start.6 = (bf16[64,768]{1,0:T(8,128)(2,1)S(1)}, bf16[64,768]{1,0:T(8,128)(2,1)}, u32[]{:S(2)}) copy-start(bf16[64,768]{1,0:T(8,128)(2,1)} %get-tuple-element.78.refs_4_) | copy-start | bytes 294916
  9.7 7.9 %copy-start.7 = (bf16[64,768]{1,0:T(8,128)(2,1)S(1)}, bf16[64,768]{1,0:T(8,128)(2,1)}, u32[]{:S(2)}) copy-start(bf16[64,768]{1,0:T(8,128)(2,1)} %get-tuple-element.79.refs_5_) | copy-start | bytes 294916
  17.7 12.9 %copy-start.4 = (f32[64,2048]{1,0:T(8,128)S(1)}, f32[64,2048]{1,0:T(8,128)}, u32[]{:S(2)}) copy-start(f32[64,2048]{1,0:T(8,128)} %ci_ref) | copy-start | bytes 1572868
  19.0 12.5 %collective-permute-start.2 = (bf16[64,640]{1,0:T(8,128)(2,1)S(1)}, bf16[64,640]{1,0:T(8,128)(2,1)S(1)}, u32[]{:S(2)}, u32[]{:S(2)}) collective-permute-start(bf16[64,640]{1,0:T(8,128)(2,1)S(1)} %get-tuple-element.85.refs_4_), channel_id=1, source_target_pairs={{0,2},{2,0},{4,6},{6,4},{8,10},{10,8},{12,14},{14,12},{16,18},{18,... | collective-permute-start | bytes 245768 | tf_op jit(solution)/shard_map/ppermute | solution.py:600
  25.4 6.1 %collective-permute-start.3 = (bf16[64,640]{1,0:T(8,128)(2,1)S(1)}, bf16[64,640]{1,0:T(8,128)(2,1)S(1)}, u32[]{:S(2)}, u32[]{:S(2)}) collective-permute-start(bf16[64,640]{1,0:T(8,128)(2,1)S(1)} %get-tuple-element.86.refs_5_), channel_id=1, source_target_pairs={{0,126},{2,4},{4,2},{6,8},{8,6},{10,12},{12,10},{14,16},{16,14},{1... | collective-permute-start | bytes 245768 | tf_op jit(solution)/shard_map/ppermute | solution.py:599
  31.1 22.0 %collective-permute-start.6 = (bf16[72,2048]{1,0:T(8,128)(2,1)S(1)}, bf16[72,2048]{1,0:T(8,128)(2,1)S(1)}, u32[]{:S(2)}, u32[]{:S(2)}) collective-permute-start(bf16[72,2048]{1,0:T(8,128)(2,1)S(1)} %lines.1.mine_ref), channel_id=1, source_target_pairs={{0,1},{1,0},{2,3},{3,2},{4,5},{5,4},{6,7},{7,6},{8,9},{9,8},{10,11... | collective-permute-start | bytes 884744 | tf_op jit(solution)/shard_map/ppermute | solution.py:647
  33.0 9.4 %collective-permute-start.4 = (bf16[64,640]{1,0:T(8,128)(2,1)S(1)}, bf16[64,640]{1,0:T(8,128)(2,1)S(1)}, u32[]{:S(2)}, u32[]{:S(2)}) collective-permute-start(bf16[64,640]{1,0:T(8,128)(2,1)S(1)} %get-tuple-element.91.refs_4_), channel_id=1, source_target_pairs={{0,2},{2,0},{4,6},{6,4},{8,10},{10,8},{12,14},{14,12},{16,18},{18,... | collective-permute-start | bytes 245768 | tf_op jit(solution)/shard_map/ppermute | solution.py:600
  36.7 5.8 %collective-permute-start.5 = (bf16[64,640]{1,0:T(8,128)(2,1)S(1)}, bf16[64,640]{1,0:T(8,128)(2,1)S(1)}, u32[]{:S(2)}, u32[]{:S(2)}) collective-permute-start(bf16[64,640]{1,0:T(8,128)(2,1)S(1)} %get-tuple-element.92.refs_5_), channel_id=1, source_target_pairs={{0,126},{2,4},{4,2},{6,8},{8,6},{10,12},{12,10},{14,16},{16,14},{1... | collective-permute-start | bytes 245768 | tf_op jit(solution)/shard_map/ppermute | solution.py:599
  43.9 9.2 %collective-permute-start.7 = (bf16[64,640]{1,0:T(8,128)(2,1)S(1)}, bf16[64,640]{1,0:T(8,128)(2,1)S(1)}, u32[]{:S(2)}, u32[]{:S(2)}) collective-permute-start(bf16[64,640]{1,0:T(8,128)(2,1)S(1)} %get-tuple-element.99.refs_4_), channel_id=1, source_target_pairs={{0,2},{2,0},{4,6},{6,4},{8,10},{10,8},{12,14},{14,12},{16,18},{18,... | collective-permute-start | bytes 245768 | tf_op jit(solution)/shard_map/ppermute | solution.py:600
  48.0 5.4 %collective-permute-start.8 = (bf16[64,640]{1,0:T(8,128)(2,1)S(1)}, bf16[64,640]{1,0:T(8,128)(2,1)S(1)}, u32[]{:S(2)}, u32[]{:S(2)}) collective-permute-start(bf16[64,640]{1,0:T(8,128)(2,1)S(1)} %get-tuple-element.100.refs_5_), channel_id=1, source_target_pairs={{0,126},{2,4},{4,2},{6,8},{8,6},{10,12},{12,10},{14,16},{16,14},{1... | collective-permute-start | bytes 245768 | tf_op jit(solution)/shard_map/ppermute | solution.py:599
  48.0 6.8 %copy-start.3 = (bf16[4,16,1024]{2,1,0:T(8,128)(2,1)S(1)}, bf16[4,16,1024]{2,1,0:T(8,128)(2,1)}, u32[]{:S(2)}) copy-start(bf16[4,16,1024]{2,1,0:T(8,128)(2,1)} %basis_ref.7) | copy-start | bytes 393220
  78.9 1.9 %collective-permute-start.9 = (bf16[32,64,128]{2,1,0:T(8,128)(2,1)S(1)}, bf16[32,64,128]{2,1,0:T(8,128)(2,1)S(1)}, u32[]{:S(2)}, u32[]{:S(2)}) collective-permute-start(bf16[32,64,128]{2,1,0:T(8,128)(2,1)S(1)} %all_to_all.32.mine_ref), channel_id=1, source_target_pairs={{0,2},{2,0},{4,6},{6,4},{8,10},{10,8},{12,14},{14,12},{16,18},{18,... | collective-permute-start | bytes 1572872 | tf_op jit(solution)/shard_map/ppermute | solution.py:673
  83.0 19.0 %collective-permute-start.10 = (bf16[64,512]{1,0:T(8,128)(2,1)S(1)}, bf16[64,512]{1,0:T(8,128)(2,1)S(1)}, u32[]{:S(2)}, u32[]{:S(2)}) collective-permute-start(bf16[64,512]{1,0:T(8,128)(2,1)S(1)} %get-tuple-element.117), channel_id=1, source_target_pairs={{0,2},{2,0},{4,6},{6,4},{8,10},{10,8},{12,14},{14,12},{16,18},{18,... | collective-permute-start | bytes 196616 | tf_op jit(solution)/shard_map/ppermute | solution.py:600
  83.5 18.5 %collective-permute-start.11 = (bf16[64,512]{1,0:T(8,128)(2,1)S(1)}, bf16[64,512]{1,0:T(8,128)(2,1)S(1)}, u32[]{:S(2)}, u32[]{:S(2)}) collective-permute-start(bf16[64,512]{1,0:T(8,128)(2,1)S(1)} %get-tuple-element.118), channel_id=1, source_target_pairs={{0,126},{2,4},{4,2},{6,8},{8,6},{10,12},{12,10},{14,16},{16,14},{1... | collective-permute-start | bytes 196616 | tf_op jit(solution)/shard_map/ppermute | solution.py:599
  108.5 6.0 %collective-permute-start.12 = (bf16[64,640]{1,0:T(8,128)(2,1)S(1)}, bf16[64,640]{1,0:T(8,128)(2,1)S(1)}, u32[]{:S(2)}, u32[]{:S(2)}) collective-permute-start(bf16[64,640]{1,0:T(8,128)(2,1)S(1)} %get-tuple-element.123.refs_4_), channel_id=1, source_target_pairs={{0,2},{2,0},{4,6},{6,4},{8,10},{10,8},{12,14},{14,12},{16,18},{18,... | collective-permute-start | bytes 245768 | tf_op jit(solution)/shard_map/ppermute | solution.py:600
  109.3 5.9 %collective-permute-start.13 = (bf16[64,640]{1,0:T(8,128)(2,1)S(1)}, bf16[64,640]{1,0:T(8,128)(2,1)S(1)}, u32[]{:S(2)}, u32[]{:S(2)}) collective-permute-start(bf16[64,640]{1,0:T(8,128)(2,1)S(1)} %get-tuple-element.124.refs_5_), channel_id=1, source_target_pairs={{0,126},{2,4},{4,2},{6,8},{8,6},{10,12},{12,10},{14,16},{16,14},{1... | collective-permute-start | bytes 245768 | tf_op jit(solution)/shard_map/ppermute | solution.py:599
  116.7 9.2 %collective-permute-start.14 = (bf16[64,640]{1,0:T(8,128)(2,1)S(1)}, bf16[64,640]{1,0:T(8,128)(2,1)S(1)}, u32[]{:S(2)}, u32[]{:S(2)}) collective-permute-start(bf16[64,640]{1,0:T(8,128)(2,1)S(1)} %get-tuple-element.129.refs_4_), channel_id=1, source_target_pairs={{0,2},{2,0},{4,6},{6,4},{8,10},{10,8},{12,14},{14,12},{16,18},{18,... | collective-permute-start | bytes 245768 | tf_op jit(solution)/shard_map/ppermute | solution.py:600
  120.7 5.4 %collective-permute-start.15 = (bf16[64,640]{1,0:T(8,128)(2,1)S(1)}, bf16[64,640]{1,0:T(8,128)(2,1)S(1)}, u32[]{:S(2)}, u32[]{:S(2)}) collective-permute-start(bf16[64,640]{1,0:T(8,128)(2,1)S(1)} %get-tuple-element.130.refs_5_), channel_id=1, source_target_pairs={{0,126},{2,4},{4,2},{6,8},{8,6},{10,12},{12,10},{14,16},{16,14},{1... | collective-permute-start | bytes 245768 | tf_op jit(solution)/shard_map/ppermute | solution.py:599
  127.6 9.5 %collective-permute-start.16 = (bf16[64,640]{1,0:T(8,128)(2,1)S(1)}, bf16[64,640]{1,0:T(8,128)(2,1)S(1)}, u32[]{:S(2)}, u32[]{:S(2)}) collective-permute-start(bf16[64,640]{1,0:T(8,128)(2,1)S(1)} %get-tuple-element.135.refs_4_), channel_id=1, source_target_pairs={{0,2},{2,0},{4,6},{6,4},{8,10},{10,8},{12,14},{14,12},{16,18},{18,... | collective-permute-start | bytes 245768 | tf_op jit(solution)/shard_map/ppermute | solution.py:600
  132.0 5.4 %collective-permute-start.17 = (bf16[64,640]{1,0:T(8,128)(2,1)S(1)}, bf16[64,640]{1,0:T(8,128)(2,1)S(1)}, u32[]{:S(2)}, u32[]{:S(2)}) collective-permute-start(bf16[64,640]{1,0:T(8,128)(2,1)S(1)} %get-tuple-element.136.refs_5_), channel_id=1, source_target_pairs={{0,126},{2,4},{4,2},{6,8},{8,6},{10,12},{12,10},{14,16},{16,14},{1... | collective-permute-start | bytes 245768 | tf_op jit(solution)/shard_map/ppermute | solution.py:599
  162.6 1.9 %collective-permute-start.18 = (bf16[32,64,128]{2,1,0:T(8,128)(2,1)S(1)}, bf16[32,64,128]{2,1,0:T(8,128)(2,1)S(1)}, u32[]{:S(2)}, u32[]{:S(2)}) collective-permute-start(bf16[32,64,128]{2,1,0:T(8,128)(2,1)S(1)} %all_to_all.34.mine_ref), channel_id=1, source_target_pairs={{0,2},{2,0},{4,6},{6,4},{8,10},{10,8},{12,14},{14,12},{16,18},{18,... | collective-permute-start | bytes 1572872 | tf_op jit(solution)/shard_map/ppermute | solution.py:673

commit v5 on v4

--- a/solution.py
+++ b/solution.py
@@ -286,6 +286,18 @@
     middle(r_ref, v_ref, u0_ref, u3_ref, dg_ref, cp_ref, L_ref, out_ref, s_ref)
 
 
+def middle_second(r_ref, sin_ref, u0_ref, u3_ref, dg_ref, cp_ref, L_ref, out_ref, s_ref, v_ref):
+    subs, own, order = L_ref.shape
+
+    def step(j, carry):
+        at = pl.multiple_of(j * own, own)
+        v_ref[:, pl.ds(at, own)] = dot_t(sin_ref[:, pl.ds(at, order)], L_ref[j])
+        return carry
+
+    lax.fori_loop(1, subs - 1, step, 0)
+    middle(r_ref, v_ref, u0_ref, u3_ref, dg_ref, cp_ref, L_ref, out_ref, s_ref)
+
+
 def middle(r_ref, v_ref, u0_ref, u3_ref, dg_ref, cp_ref, L_ref, out_ref, s_ref):
     subs, own, order = L_ref.shape
     total = r_ref.shape[1]
@@ -492,8 +504,8 @@
 
 
 def second(core_ref, sums_ref, x_ref, image_ref, r_ref, ha0_ref, hb0_ref, ha_ref, hb_ref,
-           dg_ref, cp_ref, L_ref, sol_ref, res_ref, u_ref, u0_ref, u3_ref, a_ref, b_ref,
-           s_ref, sl_ref, sr_ref):
+           dg_ref, cp_ref, L_ref, sol_ref, res_ref, s_ref, u0_ref, u3_ref, a_ref, b_ref,
+           sl_ref, sr_ref):
     rows, total = r_ref.shape
     own, order = L_ref.shape[1], L_ref.shape[2]
     alpha = step_of(sums_ref, rows)
@@ -516,15 +528,6 @@
 
     u0_ref[...] = dot_t(s_ref[:, :order], L_ref[0])
     u3_ref[...] = dot_t(s_ref[:, total - own :], L_ref[subs - 1])
-    u_ref[:, :own] = u0_ref[...]
-    u_ref[:, total - own :] = u3_ref[...]
-
-    def step(j, carry):
-        at = pl.multiple_of(j * own, own)
-        u_ref[:, pl.ds(at, own)] = dot_t(s_ref[:, pl.ds(at, order)], L_ref[j])
-        return carry
-
-    lax.fori_loop(1, subs - 1, step, 0)
     edge_sends(res_ref, dg_ref, cp_ref, u0_ref, u3_ref, sl_ref, sr_ref)
 
     def send(even):
@@ -631,7 +634,8 @@
                 ga, gb = exchange(sa, sb)
                 if len(u) == 2:
                     vv = call(
-                        middle, "middle", full, [r, v, *u, dg, cp, L], [s_scratch], 8, work, 0
+                        middle_second, "middle_second", full, [r, v, *u, dg, cp, L],
+                        [s_scratch, pltpu.VMEM((rows, total), F32)], 8, work, 0,
                     )
                 else:
                     vv = call(
@@ -694,9 +698,9 @@
     halo_a, halo_b = exchange(ia, ib)
     sums = lax.all_to_all(sums, "sector", 0, 0, tiled=True)
     sol, r, v, u0, u3, sa, sb = call(
-        second, "second", [full, full, full, sub, sub, send, send],
+        second, "second", [full, full, shape((rows, total + 2 * CH), BF16), sub, sub, send, send],
         [core, sums, x, image, r, got_a0, got_b0, halo_a, halo_b, dg, cp, L],
-        [pltpu.VMEM((rows, total + 2 * CH), BF16)] + pair(send), 8, work,
+        pair(send), 8, work,
     )
     v, u, sa, sb = sweeps(v, (u0, u3), sa, sb, 1)
     x, image, sums, ia, ib = coarse_step(v, u, sa, sb)

time: 182 us -> 180 us (0.989)
    ppermute x8, starting transfers between devices: 25.4 us -> 23.3 us  [exchange(): got_a = lax.ppermute(a, 'sector', chip)]
  transfers between devices with their start and end apart: 19 -> 19, of which waited for: 6 -> 4; matrix products, arithmetic and copies ran while one was open for 0% -> 0% of each run, Pallas kernels for 24% -> 26%
where the time goes in v5:
time: 180 us
  blocking collectives  75.3 us (42%)
  Pallas kernels  70.2 us (39%)
  starting transfers between devices  29.1 us (16%)
  waiting for transfers between devices  2.54 us (1%)
    pallas_call x23, Pallas kernels, call(): pl.pallas_call(kernel, out_shape=outs, in_specs=specs or [pl.BlockSpec(me...  70.2 us
    all_to_all x2, blocking collectives, coarse_step(): lax.all_to_all(chunk, 'sector', 0, 0, axis_index_groups=planes, tiled=True)  44.1 us
    all_to_all x2, blocking collectives, body(): sums = lax.all_to_all(sums, 'sector', 0, 0, tiled=True)  31.2 us
    ppermute x8, starting transfers between devices, exchange(): got_a = lax.ppermute(a, 'sector', chip)  23.3 us
    ppermute x8, starting transfers between devices, exchange(): got_b = lax.ppermute(b, 'sector', side)  5.39 us
  transfers between devices with their start and end apart: 19, of which 4 were waited for; matrix products, arithmetic and copies ran while one was open for 0% of the time, Pallas kernels for 26%

profile of v5, /device:TPU:1, one launch (start us, length us, event | category | flops | bytes accessed | tf_op | source)
XLA Modules:
  0.0 179.9 jit_solution(18015242953926398593)
XLA Ops:
  0.6 0.0 copy-start.1
  0.7 0.6 pad_add_fusion.core_ref.refs_0_
  1.3 2.9 %first_edges.1 = (bf16[64,768]{1,0:T(8,128)(2,1)}, bf16[64,768]{1,0:T(8,128)(2,1)}) custom-call(s32[4]{0:T(128)} %pad_add_fusion.core_ref.refs_0_, f32[64,4096]{1,0:T(8,128)} %r_ref.13, f32[1,4096]{1,0:T(1,128)} %bitcast.14, bf16[4,16,1024]{2,1,0:T(8,128)(2,1)} %basis_ref.7, f32[64,2048]{1,0:T(8,128)} %ci_ref), custom_call_target="tpu_custom_call" | custom-call | bytes 1720336 | tf_op jit(solution)/shard_map/first_edges/pallas_call | solution.py:557
  4.2 1.5 collective-permute-start
  5.7 2.8 %collective-permute-start.1 = (bf16[64,768]{1,0:T(8,128)(2,1)}, bf16[64,768]{1,0:T(8,128)(2,1)S(1)}, u32[]{:S(2)}, u32[]{:S(2)}) collective-permute-start(bf16[64,768]{1,0:T(8,128)(2,1)} %get-tuple-element.79.refs_5_), channel_id=1, source_target_pairs={{0,126},{2,4},{4,2},{6,8},{8,6},{10,12},{12,10},{14,16},{16,14},{1... | collective-permute-start | bytes 294920 | tf_op jit(solution)/shard_map/ppermute | solution.py:602
  8.5 1.2 copy-done
  9.7 7.9 %middle_first.1 = (f32[64,4096]{1,0:T(8,128)S(1)}, bf16[4,1024,2048]{2,1,0:T(8,128)(2,1)S(1)}) custom-call(f32[64,4096]{1,0:T(8,128)S(1)} %copy-done, bf16[4,1024,2048]{2,1,0:T(8,128)(2,1)} %L_hbm.1), custom_call_target="tpu_custom_call" | custom-call | flops 1073741824 | bytes 17825792 | tf_op jit(solution)/shard_map/middle_first/pallas_call | solution.py:557
  17.6 0.0 collective-permute-done.refs_2_.refs_6_.a_ref.metaa_ref.ha0_ref
  17.6 0.0 collective-permute-done.1.refs_3_.refs_7_.b_ref.metab_ref.hb0_ref
  17.7 0.0 copy-start.4
  17.7 1.3 edges_first.1
  19.0 6.4 %collective-permute-start.2 = (bf16[64,640]{1,0:T(8,128)(2,1)S(1)}, bf16[64,640]{1,0:T(8,128)(2,1)S(1)}, u32[]{:S(2)}, u32[]{:S(2)}) collective-permute-start(bf16[64,640]{1,0:T(8,128)(2,1)S(1)} %get-tuple-element.85.refs_4_), channel_id=1, source_target_pairs={{0,2},{2,0},{4,6},{6,4},{8,10},{10,8},{12,14},{14,12},{16,18},{18,... | collective-permute-start | bytes 245768 | tf_op jit(solution)/shard_map/ppermute | solution.py:603
  25.4 0.0 collective-permute-start.3
  25.4 5.1 %middle_near.5.refs_1_.v_ref = f32[64,4096]{1,0:T(8,128)S(1)} custom-call(f32[64,4096]{1,0:T(8,128)S(1)} %copy-done, f32[64,4096]{1,0:T(8,128)S(1)} %get-tuple-element.77.refs_1_.v_ref, f32[64,640]{1,0:T(8,128)S(1)} %get-tuple-element.81.near_l_ref, f32[64,640]{1,0:T(8,128)S(1)} %get-tuple-element.82.near_r_ref, ...), custom_call_target="tpu_custom_call" | custom-call | flops 1073741824 | bytes 19398656 | tf_op jit(solution)/shard_map/middle_near/pallas_call | solution.py:557
  30.5 0.6 lines.1.mine_ref
  31.1 0.4 collective-permute-start.6
  31.5 1.5 edges.6
  33.0 3.6 %collective-permute-start.4 = (bf16[64,640]{1,0:T(8,128)(2,1)S(1)}, bf16[64,640]{1,0:T(8,128)(2,1)S(1)}, u32[]{:S(2)}, u32[]{:S(2)}) collective-permute-start(bf16[64,640]{1,0:T(8,128)(2,1)S(1)} %get-tuple-element.91.refs_4_), channel_id=1, source_target_pairs={{0,2},{2,0},{4,6},{6,4},{8,10},{10,8},{12,14},{14,12},{16,18},{18,... | collective-permute-start | bytes 245768 | tf_op jit(solution)/shard_map/ppermute | solution.py:603
  36.7 0.7 collective-permute-start.5
  37.3 5.1 %middle_near.6.refs_1_.v_ref = f32[64,4096]{1,0:T(8,128)S(1)} custom-call(f32[64,4096]{1,0:T(8,128)S(1)} %copy-done, f32[64,4096]{1,0:T(8,128)S(1)} %middle_near.5.refs_1_.v_ref, f32[64,640]{1,0:T(8,128)S(1)} %get-tuple-element.87.near_l_ref, f32[64,640]{1,0:T(8,128)S(1)} %get-tuple-element.88.near_r_ref, bf16[64,640]{1,0:T(8,128)(2,1)S(1)} %get-tuple-element.89.wl_ref, ...), custom_call_target="tpu_custom_call" | custom-call | flops 1073741824 | bytes 19398656 | tf_op jit(solution)/shard_map/middle_near/pallas_call | solution.py:557
  42.4 0.0 collective-permute-done.5.refs_3_
  42.4 1.5 edges.7
  43.9 4.1 %collective-permute-start.7 = (bf16[64,640]{1,0:T(8,128)(2,1)S(1)}, bf16[64,640]{1,0:T(8,128)(2,1)S(1)}, u32[]{:S(2)}, u32[]{:S(2)}) collective-permute-start(bf16[64,640]{1,0:T(8,128)(2,1)S(1)} %get-tuple-element.99.refs_4_), channel_id=1, source_target_pairs={{0,2},{2,0},{4,6},{6,4},{8,10},{10,8},{12,14},{14,12},{16,18},{18,... | collective-permute-start | bytes 245768 | tf_op jit(solution)/shard_map/ppermute | solution.py:603
  48.0 0.0 collective-permute-start.8
  48.0 5.1 %middle_near.7.refs_1_.v_ref = f32[64,4096]{1,0:T(8,128)S(1)} custom-call(f32[64,4096]{1,0:T(8,128)S(1)} %copy-done, f32[64,4096]{1,0:T(8,128)S(1)} %middle_near.6.refs_1_.v_ref, f32[64,640]{1,0:T(8,128)S(1)} %get-tuple-element.93.near_l_ref, f32[64,640]{1,0:T(8,128)S(1)} %get-tuple-element.94.near_r_ref, bf16[64,640]{1,0:T(8,128)(2,1)S(1)} %get-tuple-element.95.wl_ref, ...), custom_call_target="tpu_custom_call" | custom-call | flops 1073741824 | bytes 19398656 | tf_op jit(solution)/shard_map/middle_near/pallas_call | solution.py:557
  53.1 0.0 collective-permute-done.6.other_ref
  53.2 0.2 collective-permute-done.8.refs_3_
  53.4 1.5 edges.8
  54.9 2.0 %project.2 = (bf16[32,64,128]{2,1,0:T(8,128)(2,1)S(1)}, f32[64,1024]{1,0:T(8,128)S(1)}, f32[64,1024]{1,0:T(8,128)S(1)}) custom-call(s32[4]{0:T(128)S(1)} %copy-done.5, f32[64,4096]{1,0:T(8,128)S(1)} %middle_near.7.refs_1_.v_ref, f32[64,640]{1,0:T(8,128)S(1)} %get-tuple-element.101.near_l_ref, f32[64,640]{1,0:T(8,128)S(1)} %get-tuple-element.102.near_r_ref, ...), custom_call_target="tpu_custom_call" | custom-call | bytes 19890192 | tf_op jit(solution)/shard_map/project/pallas_call | solution.py:557
  56.9 22.0 %all_to_all.32.mine_ref = bf16[32,64,128]{2,1,0:T(8,128)(2,1)S(1)} all-to-all(bf16[32,64,128]{2,1,0:T(8,128)(2,1)S(1)} %get-tuple-element.107), channel_id=1, replica_groups={{0,4,8,12,16,20,24,28,32,36,40,44,48,52,56,60,64,68,72,76,80,84,88,92,9..., dimensions={0} | all-to-all | bytes 1048576 | tf_op jit(solution)/shard_map/all_to_all | solution.py:674
  78.9 0.0 collective-permute-start.9
  78.9 1.8 %weave.1.W_ref = bf16[72,8192]{1,0:T(8,128)(2,1)S(1)} custom-call(s32[4]{0:T(128)S(1)} %copy-done.5, bf16[72,2048]{1,0:T(8,128)(2,1)S(1)} %lines.1.mine_ref, bf16[72,2048]{1,0:T(8,128)(2,1)S(1)} %collective-permute-done.6.other_ref), custom_call_target="tpu_custom_call" | custom-call | flops 67108864 | bytes 589840 | tf_op jit(solution)/shard_map/weave/pallas_call | solution.py:557
  80.7 0.1 collective-permute-done.9.other_ref
  80.8 2.2 %coarse.2 = (f32[64,4096]{1,0:T(8,128)S(1)}, f32[64,4096]{1,0:T(8,128)S(1)}, f32[64,128]{1,0:T(8,128)S(1)}, bf16[64,512]{1,0:T(8,128)(2,1)S(1)}, bf16[64,512]{1,0:T(8,128)(2,1)S(1)}) custom-call(s32[4]{0:T(128)S(1)} %copy-done.5, bf16[32,64,128]{2,1,0:T(8,128)(2,1)S(1)} %all_to_all.32.mine_ref, bf16[32,64,128]{2,1,0:T(8,128)(2,1)S(1)} %collective-permute-done.9.other_ref, ...), custom_call_target="tpu_custom_call" | custom-call | bytes 5013520 | tf_op jit(solution)/shard_map/coarse/pallas_call | solution.py:557
  83.0 0.5 collective-permute-start.10
  83.5 0.2 collective-permute-start.11
  83.7 18.3 %all_to_all.33 = f32[64,1,128]{2,1,0:T(1,128)S(1)} all-to-all(f32[64,1,128]{2,1,0:T(1,128)S(1)} %bitcast.53), channel_id=1, replica_groups=mesh['sector'=64,'lift'=2] {'sector'}, dimensions={0} | all-to-all | bytes 65536 | tf_op jit(solution)/shard_map/all_to_all | solution.py:699
  101.9 0.0 collective-permute-done.10.ha_ref
  101.9 0.0 collective-permute-done.11.hb_ref
  101.9 3.7 %second.1 = (f32[64,4096]{1,0:T(8,128)S(1)}, f32[64,4096]{1,0:T(8,128)S(1)}, bf16[64,5120]{1,0:T(8,128)(2,1)S(1)}, f32[64,1024]{1,0:T(8,128)S(1)}, f32[64,1024]{...) custom-call(s32[4]{0:T(128)S(1)} %copy-done.5, f32[64,128]{1,0:T(8,128)S(1)} %bitcast.51, ...), custom_call_target="tpu_custom_call" | custom-call | flops 1073741824 | bytes 20316176 | tf_op jit(solution)/shard_map/second/pallas_call | solution.py:557
  105.6 0.8 collective-permute-start.12
  106.5 0.5 collective-permute-start.13
  106.9 7.5 %middle_second.1.refs_1_.v_ref = f32[64,4096]{1,0:T(8,128)S(1)} custom-call(f32[64,4096]{1,0:T(8,128)S(1)} %get-tuple-element.119.r_ref.refs_8_, bf16[64,5120]{1,0:T(8,128)(2,1)S(1)} %get-tuple-element.120.sin_ref, f32[64,1024]{1,0:T(8,128)S(1)} %get-tuple-element.121.u0_ref, f32[64,1024]{1,0:T(8,128)S(1)} %get-tuple-element.122.u3_ref, ...), custom_call_target="tpu_custom_call" | custom-call | flops 1073741824 | bytes 19038208 | tf_op jit(solution)/shard_map/middle_second/pallas_call | solution.py:557
  114.5 0.0 collective-permute-done.12.refs_2_
  114.5 0.0 collective-permute-done.13.refs_3_
  114.5 1.5 edges.9
  116.0 2.0 %collective-permute-start.14 = (bf16[64,640]{1,0:T(8,128)(2,1)S(1)}, bf16[64,640]{1,0:T(8,128)(2,1)S(1)}, u32[]{:S(2)}, u32[]{:S(2)}) collective-permute-start(bf16[64,640]{1,0:T(8,128)(2,1)S(1)} %get-tuple-element.129.refs_4_), channel_id=1, source_target_pairs={{0,2},{2,0},{4,6},{6,4},{8,10},{10,8},{12,14},{14,12},{16,18},{18,... | collective-permute-start | bytes 245768 | tf_op jit(solution)/shard_map/ppermute | solution.py:603
  117.9 1.3 collective-permute-start.15
  119.2 5.1 %middle_near.8.refs_1_.v_ref = f32[64,4096]{1,0:T(8,128)S(1)} custom-call(f32[64,4096]{1,0:T(8,128)S(1)} %get-tuple-element.119.r_ref.refs_8_, f32[64,4096]{1,0:T(8,128)S(1)} %middle_second.1.refs_1_.v_ref, f32[64,640]{1,0:T(8,128)S(1)} %get-tuple-element.125.near_l_ref, f32[64,640]{1,0:T(8,128)S(1)} %get-tuple-element.126.near_r_ref, ...), custom_call_target="tpu_custom_call" | custom-call | flops 1073741824 | bytes 19398656 | tf_op jit(solution)/shard_map/middle_near/pallas_call | solution.py:557
  124.3 0.0 collective-permute-done.14.refs_2_
  124.3 0.0 collective-permute-done.15.refs_3_
  124.3 1.5 edges.10
  125.8 4.4 %collective-permute-start.16 = (bf16[64,640]{1,0:T(8,128)(2,1)S(1)}, bf16[64,640]{1,0:T(8,128)(2,1)S(1)}, u32[]{:S(2)}, u32[]{:S(2)}) collective-permute-start(bf16[64,640]{1,0:T(8,128)(2,1)S(1)} %get-tuple-element.135.refs_4_), channel_id=1, source_target_pairs={{0,2},{2,0},{4,6},{6,4},{8,10},{10,8},{12,14},{14,12},{16,18},{18,... | collective-permute-start | bytes 245768 | tf_op jit(solution)/shard_map/ppermute | solution.py:603
  130.1 5.1 %middle_near.9.refs_1_.v_ref = f32[64,4096]{1,0:T(8,128)S(1)} custom-call(f32[64,4096]{1,0:T(8,128)S(1)} %get-tuple-element.119.r_ref.refs_8_, f32[64,4096]{1,0:T(8,128)S(1)} %middle_near.8.refs_1_.v_ref, f32[64,640]{1,0:T(8,128)S(1)} %get-tuple-element.131.near_l_ref, f32[64,640]{1,0:T(8,128)S(1)} %get-tuple-element.132.near_r_ref, ...), custom_call_target="tpu_custom_call" | custom-call | flops 1073741824 | bytes 19398656 | tf_op jit(solution)/shard_map/middle_near/pallas_call | solution.py:557
  135.2 0.0 collective-permute-done.16.refs_2_
  135.2 0.3 collective-permute-done.17.refs_3_
  135.5 1.5 edges.11
  137.0 2.0 %project.3 = (bf16[32,64,128]{2,1,0:T(8,128)(2,1)S(1)}, f32[64,1024]{1,0:T(8,128)S(1)}, f32[64,1024]{1,0:T(8,128)S(1)}) custom-call(s32[4]{0:T(128)S(1)} %copy-done.5, f32[64,4096]{1,0:T(8,128)S(1)} %middle_near.9.refs_1_.v_ref, f32[64,640]{1,0:T(8,128)S(1)} %get-tuple-element.137.near_l_ref, f32[64,640]{1,0:T(8,128)S(1)} %get-tuple-element.138.near_r_ref, ...), custom_call_target="tpu_custom_call" | custom-call | bytes 19890192 | tf_op jit(solution)/shard_map/project/pallas_call | solution.py:557
  139.0 22.1 %all_to_all.34.mine_ref = bf16[32,64,128]{2,1,0:T(8,128)(2,1)S(1)} all-to-all(bf16[32,64,128]{2,1,0:T(8,128)(2,1)S(1)} %get-tuple-element.143), channel_id=1, replica_groups={{0,4,8,12,16,20,24,28,32,36,40,44,48,52,56,60,64,68,72,76,80,84,88,92,9..., dimensions={0} | all-to-all | bytes 1048576 | tf_op jit(solution)/shard_map/all_to_all | solution.py:674
  161.0 0.0 collective-permute-start.18
  161.0 1.9 %collective-permute-done.18.other_ref = bf16[32,64,128]{2,1,0:T(8,128)(2,1)S(1)} collective-permute-done((bf16[32,64,128]{2,1,0:T(8,128)(2,1)S(1)}, bf16[32,64,128]{2,1,0:T(8,128)(2,1)S(1)}, u32[]{:S(2)}, u32[]{:S(2)}) %collective-permute-start.18) | collective-permute-done | bytes 524320 | tf_op jit(solution)/shard_map/ppermute | solution.py:677
  162.9 2.2 %coarse.3 = (f32[64,4096]{1,0:T(8,128)S(1)}, f32[64,4096]{1,0:T(8,128)S(1)}, f32[64,128]{1,0:T(8,128)S(1)}, bf16[64,512]{1,0:T(8,128)(2,1)S(1)}, bf16[64,512]{1,0:T(8,128)(2,1)S(1)}) custom-call(s32[4]{0:T(128)S(1)} %copy-done.5, bf16[32,64,128]{2,1,0:T(8,128)(2,1)S(1)} %all_to_all.34.mine_ref, bf16[32,64,128]{2,1,0:T(8,128)(2,1)S(1)} %collective-permute-done.18.other_ref, ...), custom_call_target="tpu_custom_call" | custom-call | bytes 5013520 | tf_op jit(solution)/shard_map/coarse/pallas_call | solution.py:557
  165.1 12.9 %all_to_all.35 = f32[64,1,128]{2,1,0:T(1,128)S(1)} all-to-all(f32[64,1,128]{2,1,0:T(1,128)S(1)} %bitcast.54), channel_id=1, replica_groups=mesh['sector'=64,'lift'=2] {'sector'}, dimensions={0} | all-to-all | bytes 65536 | tf_op jit(solution)/shard_map/all_to_all | solution.py:707
  178.0 1.9 %finish.1 = (f32[64,4096]{1,0:T(8,128)}, f32[64,4096]{1,0:T(8,128)}) custom-call(f32[64,128]{1,0:T(8,128)S(1)} %bitcast.52, f32[64,4096]{1,0:T(8,128)S(1)} %get-tuple-element.147.x_ref, f32[64,4096]{1,0:T(8,128)S(1)} %get-tuple-element.148.image_ref, f32[64,4096]{1,0:T(8,128)S(1)} %get-tuple-element.119.r_ref.refs_8_, ...), custom_call_target="tpu_custom_call" | custom-call | bytes 4358144 | tf_op jit(solution)/shard_map/finish/pallas_call | solution.py:557
  (18 shorter events, 0.0 us)
Async XLA Ops:
  0.6 17.0 %copy-start.1 = (f32[4096]{0:T(1024)S(1)}, f32[4096]{0:T(1024)}, u32[]{:S(2)}) copy-start(f32[4096]{0:T(1024)} %param.8) | copy-start | bytes 49156
  0.6 17.0 %copy-start.2 = (f32[4096]{0:T(1024)S(1)}, f32[4096]{0:T(1024)}, u32[]{:S(2)}) copy-start(f32[4096]{0:T(1024)} %param.7) | copy-start | bytes 49156
  1.3 16.3 %copy-start.5 = (s32[4]{0:T(128)S(1)}, s32[4]{0:T(128)}, u32[]{:S(2)}) copy-start(s32[4]{0:T(128)} %pad_add_fusion.core_ref.refs_0_) | copy-start | bytes 52
  4.2 13.4 %collective-permute-start = (bf16[64,768]{1,0:T(8,128)(2,1)}, bf16[64,768]{1,0:T(8,128)(2,1)S(1)}, u32[]{:S(2)}, u32[]{:S(2)}) collective-permute-start(bf16[64,768]{1,0:T(8,128)(2,1)} %get-tuple-element.78.refs_4_), channel_id=1, source_target_pairs={{0,2},{2,0},{4,6},{6,4},{8,10},{10,8},{12,14},{14,12},{16,18},{18,... | collective-permute-start | bytes 294920 | tf_op jit(solution)/shard_map/ppermute | solution.py:603
  5.7 11.9 %collective-permute-start.1 = (bf16[64,768]{1,0:T(8,128)(2,1)}, bf16[64,768]{1,0:T(8,128)(2,1)S(1)}, u32[]{:S(2)}, u32[]{:S(2)}) collective-permute-start(bf16[64,768]{1,0:T(8,128)(2,1)} %get-tuple-element.79.refs_5_), channel_id=1, source_target_pairs={{0,126},{2,4},{4,2},{6,8},{8,6},{10,12},{12,10},{14,16},{16,14},{1... | collective-permute-start | bytes 294920 | tf_op jit(solution)/shard_map/ppermute | solution.py:602
  8.5 1.2 copy-start
  9.7 7.9 %copy-start.6 = (bf16[64,768]{1,0:T(8,128)(2,1)S(1)}, bf16[64,768]{1,0:T(8,128)(2,1)}, u32[]{:S(2)}) copy-start(bf16[64,768]{1,0:T(8,128)(2,1)} %get-tuple-element.78.refs_4_) | copy-start | bytes 294916
  9.7 7.9 %copy-start.7 = (bf16[64,768]{1,0:T(8,128)(2,1)S(1)}, bf16[64,768]{1,0:T(8,128)(2,1)}, u32[]{:S(2)}) copy-start(bf16[64,768]{1,0:T(8,128)(2,1)} %get-tuple-element.79.refs_5_) | copy-start | bytes 294916
  17.7 12.9 %copy-start.4 = (f32[64,2048]{1,0:T(8,128)S(1)}, f32[64,2048]{1,0:T(8,128)}, u32[]{:S(2)}) copy-start(f32[64,2048]{1,0:T(8,128)} %ci_ref) | copy-start | bytes 1572868
  19.0 12.5 %collective-permute-start.2 = (bf16[64,640]{1,0:T(8,128)(2,1)S(1)}, bf16[64,640]{1,0:T(8,128)(2,1)S(1)}, u32[]{:S(2)}, u32[]{:S(2)}) collective-permute-start(bf16[64,640]{1,0:T(8,128)(2,1)S(1)} %get-tuple-element.85.refs_4_), channel_id=1, source_target_pairs={{0,2},{2,0},{4,6},{6,4},{8,10},{10,8},{12,14},{14,12},{16,18},{18,... | collective-permute-start | bytes 245768 | tf_op jit(solution)/shard_map/ppermute | solution.py:603
  25.4 6.1 %collective-permute-start.3 = (bf16[64,640]{1,0:T(8,128)(2,1)S(1)}, bf16[64,640]{1,0:T(8,128)(2,1)S(1)}, u32[]{:S(2)}, u32[]{:S(2)}) collective-permute-start(bf16[64,640]{1,0:T(8,128)(2,1)S(1)} %get-tuple-element.86.refs_5_), channel_id=1, source_target_pairs={{0,126},{2,4},{4,2},{6,8},{8,6},{10,12},{12,10},{14,16},{16,14},{1... | collective-permute-start | bytes 245768 | tf_op jit(solution)/shard_map/ppermute | solution.py:602
  31.1 22.0 %collective-permute-start.6 = (bf16[72,2048]{1,0:T(8,128)(2,1)S(1)}, bf16[72,2048]{1,0:T(8,128)(2,1)S(1)}, u32[]{:S(2)}, u32[]{:S(2)}) collective-permute-start(bf16[72,2048]{1,0:T(8,128)(2,1)S(1)} %lines.1.mine_ref), channel_id=1, source_target_pairs={{0,1},{1,0},{2,3},{3,2},{4,5},{5,4},{6,7},{7,6},{8,9},{9,8},{10,11... | collective-permute-start | bytes 884744 | tf_op jit(solution)/shard_map/ppermute | solution.py:651
  33.0 9.4 %collective-permute-start.4 = (bf16[64,640]{1,0:T(8,128)(2,1)S(1)}, bf16[64,640]{1,0:T(8,128)(2,1)S(1)}, u32[]{:S(2)}, u32[]{:S(2)}) collective-permute-start(bf16[64,640]{1,0:T(8,128)(2,1)S(1)} %get-tuple-element.91.refs_4_), channel_id=1, source_target_pairs={{0,2},{2,0},{4,6},{6,4},{8,10},{10,8},{12,14},{14,12},{16,18},{18,... | collective-permute-start | bytes 245768 | tf_op jit(solution)/shard_map/ppermute | solution.py:603
  36.7 5.8 %collective-permute-start.5 = (bf16[64,640]{1,0:T(8,128)(2,1)S(1)}, bf16[64,640]{1,0:T(8,128)(2,1)S(1)}, u32[]{:S(2)}, u32[]{:S(2)}) collective-permute-start(bf16[64,640]{1,0:T(8,128)(2,1)S(1)} %get-tuple-element.92.refs_5_), channel_id=1, source_target_pairs={{0,126},{2,4},{4,2},{6,8},{8,6},{10,12},{12,10},{14,16},{16,14},{1... | collective-permute-start | bytes 245768 | tf_op jit(solution)/shard_map/ppermute | solution.py:602
  43.9 9.2 %collective-permute-start.7 = (bf16[64,640]{1,0:T(8,128)(2,1)S(1)}, bf16[64,640]{1,0:T(8,128)(2,1)S(1)}, u32[]{:S(2)}, u32[]{:S(2)}) collective-permute-start(bf16[64,640]{1,0:T(8,128)(2,1)S(1)} %get-tuple-element.99.refs_4_), channel_id=1, source_target_pairs={{0,2},{2,0},{4,6},{6,4},{8,10},{10,8},{12,14},{14,12},{16,18},{18,... | collective-permute-start | bytes 245768 | tf_op jit(solution)/shard_map/ppermute | solution.py:603
  48.0 5.4 %collective-permute-start.8 = (bf16[64,640]{1,0:T(8,128)(2,1)S(1)}, bf16[64,640]{1,0:T(8,128)(2,1)S(1)}, u32[]{:S(2)}, u32[]{:S(2)}) collective-permute-start(bf16[64,640]{1,0:T(8,128)(2,1)S(1)} %get-tuple-element.100.refs_5_), channel_id=1, source_target_pairs={{0,126},{2,4},{4,2},{6,8},{8,6},{10,12},{12,10},{14,16},{16,14},{1... | collective-permute-start | bytes 245768 | tf_op jit(solution)/shard_map/ppermute | solution.py:602
  48.0 6.8 %copy-start.3 = (bf16[4,16,1024]{2,1,0:T(8,128)(2,1)S(1)}, bf16[4,16,1024]{2,1,0:T(8,128)(2,1)}, u32[]{:S(2)}) copy-start(bf16[4,16,1024]{2,1,0:T(8,128)(2,1)} %basis_ref.7) | copy-start | bytes 393220
  78.9 1.9 %collective-permute-start.9 = (bf16[32,64,128]{2,1,0:T(8,128)(2,1)S(1)}, bf16[32,64,128]{2,1,0:T(8,128)(2,1)S(1)}, u32[]{:S(2)}, u32[]{:S(2)}) collective-permute-start(bf16[32,64,128]{2,1,0:T(8,128)(2,1)S(1)} %all_to_all.32.mine_ref), channel_id=1, source_target_pairs={{0,2},{2,0},{4,6},{6,4},{8,10},{10,8},{12,14},{14,12},{16,18},{18,... | collective-permute-start | bytes 1572872 | tf_op jit(solution)/shard_map/ppermute | solution.py:677
  83.0 19.0 %collective-permute-start.10 = (bf16[64,512]{1,0:T(8,128)(2,1)S(1)}, bf16[64,512]{1,0:T(8,128)(2,1)S(1)}, u32[]{:S(2)}, u32[]{:S(2)}) collective-permute-start(bf16[64,512]{1,0:T(8,128)(2,1)S(1)} %get-tuple-element.117), channel_id=1, source_target_pairs={{0,2},{2,0},{4,6},{6,4},{8,10},{10,8},{12,14},{14,12},{16,18},{18,... | collective-permute-start | bytes 196616 | tf_op jit(solution)/shard_map/ppermute | solution.py:603
  83.5 18.5 %collective-permute-start.11 = (bf16[64,512]{1,0:T(8,128)(2,1)S(1)}, bf16[64,512]{1,0:T(8,128)(2,1)S(1)}, u32[]{:S(2)}, u32[]{:S(2)}) collective-permute-start(bf16[64,512]{1,0:T(8,128)(2,1)S(1)} %get-tuple-element.118), channel_id=1, source_target_pairs={{0,126},{2,4},{4,2},{6,8},{8,6},{10,12},{12,10},{14,16},{16,14},{1... | collective-permute-start | bytes 196616 | tf_op jit(solution)/shard_map/ppermute | solution.py:602
  105.6 8.8 %collective-permute-start.12 = (bf16[64,640]{1,0:T(8,128)(2,1)S(1)}, bf16[64,640]{1,0:T(8,128)(2,1)S(1)}, u32[]{:S(2)}, u32[]{:S(2)}) collective-permute-start(bf16[64,640]{1,0:T(8,128)(2,1)S(1)} %get-tuple-element.123.refs_4_), channel_id=1, source_target_pairs={{0,2},{2,0},{4,6},{6,4},{8,10},{10,8},{12,14},{14,12},{16,18},{18,... | collective-permute-start | bytes 245768 | tf_op jit(solution)/shard_map/ppermute | solution.py:603
  106.5 8.0 %collective-permute-start.13 = (bf16[64,640]{1,0:T(8,128)(2,1)S(1)}, bf16[64,640]{1,0:T(8,128)(2,1)S(1)}, u32[]{:S(2)}, u32[]{:S(2)}) collective-permute-start(bf16[64,640]{1,0:T(8,128)(2,1)S(1)} %get-tuple-element.124.refs_5_), channel_id=1, source_target_pairs={{0,126},{2,4},{4,2},{6,8},{8,6},{10,12},{12,10},{14,16},{16,14},{1... | collective-permute-start | bytes 245768 | tf_op jit(solution)/shard_map/ppermute | solution.py:602
  116.0 8.3 %collective-permute-start.14 = (bf16[64,640]{1,0:T(8,128)(2,1)S(1)}, bf16[64,640]{1,0:T(8,128)(2,1)S(1)}, u32[]{:S(2)}, u32[]{:S(2)}) collective-permute-start(bf16[64,640]{1,0:T(8,128)(2,1)S(1)} %get-tuple-element.129.refs_4_), channel_id=1, source_target_pairs={{0,2},{2,0},{4,6},{6,4},{8,10},{10,8},{12,14},{14,12},{16,18},{18,... | collective-permute-start | bytes 245768 | tf_op jit(solution)/shard_map/ppermute | solution.py:603
  117.9 6.3 %collective-permute-start.15 = (bf16[64,640]{1,0:T(8,128)(2,1)S(1)}, bf16[64,640]{1,0:T(8,128)(2,1)S(1)}, u32[]{:S(2)}, u32[]{:S(2)}) collective-permute-start(bf16[64,640]{1,0:T(8,128)(2,1)S(1)} %get-tuple-element.130.refs_5_), channel_id=1, source_target_pairs={{0,126},{2,4},{4,2},{6,8},{8,6},{10,12},{12,10},{14,16},{16,14},{1... | collective-permute-start | bytes 245768 | tf_op jit(solution)/shard_map/ppermute | solution.py:602
  125.8 9.4 %collective-permute-start.16 = (bf16[64,640]{1,0:T(8,128)(2,1)S(1)}, bf16[64,640]{1,0:T(8,128)(2,1)S(1)}, u32[]{:S(2)}, u32[]{:S(2)}) collective-permute-start(bf16[64,640]{1,0:T(8,128)(2,1)S(1)} %get-tuple-element.135.refs_4_), channel_id=1, source_target_pairs={{0,2},{2,0},{4,6},{6,4},{8,10},{10,8},{12,14},{14,12},{16,18},{18,... | collective-permute-start | bytes 245768 | tf_op jit(solution)/shard_map/ppermute | solution.py:603
  130.1 5.4 %collective-permute-start.17 = (bf16[64,640]{1,0:T(8,128)(2,1)S(1)}, bf16[64,640]{1,0:T(8,128)(2,1)S(1)}, u32[]{:S(2)}, u32[]{:S(2)}) collective-permute-start(bf16[64,640]{1,0:T(8,128)(2,1)S(1)} %get-tuple-element.136.refs_5_), channel_id=1, source_target_pairs={{0,126},{2,4},{4,2},{6,8},{8,6},{10,12},{12,10},{14,16},{16,14},{1... | collective-permute-start | bytes 245768 | tf_op jit(solution)/shard_map/ppermute | solution.py:602
  161.0 1.9 %collective-permute-start.18 = (bf16[32,64,128]{2,1,0:T(8,128)(2,1)S(1)}, bf16[32,64,128]{2,1,0:T(8,128)(2,1)S(1)}, u32[]{:S(2)}, u32[]{:S(2)}) collective-permute-start(bf16[32,64,128]{2,1,0:T(8,128)(2,1)S(1)} %all_to_all.34.mine_ref), channel_id=1, source_target_pairs={{0,2},{2,0},{4,6},{6,4},{8,10},{10,8},{12,14},{14,12},{16,18},{18,... | collective-permute-start | bytes 1572872 | tf_op jit(solution)/shard_map/ppermute | solution.py:677
